TPU v7x, 128 devices: a whole 4x4x4 slice. The times are simulated.
128 devices in a mesh: image: 8 (over x, core), space: 16 (over y, z).
Axes of the slice: x: 4, y: 4, z: 4, core: 2. Of those that a mesh axis runs over, the one named last changes fastest.
Arguments:
- positions: float32 [16, 3, 4096], P('image', None, 'space'), may hold values from -6 to 6
- velocity: float32 [16, 3, 4096], P('image', None, 'space'), may hold values from -4 to 4
- start_state: float32 [3, 4096], P(None, 'space'), may hold values from -6 to 6
- end_state: float32 [3, 4096], P(None, 'space'), may hold values from -6 to 6
- neighbours: int32 [16, 16, 4096], P('image', None, 'space'), may hold values from 0 to 511, as said below
- counts: int32 [16, 4096], P('image', 'space'), may hold values from 1 to 16, as said below
- climb_index: int32 [1], replicated, may hold values from 0 to 15
- radial_a1: float32 [8, 64], replicated, may hold values from -2 to 2
- radial_b1: float32 [64, 128], replicated, may hold values from -0.75 to 0.75
- mix_first: float32 [384, 128], replicated, may hold values from -0.5 to 0.5
- read_first: float32 [128], replicated, may hold values from -0.5 to 0.5
- radial_a2: float32 [8, 64], replicated, may hold values from -2 to 2
- radial_b2: float32 [64, 128], replicated, may hold values from -0.75 to 0.75
- mix_second: float32 [384, 128], replicated, may hold values from -0.5 to 0.5
- read_second: float32 [128], replicated, may hold values from -0.5 to 0.5
Outputs:
- neb_force: float32 [16, 3, 4096], P('image', None, 'space')
- velocity_next: float32 [16, 3, 4096], P('image', None, 'space')
- position_next: float32 [16, 3, 4096], P('image', None, 'space')
- image_energy: float32 [16], P('image')
Inputs may be any that keep to these rules, and one draw needn't show every extreme that they name: `neighbours`: A slab's extended atoms are, in order, the last 128 atoms of the slab below, its own 256 atoms, and the first 128 atoms of the slab above; the first and last slabs are beside each other. `counts`: atoms in the middle of the image have a higher least number of live neighbours than those at its ends.
All inputs are finite; a program needn't handle non-finite values.
Results may differ from a plain program's by a relative error of at most 0.0003.
Values sent between devices are 32-bit elements; how exact they have to be, the bound alone decides.
No kernel may reach another device: no remote copies, remote signals or barrier semaphores. Data moves between devices by JAX's collectives and lax.ppermute only.
A program may use at most 64 MiB of HBM per device.

v0:
```python
import math

import jax
import jax.numpy as jnp
from jax import lax
from jax.sharding import PartitionSpec as P

highest = lax.Precision.HIGHEST


def padded(cells, sides, width, closed):
    for axis, dim in sides:
        count = lax.axis_size(axis)
        ends = count if closed else count - 1
        head = lax.slice_in_dim(cells, 0, width, axis=dim)
        tail = lax.slice_in_dim(cells, cells.shape[dim] - width, cells.shape[dim], axis=dim)
        cells = jnp.concatenate(
            [
                lax.ppermute(tail, axis, [(i, (i + 1) % count) for i in range(ends)]),
                cells,
                lax.ppermute(head, axis, [((i + 1) % count, i) for i in range(ends)]),
            ],
            axis=dim,
        )
    return cells


def harmonics(unit):
    ux = unit[0]
    uy = unit[1]
    uz = unit[2]
    return jnp.stack(
        [
            jnp.ones_like(ux),
            ux,
            uy,
            uz,
            ux * uy,
            uy * uz,
            ux * uz,
            0.5 * (ux * ux - uy * uy),
            (3.0 * uz * uz - 1.0) / (2.0 * math.sqrt(3.0)),
        ]
    )


def layer_out(center, nb_pos, live_mask, radial_a, radial_b, mixing, nb_feat):
    offset = nb_pos - center[:, None, :]
    length = jnp.sqrt(jnp.sum(offset * offset, axis=0) + 1.0)
    angular = harmonics(offset / length[None])
    centres = 0.5 * jnp.arange(radial_a.shape[0]).astype(center.dtype)
    spread = length[None] - centres[:, None, None]
    basis = jnp.exp(-spread * spread / 0.5)
    hidden = jax.nn.silu(jnp.einsum("bka,bh->hka", basis, radial_a, precision=highest))
    radial = jnp.einsum("hka,hc->cka", hidden, radial_b, precision=highest) * live_mask[None]
    if nb_feat is not None:
        radial = radial * nb_feat
    moments = jnp.einsum("cka,lka->cla", radial, angular, precision=highest) / live_mask.shape[0]
    invariants = jnp.concatenate(
        [
            moments[:, 0],
            jnp.sum(moments[:, 1:4] * moments[:, 1:4], axis=1),
            jnp.sum(moments[:, 4:9] * moments[:, 4:9], axis=1),
        ],
        axis=0,
    )
    return jax.nn.silu(jnp.einsum("fa,fc->ca", invariants, mixing, precision=highest))


def own_part(grad_ext, atoms):
    ghost = (grad_ext.shape[-1] - atoms) // 2
    return grad_ext[..., ghost : ghost + atoms]


def ghost_parts(grad_ext, atoms):
    ghost = (grad_ext.shape[-1] - atoms) // 2
    return jnp.concatenate([grad_ext[..., :ghost], grad_ext[..., ghost + atoms :]], axis=-1)


def add_returned(own, returned):
    ghost = returned.shape[-1] // 4
    atoms = own.shape[-1]
    leading = [(0, 0)] * (own.ndim - 1)
    lower = jnp.pad(returned[..., :ghost], leading + [(0, atoms - ghost)])
    upper = jnp.pad(returned[..., 3 * ghost :], leading + [(atoms - ghost, 0)])
    return own + lower + upper


def local(
    positions,
    velocity,
    start_state,
    end_state,
    neighbours,
    counts,
    climb_index,
    radial_a1,
    radial_b1,
    mix_first,
    read_first,
    radial_a2,
    radial_b2,
    mix_second,
    read_second,
):
    atoms = positions.shape[2]
    ghost = atoms // 2
    img_count = positions.shape[0]
    slots = lax.broadcasted_iota(jnp.int32, neighbours.shape, 1)
    live_all = (slots < counts[:, None, :]).astype(jnp.float32)

    def first_layer(ext_pos, nb_idx, live_mask):
        center = ext_pos[:, ghost : ghost + atoms]
        return layer_out(
            center, ext_pos[:, nb_idx], live_mask, radial_a1, radial_b1, mix_first, None
        )

    def second_energy(ext_pos, ext_feat, nb_idx, live_mask):
        center = ext_pos[:, ghost : ghost + atoms]
        second = layer_out(
            center,
            ext_pos[:, nb_idx],
            live_mask,
            radial_a2,
            radial_b2,
            mix_second,
            ext_feat[:, nb_idx],
        )
        return jnp.sum(read_second[:, None] * second)

    def one_image(items):
        image_pos, nb_idx, live_mask = items
        ext_pos = padded(image_pos, (("space", 1),), ghost, True)

        def layer_one(pos_arg):
            return first_layer(pos_arg, nb_idx, live_mask)

        feat_own, back_one = jax.vjp(layer_one, ext_pos)
        ext_feat = padded(feat_own, (("space", 1),), ghost, True)

        def layer_two(pos_arg, feat_arg):
            return second_energy(pos_arg, feat_arg, nb_idx, live_mask)

        energy_two, back_two = jax.vjp(layer_two, ext_pos, ext_feat)
        grad_pos2, grad_feat = back_two(jnp.ones_like(energy_two))
        returned = padded(ghost_parts(grad_feat, atoms), (("space", 1),), ghost, True)
        feat_cot = add_returned(own_part(grad_feat, atoms), returned) + read_first[:, None]
        grad_total = back_one(feat_cot)[0] + grad_pos2
        back_pos = padded(ghost_parts(grad_total, atoms), (("space", 1),), ghost, True)
        image_force = -add_returned(own_part(grad_total, atoms), back_pos)
        energy = jnp.sum(read_first[:, None] * feat_own) + energy_two
        return (image_force, energy)

    forces, energies = lax.map(one_image, (positions, neighbours, live_all))
    chain = padded(positions, (("image", 0),), 1, False)
    first_dev = lax.axis_index("image") == 0
    last_dev = lax.axis_index("image") == lax.axis_size("image") - 1
    prev_pos = jnp.concatenate(
        [jnp.where(first_dev, start_state, chain[0])[None], chain[1:img_count]], axis=0
    )
    next_pos = jnp.concatenate(
        [chain[2 : img_count + 1], jnp.where(last_dev, end_state, chain[img_count + 1])[None]],
        axis=0,
    )
    spread = next_pos - prev_pos
    ahead = next_pos - positions
    behind = positions - prev_pos
    ahead_loc = jnp.sum(ahead * ahead, axis=(1, 2))
    behind_loc = jnp.sum(behind * behind, axis=(1, 2))
    spread_loc = jnp.sum(spread * spread, axis=(1, 2))
    dist_ahead, dist_behind, spread_sq, energy_sum = lax.psum(
        (ahead_loc, behind_loc, spread_loc, energies), "space"
    )
    tangent = spread / jnp.sqrt(spread_sq + 1e-06)[:, None, None]
    along = lax.psum(jnp.sum(forces * tangent, axis=(1, 2)), "space")
    spring = 5.0 * (jnp.sqrt(dist_ahead) - jnp.sqrt(dist_behind))
    image_ids = lax.axis_index("image") * img_count + jnp.arange(img_count)
    climbing = (image_ids == climb_index[0]).astype(jnp.float32)
    coef = -(1.0 + climbing) * along + (1.0 - climbing) * spring
    neb_force = forces + coef[:, None, None] * tangent
    vel_sq, force_sq = lax.psum(
        (jnp.sum(velocity * velocity), jnp.sum(neb_force * neb_force)), ("image", "space")
    )
    velocity_next = (
        0.9 * velocity + 0.1 * jnp.sqrt(vel_sq / (force_sq + 1e-06)) * neb_force + 0.1 * neb_force
    )
    position_next = positions + 0.1 * velocity_next
    image_energy = energy_sum / (atoms * lax.axis_size("space"))
    return (neb_force, velocity_next, position_next, image_energy)


def solution(mesh):
    in_specs = (
        P("image", None, "space"),
        P("image", None, "space"),
        P(None, "space"),
        P(None, "space"),
        P("image", None, "space"),
        P("image", "space"),
        P(),
        P(),
        P(),
        P(),
        P(),
        P(),
        P(),
        P(),
        P(),
    )
    out_specs = (
        P("image", None, "space"),
        P("image", None, "space"),
        P("image", None, "space"),
        P("image"),
    )
    return jax.shard_map(local, mesh=mesh, in_specs=in_specs, out_specs=out_specs, check_vma=False)
```

profile of v0, /device:TPU:1, one launch (start us, length us, event | category | flops | bytes accessed | tf_op | source)
XLA Modules:
  0.0 567.9 jit_solution(13672815025296068187)
XLA Ops:
  2.6 4.5 collective-permute-start.9
  14.3 34.7 %psum.49 = f32[2]{0:T(128)S(1)} all-reduce(f32[2]{0:T(128)S(1)} %get-tuple-element.306), channel_id=1, replica_groups=mesh['image'=8,'space'=16] {'space'}, use_global_device_ids=true, to_apply=%region_19.20 | all-reduce | flops 2 | bytes 16 | tf_op jit(solution)/shard_map/psum | solution.py:171
  49.5 396.4 %while.14 = (s32[]{:T(128)}, f32[2,3,256]{2,1,0:T(4,128)}, f32[2]{0:T(128)}, f32[2,3,256]{2,1,0:T(4,128)}, s32[2,16,256]{2,1,0:T(8,128)}, /*index=5*/f32[8,64]{1...) while((s32[]{:T(128)}, f32[2,3,256]{2,1,0:T(4,128)}, ...), condition=%wide.region_17.18_spmd, body=%wide.region_0.17_spmd.sunk | while | flops 2677775104 | bytes 138035984 | solution.py:154
  53.2 2.8 collective-permute-done.1
  56.2 10.8 %gather_fusion = f32[4096,3]{1,0:T(8,128)S(1)} fusion(f32[3,512]{0,1:T(8,128)S(1)} %copy.334, s32[4096]{0:T(1024)S(1)} %broadcast_clamp_fusion.2), kind=kCustom, calls=%fused_computation.clone.1 | custom fusion | bytes 114688 | tf_op jit(solution)/shard_map/while/body/eval_jaxpr/jvp()/gather | solution.py:115
  70.8 3.9 multiply_bitcast_fusion.6
  74.8 4.5 multiply_bitcast_fusion.7
  80.4 2.4 multiply_reduce_fusion.26
  86.0 3.9 collective-permute-done.3
  89.9 15.4 %gather_fusion.1 = f32[4096,128]{1,0:T(8,128)} fusion(f32[128,512]{0,1:T(8,128)S(1)} %pad_maximum_fusion.7, s32[4096]{0:T(1024)} %copy-done.16), kind=kCustom, calls=%fused_computation.1.clone.1 | custom fusion | bytes 4210688 | tf_op jit(solution)/shard_map/while/body/eval_jaxpr/jvp()/gather | solution.py:127
  105.4 6.2 %bitcast_multiply_fusion.11 = (f32[128,16,256]{0,2,1:T(8,128)S(1)}, f32[16,256,128]{2,1,0:T(8,128)}) fusion(f32[128,16,256]{0,2,1:T(8,128)} %bitcast.269, f32[16,256]{1,0:T(8,128)S(1)} %dynamic-slice_bitcast_fusion.5, f32[64,128]{1,0:T(8,128)} %get-tuple-element.595, f32[64,16,256]{2,0,1:T(8,128)S(1)} %convolution_bitcast_fusion.12), kind=kOutput, calls=%fused_computation.19.clone.1 | convolution fusion | flops 404750336 | bytes 7389184 | tf_op jit(solution)/shard_map/while/body/eval_jaxpr/jvp(hka,hc->cka)/dot_general | solution.py:55
  111.6 4.5 multiply_bitcast_fusion.8
  119.1 6.2 %fusion.288 = f32[256,9,16]{2,1,0:T(8,128)} fusion(f32[128,16,256]{0,2,1:T(8,128)S(1)} %get-tuple-element.523, f32[128,1,256]{0,1,2:T(1,128)S(1)} %bitcast.277, f32[128,3,256]{0,1,2:T(4,128)S(1)} %slice_multiply_fusion.12, f32[128,5,256]{0,1,2:T(8,128)S(1)} %slice_multiply_fusion.13), kind=kOutput, calls=%fused_computation.25.clone.1 | convolution fusion | flops 58097664 | bytes 3424256 | tf_op jit(solution)/shard_map/while/body/eval_jaxpr/transpose(jvp(cka,lka->cla))/dot_general | solution.py:58
  125.2 4.6 fusion.282
  131.9 4.8 fusion.283
  136.8 2.4 bitcast_multiply_fusion.12
  140.9 22.7 %scatter_custom_fusion.9 = f32[128,512]{0,1:T(8,128)S(1)} fusion(s32[4096]{0:T(1024)S(1)} %bitcast.284, f32[4096,128]{1,0:T(8,128)} %bitcast.274, f32[]{:T(128)} %constant.107.clone.38..sunk), kind=kCustom, calls=%fused_computation.131.clone.1 | custom fusion | flops 524288 | bytes 262656 | tf_op jit(solution)/shard_map/while/body/eval_jaxpr/transpose(jvp())/scatter-add | solution.py:127
  166.8 3.6 collective-permute-done.5
  172.4 4.3 fusion.292
  176.7 6.2 %fusion.287 = f32[256,9,16]{2,1,0:T(8,128)} fusion(f32[128,16,256]{0,2,1:T(8,128)S(1)} %copy-done.4, f32[128,1,256]{0,1,2:T(1,128)S(1)} %bitcast.276, f32[128,3,256]{0,1,2:T(4,128)S(1)} %slice_multiply_fusion.14, f32[128,5,256]{0,1,2:T(8,128)S(1)} %slice_multiply_fusion.15), kind=kOutput, calls=%fused_computation.29.clone.1 | convolution fusion | flops 58097664 | bytes 3424256 | tf_op jit(solution)/shard_map/while/body/eval_jaxpr/transpose(jvp(cka,lka->cla))/dot_general | solution.py:58
  182.9 2.3 copy.338
  186.1 3.8 fusion.293
  194.2 22.8 %scatter_fusion = f32[3,512]{0,1:T(8,128)S(1)} fusion(f32[3,512]{0,1:T(8,128)S(1)} %pad.344, s32[4096]{0:T(1024)S(1)} %bitcast.285, f32[4096,3]{1,0:T(8,128)} %bitcast.272), kind=kCustom, calls=%fused_computation.3.clone.1 | custom fusion | flops 12288 | bytes 163840 | tf_op jit(solution)/shard_map/while/body/eval_jaxpr/transpose(jvp())/scatter-add | solution.py:115
  217.0 22.5 %scatter_fusion.1 = f32[3,512]{0,1:T(8,128)S(1)} fusion(f32[3,512]{0,1:T(8,128)S(1)} %pad.345, s32[4096]{0:T(1024)S(1)} %bitcast.286, f32[4096,3]{1,0:T(8,128)S(1)} %bitcast.271), kind=kCustom, calls=%fused_computation.4.clone.1 | custom fusion | flops 12288 | bytes 163840 | tf_op jit(solution)/shard_map/while/body/eval_jaxpr/transpose(jvp())/scatter-add | solution.py:122
  242.7 3.4 collective-permute-done.7
  250.7 2.8 collective-permute-done.1
  253.7 10.8 %gather_fusion = f32[4096,3]{1,0:T(8,128)S(1)} fusion(f32[3,512]{0,1:T(8,128)S(1)} %copy.334, s32[4096]{0:T(1024)S(1)} %broadcast_clamp_fusion.2), kind=kCustom, calls=%fused_computation.clone.1 | custom fusion | bytes 114688 | tf_op jit(solution)/shard_map/while/body/eval_jaxpr/jvp()/gather | solution.py:115
  268.3 3.9 multiply_bitcast_fusion.6
  272.3 4.5 multiply_bitcast_fusion.7
  283.3 3.9 collective-permute-done.3
  287.2 15.4 %gather_fusion.1 = f32[4096,128]{1,0:T(8,128)} fusion(f32[128,512]{0,1:T(8,128)S(1)} %pad_maximum_fusion.7, s32[4096]{0:T(1024)} %copy-done.16), kind=kCustom, calls=%fused_computation.1.clone.1 | custom fusion | bytes 4210688 | tf_op jit(solution)/shard_map/while/body/eval_jaxpr/jvp()/gather | solution.py:127
  302.6 6.2 %bitcast_multiply_fusion.11 = (f32[128,16,256]{0,2,1:T(8,128)S(1)}, f32[16,256,128]{2,1,0:T(8,128)}) fusion(f32[128,16,256]{0,2,1:T(8,128)} %bitcast.269, f32[16,256]{1,0:T(8,128)S(1)} %dynamic-slice_bitcast_fusion.5, f32[64,128]{1,0:T(8,128)} %get-tuple-element.595, f32[64,16,256]{2,0,1:T(8,128)S(1)} %convolution_bitcast_fusion.12), kind=kOutput, calls=%fused_computation.19.clone.1 | convolution fusion | flops 404750336 | bytes 7389184 | tf_op jit(solution)/shard_map/while/body/eval_jaxpr/jvp(hka,hc->cka)/dot_general | solution.py:55
  308.8 4.5 multiply_bitcast_fusion.8
  316.3 6.2 %fusion.288 = f32[256,9,16]{2,1,0:T(8,128)} fusion(f32[128,16,256]{0,2,1:T(8,128)S(1)} %get-tuple-element.523, f32[128,1,256]{0,1,2:T(1,128)S(1)} %bitcast.277, f32[128,3,256]{0,1,2:T(4,128)S(1)} %slice_multiply_fusion.12, f32[128,5,256]{0,1,2:T(8,128)S(1)} %slice_multiply_fusion.13), kind=kOutput, calls=%fused_computation.25.clone.1 | convolution fusion | flops 58097664 | bytes 3424256 | tf_op jit(solution)/shard_map/while/body/eval_jaxpr/transpose(jvp(cka,lka->cla))/dot_general | solution.py:58
  322.5 4.6 fusion.282
  329.2 4.8 fusion.283
  334.1 2.4 bitcast_multiply_fusion.12
  338.1 22.7 %scatter_custom_fusion.9 = f32[128,512]{0,1:T(8,128)S(1)} fusion(s32[4096]{0:T(1024)S(1)} %bitcast.284, f32[4096,128]{1,0:T(8,128)} %bitcast.274, f32[]{:T(128)} %constant.107.clone.38..sunk), kind=kCustom, calls=%fused_computation.131.clone.1 | custom fusion | flops 524288 | bytes 262656 | tf_op jit(solution)/shard_map/while/body/eval_jaxpr/transpose(jvp())/scatter-add | solution.py:127
  364.1 3.6 collective-permute-done.5
  369.7 4.3 fusion.292
  374.0 6.2 %fusion.287 = f32[256,9,16]{2,1,0:T(8,128)} fusion(f32[128,16,256]{0,2,1:T(8,128)S(1)} %copy-done.4, f32[128,1,256]{0,1,2:T(1,128)S(1)} %bitcast.276, f32[128,3,256]{0,1,2:T(4,128)S(1)} %slice_multiply_fusion.14, f32[128,5,256]{0,1,2:T(8,128)S(1)} %slice_multiply_fusion.15), kind=kOutput, calls=%fused_computation.29.clone.1 | convolution fusion | flops 58097664 | bytes 3424256 | tf_op jit(solution)/shard_map/while/body/eval_jaxpr/transpose(jvp(cka,lka->cla))/dot_general | solution.py:58
  380.2 2.3 copy.338
  383.4 3.8 fusion.293
  391.4 22.8 %scatter_fusion = f32[3,512]{0,1:T(8,128)S(1)} fusion(f32[3,512]{0,1:T(8,128)S(1)} %pad.344, s32[4096]{0:T(1024)S(1)} %bitcast.285, f32[4096,3]{1,0:T(8,128)} %bitcast.272), kind=kCustom, calls=%fused_computation.3.clone.1 | custom fusion | flops 12288 | bytes 163840 | tf_op jit(solution)/shard_map/while/body/eval_jaxpr/transpose(jvp())/scatter-add | solution.py:115
  414.2 22.5 %scatter_fusion.1 = f32[3,512]{0,1:T(8,128)S(1)} fusion(f32[3,512]{0,1:T(8,128)S(1)} %pad.345, s32[4096]{0:T(1024)S(1)} %bitcast.286, f32[4096,3]{1,0:T(8,128)S(1)} %bitcast.271), kind=kCustom, calls=%fused_computation.4.clone.1 | custom fusion | flops 12288 | bytes 163840 | tf_op jit(solution)/shard_map/while/body/eval_jaxpr/transpose(jvp())/scatter-add | solution.py:122
  440.0 3.4 collective-permute-done.7
  446.9 28.6 %all-reduce.19 = (f32[2]{0:T(128)S(1)}, f32[2]{0:T(128)S(1)}, f32[2]{0:T(128)S(1)}, f32[2]{0:T(128)S(1)}) all-reduce(f32[2]{0:T(128)} %get-tuple-element.307, f32[2]{0:T(128)} %get-tuple-element.305, f32[2]{0:T(128)S(1)} %get-tuple-element.354, f32[2]{0:T(128)} %get-tuple-element.180), channel_id=1, replica_groups=mesh['image'=8,'space'=16] {'space'}, use_global_device_ids=true, to_apply=%region_25.26 | all-reduce | flops 8 | bytes 64 | tf_op jit(solution)/shard_map/psum | solution.py:171
  477.4 86.4 %all-reduce.18 = (f32[]{:T(128)}, f32[]{:T(128)}) all-reduce(f32[]{:T(128)} %multiply_reduce_fusion.14, f32[]{:T(128)} %get-tuple-element.352), channel_id=1, replica_groups=mesh['image'=8,'space'=16] {'image','space'}, use_global_device_ids=true, to_apply=%region_27.28 | all-reduce | flops 2 | bytes 16 | tf_op jit(solution)/shard_map/psum | solution.py:181
  (323 shorter events, 79.0 us)
Async XLA Ops:
  2.6 46.9 %copy-start.32 = (f32[1,3,256]{2,1,0:T(4,128)}, f32[1,3,256]{2,1,0:T(4,128)S(1)}, u32[]{:S(2)}) copy-start(f32[1,3,256]{2,1,0:T(4,128)S(1)} %get-tuple-element.387) | copy-start | bytes 9220
  2.6 46.9 %copy-start.33 = (f32[1,3,256]{2,1,0:T(4,128)}, f32[1,3,256]{2,1,0:T(4,128)S(1)}, u32[]{:S(2)}) copy-start(f32[1,3,256]{2,1,0:T(4,128)S(1)} %get-tuple-element.388) | copy-start | bytes 9220
  2.6 9.7 %collective-permute-start.9 = (f32[1,3,256]{2,1,0:T(4,128)S(1)}, f32[1,3,256]{2,1,0:T(4,128)S(1)}, u32[]{:S(2)}, u32[]{:S(2)}) collective-permute-start(f32[1,3,256]{2,1,0:T(4,128)S(1)} %get-tuple-element.387), channel_id=1, source_target_pairs={{0,16},{16,32},{32,48},{48,64},{64,80},{80,96},{96,112},{1,17},{17... | collective-permute-start | bytes 9224 | tf_op jit(solution)/shard_map/ppermute | solution.py:19
  7.1 5.3 collective-permute-start.8
  50.2 19.5 %copy-start.10 = (f32[3,256]{1,0:T(4,128)}, f32[3,256]{1,0:T(4,128)S(1)}, u32[]{:S(2)}) copy-start(f32[3,256]{1,0:T(4,128)S(1)} %dynamic-slice_bitcast_fusion.4) | copy-start | bytes 9220 | tf_op jit(solution)/shard_map/while
  50.2 3.0 collective-permute-start
  50.2 5.8 %collective-permute-start.1 = (f32[3,128]{1,0:T(4,128)S(1)}, f32[3,128]{1,0:T(4,128)S(1)}, u32[]{:S(2)}, u32[]{:S(2)}) collective-permute-start(f32[3,128]{1,0:T(4,128)S(1)} %get-tuple-element.516), channel_id=1, source_target_pairs={{0,1},{1,2},{2,3},{3,4},{4,5},{5,6},{6,7},{7,8},{8,9},{9,10},{10,1... | collective-permute-start | bytes 4616 | tf_op jit(solution)/shard_map/while/body/eval_jaxpr/ppermute | solution.py:19
  53.2 14.5 %copy-start.16 = (s32[4096]{0:T(1024)}, s32[4096]{0:T(1024)S(1)}, u32[]{:S(2)}) copy-start(s32[4096]{0:T(1024)S(1)} %broadcast_clamp_fusion.2) | copy-start | bytes 49156 | tf_op jit(solution)/shard_map/while
  53.2 16.6 %copy-start.26 = (f32[8]{0:T(128)}, f32[8]{0:T(128)S(1)}, u32[]{:S(2)}) copy-start(f32[8]{0:T(128)S(1)} %convert_multiply_fusion.2) | copy-start | bytes 100 | tf_op jit(solution)/shard_map/while
  79.3 6.1 %copy-start.1 = (f32[128,9,256]{0,1,2:T(8,128)}, f32[128,9,256]{0,1,2:T(8,128)S(1)}, u32[]{:S(2)}) copy-start(f32[128,9,256]{0,1,2:T(8,128)S(1)} %multiply_bitcast_fusion.7) | copy-start | bytes 3538948 | tf_op jit(solution)/shard_map/while
  79.3 5.0 copy-start.24
  79.3 5.0 copy-start.27
  82.8 3.2 collective-permute-start.2
  83.5 6.4 %collective-permute-start.3 = (f32[128,128]{0,1:T(8,128)S(1)}, f32[128,128]{0,1:T(8,128)S(1)}, u32[]{:S(2)}, u32[]{:S(2)}) collective-permute-start(f32[128,128]{0,1:T(8,128)S(1)} %get-tuple-element.522), channel_id=1, source_target_pairs={{0,1},{1,2},{2,3},{3,4},{4,5},{5,6},{6,7},{7,8},{8,9},{9,10},{10,1... | collective-permute-start | bytes 196616 | tf_op jit(solution)/shard_map/while/body/eval_jaxpr/ppermute | solution.py:19
  131.9 33.4 %copy-start.9 = (f32[256,9,16]{0,2,1:T(8,128)}, f32[256,9,16]{0,2,1:T(8,128)S(1)}, u32[]{:S(2)}) copy-start(f32[256,9,16]{0,2,1:T(8,128)S(1)} %copy.339) | copy-start | bytes 442372 | tf_op jit(solution)/shard_map/while
  131.9 4.8 copy-start
  131.9 4.8 copy-start.5
  163.6 8.4 %copy-start.2 = (f32[128,9,256]{0,1,2:T(8,128)S(1)}, f32[128,9,256]{0,1,2:T(8,128)}, u32[]{:S(2)}) copy-start(f32[128,9,256]{0,1,2:T(8,128)} %copy-done.1) | copy-start | bytes 3538948 | tf_op jit(solution)/shard_map/while
  163.6 3.2 collective-permute-start.4
  163.7 6.7 %collective-permute-start.5 = (f32[128,128]{0,1:T(8,128)S(1)}, f32[128,128]{0,1:T(8,128)S(1)}, u32[]{:S(2)}, u32[]{:S(2)}) collective-permute-start(f32[128,128]{0,1:T(8,128)S(1)} %get-tuple-element.531), channel_id=1, source_target_pairs={{0,1},{1,2},{2,3},{3,4},{4,5},{5,6},{6,7},{7,8},{8,9},{9,10},{10,1... | collective-permute-start | bytes 196616 | tf_op jit(solution)/shard_map/while/body/eval_jaxpr/ppermute | solution.py:19
  185.2 4.7 copy-start.23
  185.2 4.7 copy-start.29
  193.5 48.8 %copy-start.38 = (f32[2]{0:T(128)S(1)}, f32[2]{0:T(128)}, u32[]{:S(2)}) copy-start(f32[2]{0:T(128)} %get-tuple-element.572) | copy-start | bytes 28 | tf_op jit(solution)/shard_map/while
  194.2 52.0 %copy-start.34 = (f32[2,3,256]{2,1,0:T(4,128)S(1)}, f32[2,3,256]{2,1,0:T(4,128)}, u32[]{:S(2)}) copy-start(f32[2,3,256]{2,1,0:T(4,128)} %get-tuple-element.571) | copy-start | bytes 18436 | tf_op jit(solution)/shard_map/while
  239.5 3.2 collective-permute-start.6
  239.6 6.5 %collective-permute-start.7 = (f32[3,128]{0,1:T(8,128)S(1)}, f32[3,128]{0,1:T(8,128)S(1)}, u32[]{:S(2)}, u32[]{:S(2)}) collective-permute-start(f32[3,128]{0,1:T(8,128)S(1)} %get-tuple-element.551), channel_id=1, source_target_pairs={{0,1},{1,2},{2,3},{3,4},{4,5},{5,6},{6,7},{7,8},{8,9},{9,10},{10,1... | collective-permute-start | bytes 4616 | tf_op jit(solution)/shard_map/while/body/eval_jaxpr/ppermute | solution.py:19
  247.7 19.5 %copy-start.10 = (f32[3,256]{1,0:T(4,128)}, f32[3,256]{1,0:T(4,128)S(1)}, u32[]{:S(2)}) copy-start(f32[3,256]{1,0:T(4,128)S(1)} %dynamic-slice_bitcast_fusion.4) | copy-start | bytes 9220 | tf_op jit(solution)/shard_map/while
  247.7 3.0 collective-permute-start
  247.7 5.8 %collective-permute-start.1 = (f32[3,128]{1,0:T(4,128)S(1)}, f32[3,128]{1,0:T(4,128)S(1)}, u32[]{:S(2)}, u32[]{:S(2)}) collective-permute-start(f32[3,128]{1,0:T(4,128)S(1)} %get-tuple-element.516), channel_id=1, source_target_pairs={{0,1},{1,2},{2,3},{3,4},{4,5},{5,6},{6,7},{7,8},{8,9},{9,10},{10,1... | collective-permute-start | bytes 4616 | tf_op jit(solution)/shard_map/while/body/eval_jaxpr/ppermute | solution.py:19
  250.6 14.5 %copy-start.16 = (s32[4096]{0:T(1024)}, s32[4096]{0:T(1024)S(1)}, u32[]{:S(2)}) copy-start(s32[4096]{0:T(1024)S(1)} %broadcast_clamp_fusion.2) | copy-start | bytes 49156 | tf_op jit(solution)/shard_map/while
  250.6 16.6 %copy-start.26 = (f32[8]{0:T(128)}, f32[8]{0:T(128)S(1)}, u32[]{:S(2)}) copy-start(f32[8]{0:T(128)S(1)} %convert_multiply_fusion.2) | copy-start | bytes 100 | tf_op jit(solution)/shard_map/while
  276.7 6.0 %copy-start.1 = (f32[128,9,256]{0,1,2:T(8,128)}, f32[128,9,256]{0,1,2:T(8,128)S(1)}, u32[]{:S(2)}) copy-start(f32[128,9,256]{0,1,2:T(8,128)S(1)} %multiply_bitcast_fusion.7) | copy-start | bytes 3538948 | tf_op jit(solution)/shard_map/while
  276.8 4.9 copy-start.24
  276.8 4.9 copy-start.27
  280.1 3.2 collective-permute-start.2
  280.7 6.4 %collective-permute-start.3 = (f32[128,128]{0,1:T(8,128)S(1)}, f32[128,128]{0,1:T(8,128)S(1)}, u32[]{:S(2)}, u32[]{:S(2)}) collective-permute-start(f32[128,128]{0,1:T(8,128)S(1)} %get-tuple-element.522), channel_id=1, source_target_pairs={{0,1},{1,2},{2,3},{3,4},{4,5},{5,6},{6,7},{7,8},{8,9},{9,10},{10,1... | collective-permute-start | bytes 196616 | tf_op jit(solution)/shard_map/while/body/eval_jaxpr/ppermute | solution.py:19
  329.2 33.4 %copy-start.9 = (f32[256,9,16]{0,2,1:T(8,128)}, f32[256,9,16]{0,2,1:T(8,128)S(1)}, u32[]{:S(2)}) copy-start(f32[256,9,16]{0,2,1:T(8,128)S(1)} %copy.339) | copy-start | bytes 442372 | tf_op jit(solution)/shard_map/while
  329.2 4.8 copy-start
  329.2 4.8 copy-start.5
  360.8 8.4 %copy-start.2 = (f32[128,9,256]{0,1,2:T(8,128)S(1)}, f32[128,9,256]{0,1,2:T(8,128)}, u32[]{:S(2)}) copy-start(f32[128,9,256]{0,1,2:T(8,128)} %copy-done.1) | copy-start | bytes 3538948 | tf_op jit(solution)/shard_map/while
  360.9 3.2 collective-permute-start.4
  361.0 6.7 %collective-permute-start.5 = (f32[128,128]{0,1:T(8,128)S(1)}, f32[128,128]{0,1:T(8,128)S(1)}, u32[]{:S(2)}, u32[]{:S(2)}) collective-permute-start(f32[128,128]{0,1:T(8,128)S(1)} %get-tuple-element.531), channel_id=1, source_target_pairs={{0,1},{1,2},{2,3},{3,4},{4,5},{5,6},{6,7},{7,8},{8,9},{9,10},{10,1... | collective-permute-start | bytes 196616 | tf_op jit(solution)/shard_map/while/body/eval_jaxpr/ppermute | solution.py:19
  382.5 4.7 copy-start.23
  382.5 4.7 copy-start.29
  390.8 48.8 %copy-start.38 = (f32[2]{0:T(128)S(1)}, f32[2]{0:T(128)}, u32[]{:S(2)}) copy-start(f32[2]{0:T(128)} %get-tuple-element.572) | copy-start | bytes 28 | tf_op jit(solution)/shard_map/while
  391.4 52.0 %copy-start.34 = (f32[2,3,256]{2,1,0:T(4,128)S(1)}, f32[2,3,256]{2,1,0:T(4,128)}, u32[]{:S(2)}) copy-start(f32[2,3,256]{2,1,0:T(4,128)} %get-tuple-element.571) | copy-start | bytes 18436 | tf_op jit(solution)/shard_map/while
  436.8 3.2 collective-permute-start.6
  436.9 6.5 %collective-permute-start.7 = (f32[3,128]{0,1:T(8,128)S(1)}, f32[3,128]{0,1:T(8,128)S(1)}, u32[]{:S(2)}, u32[]{:S(2)}) collective-permute-start(f32[3,128]{0,1:T(8,128)S(1)} %get-tuple-element.551), channel_id=1, source_target_pairs={{0,1},{1,2},{2,3},{3,4},{4,5},{5,6},{6,7},{7,8},{8,9},{9,10},{10,1... | collective-permute-start | bytes 4616 | tf_op jit(solution)/shard_map/while/body/eval_jaxpr/ppermute | solution.py:19
  (46 other events, 105.6 us)
where the time goes:
time: 571 us; the launch traced here: 568 us
  other arithmetic  158 us (28%)
  blocking collectives  150 us (26%)
  matrix products  118 us (21%)
  local copies, waits for them, and re-layouts  81.4 us (14%)
  waiting for transfers between devices  31.9 us (6%)
  starting transfers between devices  18.9 us (3%)
  loops' own time  6.27 us (1%)
    psum x1, blocking collectives, local(): lax.psum((jnp.sum(velocity * velocity), jnp.sum(neb_force * neb_force)),...  86.4 us
    psum x2, blocking collectives, local(): lax.psum((ahead_loc, behind_loc, spread_loc, energies), 'space')  63.3 us
    dot_general x12, matrix products, layer_out(): jnp.einsum('cka,lka->cla', radial, angular, precision=highest)  60.4 us
    scatter-add x2, other arithmetic, first_layer(): ext_pos[:, nb_idx]  45.6 us
    scatter-add x2, other arithmetic, second_energy(): ext_feat[:, nb_idx]  45.4 us
    scatter-add x2, other arithmetic, second_energy(): ext_pos[:, nb_idx]  45 us
    dot_general x8, matrix products, layer_out(): jnp.einsum('hka,hc->cka', hidden, radial_b, precision=highest)  37.5 us
    gather x2, local copies, waits for them, and re-layouts, second_energy(): ext_feat[:, nb_idx]  30.9 us
  transfers between devices with their start and end apart: 18, of which 14 were waited for; matrix products, arithmetic and copies ran while one was open for 1% of the time, Pallas kernels for 0%

commit v1 on v0

v1 whole, which is shorter than its diff:
```python
import functools
import math

import jax
import jax.numpy as jnp
from jax import lax
from jax.experimental import pallas as pl
from jax.experimental.pallas import tpu as pltpu
from jax.sharding import PartitionSpec as P

f32 = jnp.float32
bf16 = jnp.bfloat16
RT3 = math.sqrt(3.0)
NL = 9


def split(x):
    hi = x.astype(bf16)
    lo = (x - hi.astype(f32)).astype(bf16)
    return hi, lo


def dot(a, b):
    return lax.dot_general(a, b, (((1,), (0,)), ((), ())), preferred_element_type=f32)


def dot_nt(a, b):
    return lax.dot_general(a, b, (((1,), (1,)), ((), ())), preferred_element_type=f32)


def pack_left(w):
    hi, lo = split(w)
    return jnp.concatenate([hi, hi, lo], axis=1)


def pack_right(x):
    hi, lo = split(x)
    return jnp.concatenate([hi, lo, hi], axis=0)


def one_hot(row, extent):
    ids = lax.broadcasted_iota(jnp.int32, (extent, row.shape[1]), 0)
    return jnp.where(ids == row, 1.0, 0.0).astype(bf16)


def silu_parts(z):
    s = 0.5 + 0.5 * jnp.tanh(0.5 * z)
    h = z * s
    return h, s + h * (1.0 - s)


def basis_of(row, nb):
    centres = 0.5 * lax.broadcasted_iota(jnp.int32, (nb, row.shape[1]), 0).astype(f32)
    spread = row - centres
    basis = jnp.exp(-2.0 * spread * spread)
    return basis, -4.0 * spread * basis


def moments_into(edge_tile, yb_ref, m_ref, chans, slots, atoms):
    def tile(t, carry):
        c0 = pl.multiple_of(t * 16, 16)
        for a0 in range(0, atoms, 128):
            acc = [jnp.zeros((16, 128), f32) for _ in range(NL)]
            for k in range(slots):
                e = edge_tile(k, c0, a0)
                for l in range(NL):
                    y = yb_ref[k, l, :, a0 : a0 + 128]
                    acc[l] = acc[l] + e * jnp.concatenate([y, y], axis=0)
            for l in range(NL):
                m_ref[l, pl.ds(c0, 16), a0 : a0 + 128] = acc[l]
        return carry

    lax.fori_loop(0, chans // 16, tile, 0)


def store_yb(yb_ref, ylive, slots, atoms):
    for k in range(slots):
        for l in range(NL):
            yb_ref[k, l] = jnp.broadcast_to(ylive[l][k : k + 1], (8, atoms))


def invariants_of(m_ref):
    m = [m_ref[l] for l in range(NL)]
    one = m[1] * m[1] + m[2] * m[2] + m[3] * m[3]
    two = m[4] * m[4] + m[5] * m[5] + m[6] * m[6] + m[7] * m[7] + m[8] * m[8]
    return jnp.concatenate([m[0], one, two], axis=0)


def moment_grads_into(m_ref, dinv, chans):
    m_ref[0] = dinv[:chans]
    d1 = 2.0 * dinv[chans : 2 * chans]
    d2 = 2.0 * dinv[2 * chans :]
    for l in range(1, NL):
        m_ref[l] = m_ref[l] * (d1 if l < 4 else d2)


def first_kernel(
    pos_ref, plo_ref, pup_ref, idx_ref, cnt_ref, a_ref, b_ref, mix_ref, read_ref,
    head_ref, tail_ref, geo_ref, hid_ref, ds_ref, mom_ref, dpre_ref, en_ref,
    yb_ref, g_ref, nb_ref,
):
    slots, atoms = idx_ref.shape[1:]
    ghost = plo_ref.shape[2]
    nb, rh = a_ref.shape
    ch = b_ref.shape[1]
    pos = pos_ref[0]
    ext = jnp.concatenate([plo_ref[0], pos, pup_ref[0]], axis=1)
    extent = ext.shape[1]
    p1 = ext.astype(bf16)
    rest = ext - p1.astype(f32)
    p2 = rest.astype(bf16)
    p3 = (rest - p2.astype(f32)).astype(bf16)
    pad = jnp.zeros((5, extent), f32)
    pieces = jnp.concatenate(
        [jnp.concatenate([p.astype(f32), pad], axis=0) for p in (p1, p2, p3)], axis=0
    ).astype(bf16)
    for k in range(slots):
        oh = one_hot(idx_ref[0, k : k + 1, :], extent)
        got = dot(pieces, oh)
        for x in range(3):
            nb_ref[x, k : k + 1, :] = (
                got[x : x + 1] + got[8 + x : 9 + x] + got[16 + x : 17 + x]
            )
    off = [nb_ref[x] - pos[x : x + 1] for x in range(3)]
    length = jnp.sqrt(off[0] * off[0] + off[1] * off[1] + off[2] * off[2] + 1.0)
    ux, uy, uz = [o / length for o in off]
    ids = lax.broadcasted_iota(jnp.int32, (slots, atoms), 0)
    live = jnp.where(ids < cnt_ref[0], 1.0 / slots, 0.0).astype(f32)
    ylive = [
        live,
        live * ux,
        live * uy,
        live * uz,
        live * (ux * uy),
        live * (uy * uz),
        live * (ux * uz),
        live * (0.5 * (ux * ux - uy * uy)),
        live * ((3.0 * uz * uz - 1.0) / (2.0 * RT3)),
    ]
    for l in range(NL):
        geo_ref[0, l] = ylive[l]
    geo_ref[0, NL] = ux
    geo_ref[0, NL + 1] = uy
    geo_ref[0, NL + 2] = uz
    geo_ref[0, NL + 3] = length
    store_yb(yb_ref, ylive, slots, atoms)
    a_pack = pack_left(a_ref[...].T)
    for k in range(slots):
        basis, _ = basis_of(length[k : k + 1], nb)
        hid, ds = silu_parts(dot(a_pack, pack_right(basis)))
        hid_ref[0, k] = hid
        ds_ref[0, k] = ds

    def hid_tile(k, c0, a0):
        return hid_ref[0, k, pl.ds(c0, 16), a0 : a0 + 128]

    moments_into(hid_tile, yb_ref, g_ref, rh, slots, atoms)
    b_pack = pack_left(b_ref[...].T)
    for l in range(NL):
        mom_ref[0, l] = dot(b_pack, pack_right(g_ref[l]))
    inv = invariants_of(mom_ref.at[0])
    feat, dpre = silu_parts(dot(pack_left(mix_ref[...].T), pack_right(inv)))
    dpre_ref[0] = dpre
    head_ref[0] = feat[:, :ghost]
    tail_ref[0] = feat[:, atoms - ghost :]
    en = read_ref[...] * feat
    total = jnp.sum(en.reshape(ch // 8, 8, atoms), axis=0)
    en_ref[0] = total[:, :128] + total[:, 128:]


def edge_back(k, edge_tile, sink, yb_ref, m_ref, dy_ref, chans, atoms):
    for a0 in range(0, atoms, 128):
        y = [yb_ref[k, l, :, a0 : a0 + 128] for l in range(NL)]
        y = [jnp.concatenate([v, v], axis=0) for v in y]
        acc = [jnp.zeros((8, 128), f32) for _ in range(NL)]
        for c0 in range(0, chans, 16):
            e = edge_tile(k, c0, a0)
            de = None
            for l in range(NL):
                dm = m_ref[l, c0 : c0 + 16, a0 : a0 + 128]
                term = dm * y[l]
                de = term if de is None else de + term
                p = e * dm
                acc[l] = acc[l] + (p[:8] + p[8:])
            sink(k, c0, a0, de)
        for l in range(NL):
            dy_ref[0, l, k : k + 1, a0 : a0 + 128] = jnp.sum(acc[l], axis=0, keepdims=True)


def second_kernel(
    head_ref, tail_ref, hlo_ref, hup_ref, idx_ref, geo_ref, a_ref, b_ref, mix_ref, read_ref,
    dfh_ref, dft_ref, dlo_ref, dup_ref, dy_ref, dlen_ref, en_ref,
    yb_ref, hf_ref, oh_ref, q_ref, rad_ref, ds_ref, m_ref, dq_ref, dr_ref,
):
    slots, atoms = idx_ref.shape[1:]
    ghost = hlo_ref.shape[2]
    nb, rh = a_ref.shape
    ch = b_ref.shape[1]
    extent = atoms + 2 * ghost
    parts = (hlo_ref, head_ref, tail_ref, hup_ref)
    for n, ref in enumerate(parts):
        hi, lo = split(ref[0])
        hf_ref[:ch, n * ghost : (n + 1) * ghost] = hi
        hf_ref[ch:, n * ghost : (n + 1) * ghost] = lo
    store_yb(yb_ref, [geo_ref[0, l] for l in range(NL)], slots, atoms)
    a_pack = pack_left(a_ref[...].T)
    b_pack = pack_left(b_ref[...].T)
    for k in range(slots):
        oh = one_hot(idx_ref[0, k : k + 1, :], extent)
        oh_ref[:, k * atoms : (k + 1) * atoms] = oh
        got = dot(hf_ref[...], oh)
        q_ref[k] = got[:ch] + got[ch:]
        basis, _ = basis_of(geo_ref[0, NL + 3, k : k + 1, :], nb)
        hid, ds = silu_parts(dot(a_pack, pack_right(basis)))
        ds_ref[k] = ds
        rad_ref[k] = dot(b_pack, pack_right(hid))

    def edge_tile(k, c0, a0):
        cs = pl.ds(c0, 16)
        return rad_ref[k, cs, a0 : a0 + 128] * q_ref[k, cs, a0 : a0 + 128]

    moments_into(edge_tile, yb_ref, m_ref, ch, slots, atoms)
    inv = invariants_of(m_ref)
    mix = mix_ref[...]
    feat, dpre = silu_parts(dot(pack_left(mix.T), pack_right(inv)))
    en = read_ref[...] * feat
    total = jnp.sum(en.reshape(ch // 8, 8, atoms), axis=0)
    en_ref[0] = total[:, :128] + total[:, 128:]
    dpre = read_ref[...] * dpre
    dinv = dot(pack_left(mix), pack_right(dpre))
    moment_grads_into(m_ref, dinv, ch)
    bt_pack = pack_left(b_ref[...])
    at_pack = pack_left(a_ref[...])

    def slot(k):
        k0 = k * atoms

        def sink(kk, c0, a0, de):
            cs = slice(c0, c0 + 16)
            hi, lo = split(de * rad_ref[kk, cs, a0 : a0 + 128])
            ls = slice(k0 + a0, k0 + a0 + 128)
            dq_ref[cs, ls] = hi
            dq_ref[ch + c0 : ch + c0 + 16, ls] = lo
            hi, lo = split(de * q_ref[kk, cs, a0 : a0 + 128])
            dr_ref[cs, a0 : a0 + 128] = hi
            dr_ref[ch + c0 : ch + c0 + 16, a0 : a0 + 128] = lo
            dr_ref[2 * ch + c0 : 2 * ch + c0 + 16, a0 : a0 + 128] = hi

        edge_back(k, edge_tile, sink, yb_ref, m_ref, dy_ref, ch, atoms)
        dz = dot(bt_pack, dr_ref[...]) * ds_ref[k]
        dbasis = dot(at_pack, pack_right(dz))
        _, slope = basis_of(geo_ref[0, NL + 3, k : k + 1, :], nb)
        dlen_ref[0, k : k + 1, :] = jnp.sum(dbasis * slope, axis=0, keepdims=True)

    for k in range(slots):
        slot(k)
    back = dot_nt(dq_ref[...], oh_ref[...])
    back = back[:ch] + back[ch:]
    dlo_ref[0] = back[:, :ghost]
    dfh_ref[0] = back[:, ghost : 2 * ghost]
    dft_ref[0] = back[:, 2 * ghost : 3 * ghost]
    dup_ref[0] = back[:, 3 * ghost :]


def third_kernel(
    dfh_ref, dft_ref, rlo_ref, rup_ref, idx_ref, geo_ref, hid_ref, ds_ref, mom_ref, dpre_ref,
    dy2_ref, dlen2_ref, a_ref, b_ref, mix_ref, read_ref,
    own_ref, flo_ref, fup_ref,
    yb_ref, m_ref, dg_ref, dy_ref, dr_ref, dlen_ref, doff_ref,
):
    slots, atoms = idx_ref.shape[1:]
    ghost = rlo_ref.shape[2]
    nb, rh = a_ref.shape
    ch = b_ref.shape[1]
    extent = atoms + 2 * ghost
    store_yb(yb_ref, [geo_ref[0, l] for l in range(NL)], slots, atoms)
    cot = jnp.concatenate([dfh_ref[0] + rlo_ref[0], dft_ref[0] + rup_ref[0]], axis=1)
    dpre = (cot + read_ref[...]) * dpre_ref[0]
    dinv = dot(pack_left(mix_ref[...]), pack_right(dpre))
    for l in range(NL):
        m_ref[l] = mom_ref[0, l]
    moment_grads_into(m_ref, dinv, ch)
    bt_pack = pack_left(b_ref[...])
    at_pack = pack_left(a_ref[...])
    for l in range(NL):
        dg_ref[l] = dot(bt_pack, pack_right(m_ref[l]))

    def edge_tile(k, c0, a0):
        return hid_ref[0, k, pl.ds(c0, 16), a0 : a0 + 128]

    def slot(k):
        def sink(kk, c0, a0, de):
            cs = slice(c0, c0 + 16)
            hi, lo = split(de * ds_ref[0, kk, cs, a0 : a0 + 128])
            dr_ref[cs, a0 : a0 + 128] = hi
            dr_ref[rh + c0 : rh + c0 + 16, a0 : a0 + 128] = lo
            dr_ref[2 * rh + c0 : 2 * rh + c0 + 16, a0 : a0 + 128] = hi

        edge_back(k, edge_tile, sink, yb_ref, dg_ref, dy_ref, rh, atoms)
        dbasis = dot(at_pack, dr_ref[...])
        _, slope = basis_of(geo_ref[0, NL + 3, k : k + 1, :], nb)
        dlen_ref[k : k + 1, :] = jnp.sum(dbasis * slope, axis=0, keepdims=True)

    for k in range(slots):
        slot(k)
    live = geo_ref[0, 0]
    dy = [live * (dy_ref[0, l] + dy2_ref[0, l]) for l in range(NL)]
    ux, uy, uz, length = [geo_ref[0, NL + n] for n in range(4)]
    dux = dy[1] + uy * dy[4] + uz * dy[6] + ux * dy[7]
    duy = dy[2] + ux * dy[4] + uz * dy[5] - uy * dy[7]
    duz = dy[3] + uy * dy[5] + ux * dy[6] + RT3 * uz * dy[8]
    radial = dlen_ref[...] + dlen2_ref[0] - (dux * ux + duy * uy + duz * uz) / length
    doff = [du / length + radial * u for du, u in ((dux, ux), (duy, uy), (duz, uz))]
    centre = jnp.concatenate([jnp.sum(d, axis=0, keepdims=True) for d in doff], axis=0)
    for x in range(3):
        doff_ref[x] = doff[x]
    back = jnp.zeros((16, extent), f32)
    pad = jnp.zeros((5, atoms), f32)
    for k in range(slots):
        rows = jnp.concatenate([doff_ref[x, k : k + 1, :] for x in range(3)] + [pad], axis=0)
        hi = rows.astype(bf16).astype(f32)
        both = jnp.concatenate([hi, rows - hi], axis=0).astype(bf16)
        back = back + dot_nt(both, one_hot(idx_ref[0, k : k + 1, :], extent))
    force = back[8:11] + back[:3]
    own_ref[0] = centre - force[:, ghost : ghost + atoms]
    flo_ref[0] = -force[:, :ghost]
    fup_ref[0] = -force[:, ghost + atoms :]


def lane_row(values):
    lane = lax.broadcasted_iota(jnp.int32, (1, 128), 1)
    row = jnp.zeros((1, 128), f32)
    for n, v in enumerate(values):
        row = jnp.where(lane == n, v, row)
    return row


def total_of(x):
    return jnp.sum(jnp.sum(x, axis=1, keepdims=True), axis=0, keepdims=True)


def chain_of(pos_ref, before_ref, after_ref, start_ref, end_ref, edge_ref):
    count = pos_ref.shape[0]
    before = jnp.where(edge_ref[0] > 0, start_ref[...], before_ref[...])
    after = jnp.where(edge_ref[1] > 0, end_ref[...], after_ref[...])
    prev = [before] + [pos_ref[i] for i in range(count - 1)]
    nxt = [pos_ref[i] for i in range(1, count)] + [after]
    return prev, nxt


def partial_kernel(
    edge_ref, own_ref, rlo_ref, rup_ref, pos_ref, before_ref, after_ref, start_ref, end_ref,
    vel_ref, en1_ref, en2_ref, force_ref, send_ref,
):
    count = pos_ref.shape[0]
    prev, nxt = chain_of(pos_ref, before_ref, after_ref, start_ref, end_ref, edge_ref)
    values = []
    vel = jnp.zeros((1, 1), f32)
    for i in range(count):
        force = own_ref[i] + jnp.concatenate([rlo_ref[i], rup_ref[i]], axis=1)
        force_ref[i] = force
        spread = nxt[i] - prev[i]
        ahead = nxt[i] - pos_ref[i]
        behind = pos_ref[i] - prev[i]
        values += [
            total_of(ahead * ahead),
            total_of(behind * behind),
            total_of(spread * spread),
            total_of(force * force),
            total_of(force * spread),
            total_of(en1_ref[i]) + total_of(en2_ref[i]),
        ]
        v = vel_ref[i]
        vel = vel + total_of(v * v)
    send_ref[...] = jnp.broadcast_to(lane_row(values + [vel]), send_ref.shape)


def final_kernel(
    edge_ref, got_ref, climb_ref, force_ref, pos_ref, before_ref, after_ref, start_ref, end_ref,
    vel_ref, neb_ref, vnext_ref, pnext_ref, en_ref,
    *, images, slabs,
):
    count = pos_ref.shape[0]
    atoms = pos_ref.shape[2]
    me = edge_ref[2]
    prev, nxt = chain_of(pos_ref, before_ref, after_ref, start_ref, end_ref, edge_ref)
    rows = [
        jnp.sum(got_ref[g * slabs : (g + 1) * slabs, :], axis=0, keepdims=True)
        for g in range(images)
    ]
    table = jnp.concatenate(rows, axis=0)
    vel_sq = jnp.sum(table[:, 6 * count : 6 * count + 1], axis=0, keepdims=True)
    group = lax.broadcasted_iota(jnp.int32, (images, 1), 0)
    force_sq = jnp.zeros((1, 1), f32)
    mine = []
    for i in range(count):
        ahead, behind, spread_sq, ff, fd, energy = [
            table[:, 6 * i + n : 6 * i + n + 1] for n in range(6)
        ]
        norm = 1.0 / jnp.sqrt(spread_sq + 1e-06)
        along = fd * norm
        climbing = jnp.where(group * count + i == climb_ref[0], 1.0, 0.0).astype(f32)
        spring = 5.0 * (jnp.sqrt(ahead) - jnp.sqrt(behind))
        coef = -(1.0 + climbing) * along + (1.0 - climbing) * spring
        scale = coef * norm
        part = ff + 2.0 * coef * along + scale * scale * spread_sq
        force_sq = force_sq + jnp.sum(part, axis=0, keepdims=True)
        here = group == me
        mine.append(
            (
                jnp.sum(jnp.where(here, scale, 0.0), axis=0, keepdims=True),
                jnp.sum(jnp.where(here, energy, 0.0), axis=0, keepdims=True),
            )
        )
    gain = 0.1 * jnp.sqrt(vel_sq / (force_sq + 1e-06))
    for i in range(count):
        scale, energy = mine[i]
        neb = force_ref[i] + scale * (nxt[i] - prev[i])
        neb_ref[i] = neb
        vnext = 0.9 * vel_ref[i] + gain * neb + 0.1 * neb
        vnext_ref[i] = vnext
        pnext_ref[i] = pos_ref[i] + 0.1 * vnext
        en_ref[i] = jnp.broadcast_to(energy * (1.0 / (atoms * slabs)), (8, 128))


def per_image(shape):
    rank = len(shape)
    return pl.BlockSpec((1,) + shape, lambda i: (i,) + (0,) * rank)


def whole(shape):
    rank = len(shape)
    return pl.BlockSpec(shape, lambda i: (0,) * rank)


def out(*shape):
    return jax.ShapeDtypeStruct(shape, f32)


VMEM = pl.BlockSpec(memory_space=pltpu.VMEM)
SMEM = pl.BlockSpec(memory_space=pltpu.SMEM)


def neighbours_of(cells, axis):
    count = lax.axis_size(axis)
    up = [(i, (i + 1) % count) for i in range(count)]
    down = [((i + 1) % count, i) for i in range(count)]
    to_below, to_above = cells
    return lax.ppermute(to_above, axis, up), lax.ppermute(to_below, axis, down)


def local(
    positions,
    velocity,
    start_state,
    end_state,
    neighbours,
    counts,
    climb_index,
    radial_a1,
    radial_b1,
    mix_first,
    read_first,
    radial_a2,
    radial_b2,
    mix_second,
    read_second,
):
    images, _, atoms = positions.shape
    slots = neighbours.shape[1]
    ghost = atoms // 2
    nb, rh = radial_a1.shape
    ch = radial_b1.shape[1]
    extent = atoms + 2 * ghost
    space = lax.axis_size("space")
    chain = lax.axis_size("image")
    params = pltpu.CompilerParams(dimension_semantics=("arbitrary",))

    plo, pup = neighbours_of((positions[:, :, :ghost], positions[:, :, ghost:]), "space")
    before = lax.ppermute(positions[images - 1], "image", [(i, i + 1) for i in range(chain - 1)])
    after = lax.ppermute(positions[0], "image", [(i + 1, i) for i in range(chain - 1)])
    counts3 = counts.reshape(images, 1, atoms)
    read1 = read_first.reshape(ch, 1)
    read2 = read_second.reshape(ch, 1)
    geo_n = NL + 4

    head, tail, geo, hid, ds, mom, dpre, en1 = pl.pallas_call(
        first_kernel,
        grid=(images,),
        in_specs=[
            per_image((3, atoms)),
            per_image((3, ghost)),
            per_image((3, ghost)),
            per_image((slots, atoms)),
            per_image((1, atoms)),
            whole((nb, rh)),
            whole((rh, ch)),
            whole((3 * ch, ch)),
            whole((ch, 1)),
        ],
        out_specs=[
            per_image((ch, ghost)),
            per_image((ch, ghost)),
            per_image((geo_n, slots, atoms)),
            per_image((slots, rh, atoms)),
            per_image((slots, rh, atoms)),
            per_image((NL, ch, atoms)),
            per_image((ch, atoms)),
            per_image((8, 128)),
        ],
        out_shape=[
            out(images, ch, ghost),
            out(images, ch, ghost),
            out(images, geo_n, slots, atoms),
            out(images, slots, rh, atoms),
            out(images, slots, rh, atoms),
            out(images, NL, ch, atoms),
            out(images, ch, atoms),
            out(images, 8, 128),
        ],
        scratch_shapes=[
            pltpu.VMEM((slots, NL, 8, atoms), f32),
            pltpu.VMEM((NL, rh, atoms), f32),
            pltpu.VMEM((3, slots, atoms), f32),
        ],
        compiler_params=params,
        name="first",
    )(positions, plo, pup, neighbours, counts3, radial_a1, radial_b1, mix_first, read1)

    hlo, hup = neighbours_of((head, tail), "space")

    dfh, dft, dlo, dup, dy2, dlen2, en2 = pl.pallas_call(
        second_kernel,
        grid=(images,),
        in_specs=[per_image((ch, ghost))] * 4
        + [
            per_image((slots, atoms)),
            per_image((geo_n, slots, atoms)),
            whole((nb, rh)),
            whole((rh, ch)),
            whole((3 * ch, ch)),
            whole((ch, 1)),
        ],
        out_specs=[per_image((ch, ghost))] * 4
        + [
            per_image((NL, slots, atoms)),
            per_image((slots, atoms)),
            per_image((8, 128)),
        ],
        out_shape=[out(images, ch, ghost)] * 4
        + [
            out(images, NL, slots, atoms),
            out(images, slots, atoms),
            out(images, 8, 128),
        ],
        scratch_shapes=[
            pltpu.VMEM((slots, NL, 8, atoms), f32),
            pltpu.VMEM((2 * ch, extent), bf16),
            pltpu.VMEM((extent, slots * atoms), bf16),
            pltpu.VMEM((slots, ch, atoms), f32),
            pltpu.VMEM((slots, ch, atoms), f32),
            pltpu.VMEM((slots, rh, atoms), f32),
            pltpu.VMEM((NL, ch, atoms), f32),
            pltpu.VMEM((2 * ch, slots * atoms), bf16),
            pltpu.VMEM((3 * ch, atoms), bf16),
        ],
        compiler_params=params,
        name="second",
    )(head, tail, hlo, hup, neighbours, geo, radial_a2, radial_b2, mix_second, read2)

    rlo, rup = neighbours_of((dlo, dup), "space")

    own, flo, fup = pl.pallas_call(
        third_kernel,
        grid=(images,),
        in_specs=[per_image((ch, ghost))] * 4
        + [
            per_image((slots, atoms)),
            per_image((geo_n, slots, atoms)),
            per_image((slots, rh, atoms)),
            per_image((slots, rh, atoms)),
            per_image((NL, ch, atoms)),
            per_image((ch, atoms)),
            per_image((NL, slots, atoms)),
            per_image((slots, atoms)),
            whole((nb, rh)),
            whole((rh, ch)),
            whole((3 * ch, ch)),
            whole((ch, 1)),
        ],
        out_specs=[per_image((3, atoms)), per_image((3, ghost)), per_image((3, ghost))],
        out_shape=[out(images, 3, atoms), out(images, 3, ghost), out(images, 3, ghost)],
        scratch_shapes=[
            pltpu.VMEM((slots, NL, 8, atoms), f32),
            pltpu.VMEM((NL, ch, atoms), f32),
            pltpu.VMEM((NL, rh, atoms), f32),
            pltpu.VMEM((1, NL, slots, atoms), f32),
            pltpu.VMEM((3 * rh, atoms), bf16),
            pltpu.VMEM((slots, atoms), f32),
            pltpu.VMEM((3, slots, atoms), f32),
        ],
        compiler_params=params,
        name="third",
    )(
        dfh, dft, rlo, rup, neighbours, geo, hid, ds, mom, dpre, dy2, dlen2,
        radial_a1, radial_b1, mix_first, read1,
    )

    glo, gup = neighbours_of((flo, fup), "space")

    me = lax.axis_index("image")
    edge = jnp.stack([(me == 0).astype(jnp.int32), (me == chain - 1).astype(jnp.int32), me])
    rank = chain * space
    force, send = pl.pallas_call(
        partial_kernel,
        in_specs=[SMEM] + [VMEM] * 11,
        out_specs=[VMEM] * 2,
        out_shape=[out(images, 3, atoms), out(rank, 128)],
        name="partial",
    )(edge, own, glo, gup, positions, before, after, start_state, end_state, velocity, en1, en2)
    got = lax.all_to_all(
        send.reshape(rank, 1, 128), ("image", "space"), split_axis=0, concat_axis=0
    ).reshape(rank, 128)
    neb, vnext, pnext, energy = pl.pallas_call(
        functools.partial(final_kernel, images=chain, slabs=space),
        in_specs=[SMEM, VMEM, SMEM] + [VMEM] * 7,
        out_specs=[VMEM] * 4,
        out_shape=[out(images, 3, atoms)] * 3 + [out(images, 8, 128)],
        name="final",
    )(edge, got, climb_index, force, positions, before, after, start_state, end_state, velocity)
    return (neb, vnext, pnext, energy[:, 0, 0])


def solution(mesh):
    in_specs = (
        P("image", None, "space"),
        P("image", None, "space"),
        P(None, "space"),
        P(None, "space"),
        P("image", None, "space"),
        P("image", "space"),
        P(),
        P(),
        P(),
        P(),
        P(),
        P(),
        P(),
        P(),
        P(),
    )
    out_specs = (
        P("image", None, "space"),
        P("image", None, "space"),
        P("image", None, "space"),
        P("image"),
    )
    return jax.shard_map(local, mesh=mesh, in_specs=in_specs, out_specs=out_specs, check_vma=False)
```

time: 571 us -> 120 us (0.21)
  other arithmetic: 158 us -> 0.58 us
  blocking collectives: 150 us -> 0 us
  matrix products: 118 us -> 0 us
  local copies, waits for them, and re-layouts: 81.4 us -> 15 us
  Pallas kernels: 0 us -> 52 us
  waiting for transfers between devices: 31.9 us -> 10.1 us
  starting transfers between devices: 18.9 us -> 39.9 us
  loops' own time: 6.27 us -> 0 us
    psum x3 -> x0, blocking collectives: 150 us -> none  [the longest x1 86.4 us: local(): lax.psum((jnp.sum(velocity * velocity), jnp.sum(neb_force * neb_force)),...]
    scatter-add x6 -> x0, other arithmetic: 136 us -> none  [the longest x2 45.6 us: first_layer(): ext_pos[:, nb_idx]]
    dot_general x36 -> x0, matrix products: 118 us -> none  [the longest x12 60.4 us: layer_out(): jnp.einsum('cka,lka->cla', radial, angular, precision=highest)]
    gather x6 -> x0, local copies, waits for them, and re-layouts: 53.6 us -> none  [the longest x2 30.9 us: second_energy(): ext_feat[:, nb_idx]]
    pallas_call x0 -> x5, Pallas kernels: none -> 52 us  [the longest x1 30.3 us: local(): pl.pallas_call(second_kernel, grid=(images,), in_specs=[per_image((ch, gh...]
    ppermute x18 -> x10, waiting for transfers between devices: 31.9 us -> 1.2 us  [the longest x4 1.19 us: neighbours_of(): lax.ppermute(to_above, axis, up)]
    ppermute x18 -> x10, starting transfers between devices: 18.9 us -> 29.5 us  [the longest x4 19 us: neighbours_of(): lax.ppermute(to_below, axis, down)]
    all_to_all x0 -> x1, starting transfers between devices: none -> 10.4 us  [local(): lax.all_to_all(send.reshape(rank, 1, 128), ('image', 'space'), split_axis...]
  transfers between devices with their start and end apart: 18 -> 11, of which waited for: 14 -> 2; matrix products, arithmetic and copies ran while one was open for 1% -> 5% of each run, Pallas kernels for 0% -> 9%
where the time goes in v1:
time: 120 us; the launch traced here: 119 us
  Pallas kernels  52 us (43%)
  starting transfers between devices  39.9 us (33%)
  local copies, waits for them, and re-layouts  15 us (12%)
  waiting for transfers between devices  10.1 us (8%)
  between operations  1.46 us (1%)
    pallas_call x1, Pallas kernels, local(): pl.pallas_call(second_kernel, grid=(images,), in_specs=[per_image((ch, gh...  30.3 us
    ppermute x4, starting transfers between devices, neighbours_of(): lax.ppermute(to_below, axis, down)  19 us
    all_to_all x1, starting transfers between devices, local(): lax.all_to_all(send.reshape(rank, 1, 128), ('image', 'space'), split_axis...  10.4 us
    pallas_call x1, Pallas kernels, local(): pl.pallas_call(third_kernel, grid=(images,), in_specs=[per_image((ch, gho...  10.3 us
    unnamed x31, local copies, waits for them, and re-layouts  8.98 us
    all_to_all x1, waiting for transfers between devices, local(): lax.all_to_all(send.reshape(rank, 1, 128), ('image', 'space'), split_axis...  8.94 us
    pallas_call x1, Pallas kernels, local(): pl.pallas_call(first_kernel, grid=(images,), in_specs=[per_image((3, atom...  7.88 us
    ppermute x1, starting transfers between devices, local(): lax.ppermute(positions[images - 1], 'image', [(i, i + 1) for i in range(c...  5.66 us
  transfers between devices with their start and end apart: 11, of which 2 were waited for; matrix products, arithmetic and copies ran while one was open for 5% of the time, Pallas kernels for 9%

profile of v1, /device:TPU:1, one launch (start us, length us, event | category | flops | bytes accessed | tf_op | source)
XLA Modules:
  0.0 119.1 jit_solution(49377816208231619)
XLA Ops:
  0.6 0.7 copy.51.pos_ref
  1.3 2.5 %collective-permute-start = (f32[2,3,128]{2,1,0:T(4,128)S(1)}, f32[2,3,128]{2,1,0:T(4,128)S(1)}, u32[]{:S(2)}, u32[]{:S(2)}) collective-permute-start(f32[2,3,128]{2,1,0:T(4,128)S(1)} %get-tuple-element.67), channel_id=1, source_target_pairs={{0,1},{1,2},{2,3},{3,4},{4,5},{5,6},{6,7},{7,8},{8,9},{9,10},{10,1... | collective-permute-start | bytes 9224 | tf_op jit(solution)/shard_map/ppermute | solution.py:449
  3.8 4.6 %collective-permute-start.1 = (f32[2,3,128]{2,1,0:T(4,128)S(1)}, f32[2,3,128]{2,1,0:T(4,128)S(1)}, u32[]{:S(2)}, u32[]{:S(2)}) collective-permute-start(f32[2,3,128]{2,1,0:T(4,128)S(1)} %get-tuple-element.66), channel_id=1, source_target_pairs={{1,0},{2,1},{3,2},{4,3},{5,4},{6,5},{7,6},{8,7},{9,8},{10,9},{11,1... | collective-permute-start | bytes 9224 | tf_op jit(solution)/shard_map/ppermute | solution.py:449
  8.4 1.4 %copy.52.read_ref = f32[128,1]{1,0:T(8,128)} copy(f32[128,1]{0,1:T(1,128)} %bitcast.15) | data formatting | bytes 1024 | tf_op jit(solution)/shard_map/reshape | solution.py:483
  9.8 1.3 %reshape.23.cnt_ref = s32[2,1,256]{2,1,0:T(1,128)} reshape(s32[2,256]{1,0:T(2,128)} %param.20) | data formatting | bytes 4096 | tf_op jit(solution)/shard_map/reshape | solution.py:482
  11.1 0.0 collective-permute-done.plo_ref
  11.1 0.0 collective-permute-done.1.pup_ref
  11.1 0.6 copy-done.9
  11.7 0.6 copy-done.10
  12.3 7.9 %first.1 = (f32[2,128,128]{2,1,0:T(8,128)}, f32[2,128,128]{2,1,0:T(8,128)}, f32[2,13,16,256]{3,2,1,0:T(8,128)}, f32[2,16,64,256]{3,2,1,0:T(8,128)}, f32[2,16,64,...) custom-call(f32[2,3,256]{2,1,0:T(4,128)} %copy-done, ...), custom_call_target="tpu_custom_call" | custom-call | tf_op jit(solution)/shard_map/first/pallas_call | solution.py:487
  20.1 0.1 collective-permute-start.2
  20.2 4.8 %collective-permute-start.3 = (f32[2,128,128]{2,1,0:T(8,128)}, f32[2,128,128]{2,1,0:T(8,128)S(1)}, u32[]{:S(2)}, u32[]{:S(2)}) collective-permute-start(f32[2,128,128]{2,1,0:T(8,128)} %get-tuple-element.28.head_ref), channel_id=1, source_target_pairs={{1,0},{2,1},{3,2},{4,3},{5,4},{6,5},{7,6},{8,7},{9,8},{10,9},{11,1... | collective-permute-start | bytes 393224 | tf_op jit(solution)/shard_map/ppermute | solution.py:449
  25.0 1.4 %copy.53.read_ref = f32[128,1]{1,0:T(8,128)} copy(f32[128,1]{0,1:T(1,128)} %bitcast.16) | data formatting | bytes 1024 | tf_op jit(solution)/shard_map/reshape | solution.py:484
  26.4 1.2 collective-permute-done.2.hlo_ref
  27.6 0.6 copy-done.2
  28.2 0.1 copy-done.3
  28.3 30.3 %second.1 = (f32[2,128,128]{2,1,0:T(8,128)}, f32[2,128,128]{2,1,0:T(8,128)}, f32[2,128,128]{2,1,0:T(8,128)}, f32[2,128,128]{2,1,0:T(8,128)}, f32[2,9,16,256]{3,2...) custom-call(f32[2,128,128]{2,1,0:T(8,128)} %get-tuple-element.28.head_ref, ...), custom_call_target="tpu_custom_call" | custom-call | tf_op jit(solution)/shard_map/second/pallas_call | solution.py:532
  58.5 0.1 collective-permute-start.4
  58.6 4.8 %collective-permute-start.5 = (f32[2,128,128]{2,1,0:T(8,128)}, f32[2,128,128]{2,1,0:T(8,128)S(1)}, u32[]{:S(2)}, u32[]{:S(2)}) collective-permute-start(f32[2,128,128]{2,1,0:T(8,128)} %get-tuple-element.34), channel_id=1, source_target_pairs={{1,0},{2,1},{3,2},{4,3},{5,4},{6,5},{7,6},{8,7},{9,8},{10,9},{11,1... | collective-permute-start | bytes 393224 | tf_op jit(solution)/shard_map/ppermute | solution.py:449
  63.4 0.7 slice_bitcast_fusion
  64.1 5.7 %collective-permute-start.8 = (f32[3,256]{1,0:T(4,128)S(1)}, f32[3,256]{1,0:T(4,128)S(1)}, u32[]{:S(2)}, u32[]{:S(2)}) collective-permute-start(f32[3,256]{1,0:T(4,128)S(1)} %get-tuple-element.65), channel_id=1, source_target_pairs={{0,16},{16,32},{32,48},{48,64},{64,80},{80,96},{96,112},{1,17},{17... | collective-permute-start | bytes 9224 | tf_op jit(solution)/shard_map/ppermute | solution.py:480
  69.8 2.1 %collective-permute-start.9 = (f32[3,256]{1,0:T(4,128)S(1)}, f32[3,256]{1,0:T(4,128)S(1)}, u32[]{:S(2)}, u32[]{:S(2)}) collective-permute-start(f32[3,256]{1,0:T(4,128)S(1)} %get-tuple-element.64), channel_id=1, source_target_pairs={{16,0},{32,16},{48,32},{64,48},{80,64},{96,80},{112,96},{17,1},{33... | collective-permute-start | bytes 9224 | tf_op jit(solution)/shard_map/ppermute | solution.py:481
  71.9 0.0 collective-permute-done.4.rlo_ref
  71.9 0.0 collective-permute-done.5.rup_ref
  72.0 0.6 copy-done.4
  72.6 0.1 copy-done.5
  72.7 10.3 %third.1 = (f32[2,3,256]{2,1,0:T(4,128)}, f32[2,3,128]{2,1,0:T(4,128)}, f32[2,3,128]{2,1,0:T(4,128)}) custom-call(f32[2,128,128]{2,1,0:T(8,128)} %get-tuple-element.31.dfh_ref, f32[2,128,128]{2,1,0:T(8,128)} %get-tuple-element.32.dft_ref, f32[2,128,128]{2,1,0:T(8,128)} %copy-done.4, f32[2,128,128]{2,1,0:T(8,128)} %copy-done.5, s32[2,16,256]{2,1,0:T(8,128)} %idx_ref.5, ...), custom_call_target="tpu_custom_call" | custom-call | tf_op jit(solution)/shard_map/third/pallas_call | solution.py:573
  83.0 0.1 collective-permute-start.6
  83.1 4.8 %collective-permute-start.7 = (f32[2,3,128]{2,1,0:T(4,128)}, f32[2,3,128]{2,1,0:T(4,128)S(1)}, u32[]{:S(2)}, u32[]{:S(2)}) collective-permute-start(f32[2,3,128]{2,1,0:T(4,128)} %get-tuple-element.43), channel_id=1, source_target_pairs={{1,0},{2,1},{3,2},{4,3},{5,4},{6,5},{7,6},{8,7},{9,8},{10,9},{11,1... | collective-permute-start | bytes 9224 | tf_op jit(solution)/shard_map/ppermute | solution.py:449
  87.9 0.6 pad_add_fusion.edge_ref
  88.5 0.6 copy.58.vel_ref
  89.1 0.0 collective-permute-done.8.before_ref
  89.1 0.0 collective-permute-done.9.after_ref
  89.1 0.0 copy-start.11
  89.1 0.0 copy-start.12
  89.1 0.5 copy-done.6
  89.7 0.0 copy-done.7
  89.7 0.0 copy-done.11
  89.7 0.0 copy-done.12
  89.7 1.6 %partial.1 = (f32[2,3,256]{2,1,0:T(4,128)}, f32[128,128]{1,0:T(8,128)}) custom-call(s32[3]{0:T(128)} %pad_add_fusion.edge_ref, f32[2,3,256]{2,1,0:T(4,128)} %get-tuple-element.41.own_ref, f32[2,3,128]{2,1,0:T(4,128)} %copy-done.11, f32[2,3,128]{2,1,0:T(4,128)} %copy-done.12, f32[2,3,256]{2,1,0:T(4,128)} %copy-done, f32[3,256]{1,0:T(4,128)} %copy-done.6, ...), custom_call_target="tpu_custom_call" | custom-call | tf_op jit(solution)/shard_map/partial/pallas_call | solution.py:614
  91.3 10.4 %all-to-all-start = ((f32[128,1,128]{2,1,0:T(1,128)}), f32[128,1,128]{2,1,0:T(1,128)S(1)}, u32[]{:S(2)}, u32[]{:S(2)}) async-start(f32[128,1,128]{2,1,0:T(1,128)} %bitcast.14), calls=%async_computation | async-start | bytes 131072 | tf_op jit(solution)/shard_map/all_to_all | solution.py:621
  102.3 8.9 %all-to-all-done = f32[128,1,128]{2,1,0:T(1,128)S(1)} async-done(((f32[128,1,128]{2,1,0:T(1,128)}), f32[128,1,128]{2,1,0:T(1,128)S(1)}, u32[]{:S(2)}, u32[]{:S(2)}) %all-to-all-start) | async-done | bytes 65568 | tf_op jit(solution)/shard_map/all_to_all | solution.py:621
  111.3 0.6 copy-done.1
  111.9 2.0 %final.1 = (f32[2,3,256]{2,1,0:T(4,128)}, f32[2,3,256]{2,1,0:T(4,128)}, f32[2,3,256]{2,1,0:T(4,128)}, f32[2,8,128]{2,1,0:T(8,128)}) custom-call(s32[3]{0:T(128)} %pad_add_fusion.edge_ref, f32[128,128]{1,0:T(8,128)} %bitcast.13, s32[1]{0:T(128)S(6)} %copy.65.climb_ref, f32[2,3,256]{2,1,0:T(4,128)} %get-tuple-element.47.force_ref, f32[2,3,256]{2,1,0:T(4,128)} %copy-done, ...), custom_call_target="tpu_custom_call" | custom-call | tf_op jit(solution)/shard_map/final/pallas_call | solution.py:624
  113.9 1.3 %copy.62 = f32[2,3,256]{2,0,1:T(2,128)} copy(f32[2,3,256]{2,1,0:T(4,128)} %get-tuple-element.60) | data formatting | bytes 12288
  115.2 1.3 %copy.63 = f32[2,3,256]{2,0,1:T(2,128)} copy(f32[2,3,256]{2,1,0:T(4,128)} %get-tuple-element.61) | data formatting | bytes 12288
  116.5 1.3 %copy.64 = f32[2,3,256]{2,0,1:T(2,128)} copy(f32[2,3,256]{2,1,0:T(4,128)} %get-tuple-element.62) | data formatting | bytes 12288
  117.8 1.3 %slice_reduce_fusion = f32[2]{0:T(128)} fusion(f32[2,8,128]{2,1,0:T(8,128)} %get-tuple-element.51), kind=kLoop, calls=%fused_computation.2 | loop fusion | bytes 16 | tf_op jit(solution)/shard_map/slice | solution.py:631
  (17 shorter events, 0.0 us)
Async XLA Ops:
  1.3 9.8 %copy-start = (f32[2,3,256]{2,1,0:T(4,128)}, f32[2,3,256]{2,1,0:T(4,128)S(1)}, u32[]{:S(2)}) copy-start(f32[2,3,256]{2,1,0:T(4,128)S(1)} %copy.51.pos_ref) | copy-start | bytes 18436
  1.3 9.7 %collective-permute-start = (f32[2,3,128]{2,1,0:T(4,128)S(1)}, f32[2,3,128]{2,1,0:T(4,128)S(1)}, u32[]{:S(2)}, u32[]{:S(2)}) collective-permute-start(f32[2,3,128]{2,1,0:T(4,128)S(1)} %get-tuple-element.67), channel_id=1, source_target_pairs={{0,1},{1,2},{2,3},{3,4},{4,5},{5,6},{6,7},{7,8},{8,9},{9,10},{10,1... | collective-permute-start | bytes 9224 | tf_op jit(solution)/shard_map/ppermute | solution.py:449
  3.8 7.3 %collective-permute-start.1 = (f32[2,3,128]{2,1,0:T(4,128)S(1)}, f32[2,3,128]{2,1,0:T(4,128)S(1)}, u32[]{:S(2)}, u32[]{:S(2)}) collective-permute-start(f32[2,3,128]{2,1,0:T(4,128)S(1)} %get-tuple-element.66), channel_id=1, source_target_pairs={{1,0},{2,1},{3,2},{4,3},{5,4},{6,5},{7,6},{8,7},{9,8},{10,9},{11,1... | collective-permute-start | bytes 9224 | tf_op jit(solution)/shard_map/ppermute | solution.py:449
  11.1 0.6 copy-start.9
  11.7 0.6 copy-start.10
  20.1 7.4 %collective-permute-start.2 = (f32[2,128,128]{2,1,0:T(8,128)}, f32[2,128,128]{2,1,0:T(8,128)S(1)}, u32[]{:S(2)}, u32[]{:S(2)}) collective-permute-start(f32[2,128,128]{2,1,0:T(8,128)} %get-tuple-element.29.tail_ref), channel_id=1, source_target_pairs={{0,1},{1,2},{2,3},{3,4},{4,5},{5,6},{6,7},{7,8},{8,9},{9,10},{10,1... | collective-permute-start | bytes 393224 | tf_op jit(solution)/shard_map/ppermute | solution.py:449
  20.2 7.3 %collective-permute-start.3 = (f32[2,128,128]{2,1,0:T(8,128)}, f32[2,128,128]{2,1,0:T(8,128)S(1)}, u32[]{:S(2)}, u32[]{:S(2)}) collective-permute-start(f32[2,128,128]{2,1,0:T(8,128)} %get-tuple-element.28.head_ref), channel_id=1, source_target_pairs={{1,0},{2,1},{3,2},{4,3},{5,4},{6,5},{7,6},{8,7},{9,8},{10,9},{11,1... | collective-permute-start | bytes 393224 | tf_op jit(solution)/shard_map/ppermute | solution.py:449
  27.6 0.6 copy-start.2
  27.6 0.7 copy-start.3
  58.5 13.4 %collective-permute-start.4 = (f32[2,128,128]{2,1,0:T(8,128)}, f32[2,128,128]{2,1,0:T(8,128)S(1)}, u32[]{:S(2)}, u32[]{:S(2)}) collective-permute-start(f32[2,128,128]{2,1,0:T(8,128)} %get-tuple-element.33), channel_id=1, source_target_pairs={{0,1},{1,2},{2,3},{3,4},{4,5},{5,6},{6,7},{7,8},{8,9},{9,10},{10,1... | collective-permute-start | bytes 393224 | tf_op jit(solution)/shard_map/ppermute | solution.py:449
  58.6 13.3 %collective-permute-start.5 = (f32[2,128,128]{2,1,0:T(8,128)}, f32[2,128,128]{2,1,0:T(8,128)S(1)}, u32[]{:S(2)}, u32[]{:S(2)}) collective-permute-start(f32[2,128,128]{2,1,0:T(8,128)} %get-tuple-element.34), channel_id=1, source_target_pairs={{1,0},{2,1},{3,2},{4,3},{5,4},{6,5},{7,6},{8,7},{9,8},{10,9},{11,1... | collective-permute-start | bytes 393224 | tf_op jit(solution)/shard_map/ppermute | solution.py:449
  64.1 25.0 %collective-permute-start.8 = (f32[3,256]{1,0:T(4,128)S(1)}, f32[3,256]{1,0:T(4,128)S(1)}, u32[]{:S(2)}, u32[]{:S(2)}) collective-permute-start(f32[3,256]{1,0:T(4,128)S(1)} %get-tuple-element.65), channel_id=1, source_target_pairs={{0,16},{16,32},{32,48},{48,64},{64,80},{80,96},{96,112},{1,17},{17... | collective-permute-start | bytes 9224 | tf_op jit(solution)/shard_map/ppermute | solution.py:480
  69.8 19.3 %collective-permute-start.9 = (f32[3,256]{1,0:T(4,128)S(1)}, f32[3,256]{1,0:T(4,128)S(1)}, u32[]{:S(2)}, u32[]{:S(2)}) collective-permute-start(f32[3,256]{1,0:T(4,128)S(1)} %get-tuple-element.64), channel_id=1, source_target_pairs={{16,0},{32,16},{48,32},{64,48},{80,64},{96,80},{112,96},{17,1},{33... | collective-permute-start | bytes 9224 | tf_op jit(solution)/shard_map/ppermute | solution.py:481
  71.9 0.7 copy-start.4
  72.0 0.7 copy-start.5
  72.7 15.8 %copy-start.8 = (f32[2,3,256]{2,0,1:T(2,128)S(1)}, f32[2,3,256]{2,0,1:T(2,128)}, u32[]{:S(2)}) copy-start(f32[2,3,256]{2,0,1:T(2,128)} %param.16) | copy-start | bytes 18436
  83.0 6.1 %collective-permute-start.6 = (f32[2,3,128]{2,1,0:T(4,128)}, f32[2,3,128]{2,1,0:T(4,128)S(1)}, u32[]{:S(2)}, u32[]{:S(2)}) collective-permute-start(f32[2,3,128]{2,1,0:T(4,128)} %get-tuple-element.42), channel_id=1, source_target_pairs={{0,1},{1,2},{2,3},{3,4},{4,5},{5,6},{6,7},{7,8},{8,9},{9,10},{10,1... | collective-permute-start | bytes 9224 | tf_op jit(solution)/shard_map/ppermute | solution.py:449
  83.1 6.0 %collective-permute-start.7 = (f32[2,3,128]{2,1,0:T(4,128)}, f32[2,3,128]{2,1,0:T(4,128)S(1)}, u32[]{:S(2)}, u32[]{:S(2)}) collective-permute-start(f32[2,3,128]{2,1,0:T(4,128)} %get-tuple-element.43), channel_id=1, source_target_pairs={{1,0},{2,1},{3,2},{4,3},{5,4},{6,5},{7,6},{8,7},{9,8},{10,9},{11,1... | collective-permute-start | bytes 9224 | tf_op jit(solution)/shard_map/ppermute | solution.py:449
  89.1 0.6 copy-start.6
  89.1 0.6 copy-start.7
  89.1 0.6 copy-start.11
  89.1 0.6 copy-start.12
  91.3 20.0 %all-to-all-start = ((f32[128,1,128]{2,1,0:T(1,128)}), f32[128,1,128]{2,1,0:T(1,128)S(1)}, u32[]{:S(2)}, u32[]{:S(2)}) async-start(f32[128,1,128]{2,1,0:T(1,128)} %bitcast.14), calls=%async_computation | async-start | bytes 131072 | tf_op jit(solution)/shard_map/all_to_all | solution.py:621
  111.3 0.6 copy-start.1

commit v2 on v1

v2 whole, which is shorter than its diff:
```python
import functools
import math

import jax
import jax.numpy as jnp
from jax import lax
from jax.experimental import pallas as pl
from jax.experimental.pallas import tpu as pltpu
from jax.sharding import PartitionSpec as P

f32 = jnp.float32
bf16 = jnp.bfloat16
RT3 = math.sqrt(3.0)
NL = 9
BIG_VMEM = 36 << 20
SMALL_VMEM = 4 << 20


def split(x):
    hi = x.astype(bf16)
    lo = (x - hi.astype(f32)).astype(bf16)
    return hi, lo


def dot(a, b):
    return lax.dot_general(a, b, (((1,), (0,)), ((), ())), preferred_element_type=f32)


def dot_nt(a, b):
    return lax.dot_general(a, b, (((1,), (1,)), ((), ())), preferred_element_type=f32)


def pack_left(w):
    hi, lo = split(w)
    return jnp.concatenate([hi, hi, lo], axis=1)


def pack_right(x):
    hi, lo = split(x)
    return jnp.concatenate([hi, lo, hi], axis=0)


def one_hot(row, extent):
    step = 256
    wide = (step, row.shape[1])
    ids = lax.broadcasted_iota(jnp.int32, wide, 0).astype(f32).astype(bf16)
    zero, one = jnp.zeros(wide, bf16), jnp.ones(wide, bf16)
    parts = []
    for first in range(0, extent, step):
        here = jnp.broadcast_to((row - first).astype(f32), wide).astype(bf16)
        parts.append(jnp.where(ids == here, one, zero))
    return jnp.concatenate(parts, axis=0)


def lane_gather(row, idx):
    slots, atoms = idx.shape
    extent = row.shape[1]
    lane = idx & 127
    tile = idx >> 7
    blocks = [jnp.broadcast_to(row[:, t : t + 128], (8, 128)) for t in range(0, extent, 128)]
    out_rows = []
    for s0 in range(0, slots, 8):
        cells = []
        for a0 in range(0, atoms, 128):
            at = lane[s0 : s0 + 8, a0 : a0 + 128]
            which = tile[s0 : s0 + 8, a0 : a0 + 128]
            got = None
            for t, block in enumerate(blocks):
                v = jnp.take_along_axis(block, at, axis=1, mode="promise_in_bounds")
                got = v if got is None else jnp.where(which == t, v, got)
            cells.append(got)
        out_rows.append(jnp.concatenate(cells, axis=1))
    return jnp.concatenate(out_rows, axis=0)


def pick(block, i, axis):
    n = block.shape[axis]
    got = lax.index_in_dim(block, 0, axis, keepdims=False)
    for m in range(1, n):
        got = jnp.where(i == m, lax.index_in_dim(block, m, axis, keepdims=False), got)
    return got


def column(row_ref):
    n = row_ref.shape[1]
    return jnp.broadcast_to(row_ref[...], (8, n)).T[:, :1]


def silu_parts(z):
    s = 0.5 + 0.5 * jnp.tanh(0.5 * z)
    h = z * s
    return h, s + h * (1.0 - s)


def basis_of(row, nb):
    centres = 0.5 * lax.broadcasted_iota(jnp.int32, (nb, row.shape[1]), 0).astype(f32)
    spread = row - centres
    basis = jnp.exp(-2.0 * spread * spread)
    return basis, -4.0 * spread * basis


def moments_into(edge_tile, yb_ref, m_ref, chans, slots, atoms):
    def tile(t, carry):
        c0 = pl.multiple_of(t * 16, 16)
        for a0 in range(0, atoms, 128):
            acc = [jnp.zeros((16, 128), f32) for _ in range(NL)]
            for k in range(slots):
                e = edge_tile(k, c0, a0)
                for l in range(NL):
                    y = yb_ref[k, l, :, a0 : a0 + 128]
                    acc[l] = acc[l] + e * jnp.concatenate([y, y], axis=0)
            for l in range(NL):
                m_ref[l, pl.ds(c0, 16), a0 : a0 + 128] = acc[l]
        return carry

    lax.fori_loop(0, chans // 16, tile, 0)


def store_yb(yb_ref, ylive, slots, atoms):
    for k in range(slots):
        for l in range(NL):
            yb_ref[k, l] = jnp.broadcast_to(ylive[l][k : k + 1], (8, atoms))


def invariants_of(m_ref):
    m = [m_ref[l] for l in range(NL)]
    one = m[1] * m[1] + m[2] * m[2] + m[3] * m[3]
    two = m[4] * m[4] + m[5] * m[5] + m[6] * m[6] + m[7] * m[7] + m[8] * m[8]
    return jnp.concatenate([m[0], one, two], axis=0)


def moment_grads_into(m_ref, dinv, chans):
    m_ref[0] = dinv[:chans]
    d1 = 2.0 * dinv[chans : 2 * chans]
    d2 = 2.0 * dinv[2 * chans :]
    for l in range(1, NL):
        m_ref[l] = m_ref[l] * (d1 if l < 4 else d2)


def first_kernel(
    pos_ref, plo_ref, pup_ref, idx_ref, cnt_ref, a_ref, b_ref, mix_ref, read_ref,
    head_ref, tail_ref, geo_ref, hid_ref, dsl_ref, mom_ref, dpre_ref, en_ref,
    yb_ref, g_ref,
):
    slots, atoms = idx_ref.shape[1:]
    ghost = plo_ref.shape[2]
    nb, rh = a_ref.shape
    ch = b_ref.shape[1]
    image = pl.program_id(0)
    idx = idx_ref[0]
    pos = pick(pos_ref[...], image, 1)
    plo = pick(plo_ref[...], image, 1)
    pup = pick(pup_ref[...], image, 1)
    ext = jnp.concatenate([plo, pos, pup], axis=1)
    off = [lane_gather(ext[x : x + 1], idx) - pos[x : x + 1] for x in range(3)]
    length = jnp.sqrt(off[0] * off[0] + off[1] * off[1] + off[2] * off[2] + 1.0)
    ux, uy, uz = [o / length for o in off]
    ids = lax.broadcasted_iota(jnp.int32, (slots, atoms), 0)
    cnt = pick(cnt_ref[...][None], image, 1)
    live = jnp.where(ids < cnt, 1.0 / slots, 0.0).astype(f32)
    ylive = [
        live,
        live * ux,
        live * uy,
        live * uz,
        live * (ux * uy),
        live * (uy * uz),
        live * (ux * uz),
        live * (0.5 * (ux * ux - uy * uy)),
        live * ((3.0 * uz * uz - 1.0) / (2.0 * RT3)),
    ]
    for l in range(NL):
        geo_ref[0, l] = ylive[l]
    geo_ref[0, NL] = ux
    geo_ref[0, NL + 1] = uy
    geo_ref[0, NL + 2] = uz
    geo_ref[0, NL + 3] = length
    store_yb(yb_ref, ylive, slots, atoms)
    a_pack = pack_left(a_ref[...].T)
    for k in range(slots):
        basis, slope = basis_of(length[k : k + 1], nb)
        hid, ds = silu_parts(dot(a_pack, pack_right(basis)))
        hid_ref[0, k] = hid
        dsl_ref[0, k] = ds * dot(a_pack, pack_right(slope))

    def hid_tile(k, c0, a0):
        return hid_ref[0, k, pl.ds(c0, 16), a0 : a0 + 128]

    moments_into(hid_tile, yb_ref, g_ref, rh, slots, atoms)
    b_pack = pack_left(b_ref[...].T)
    for l in range(NL):
        mom_ref[0, l] = dot(b_pack, pack_right(g_ref[l]))
    inv = invariants_of(mom_ref.at[0])
    feat, dpre = silu_parts(dot(pack_left(mix_ref[...].T), pack_right(inv)))
    dpre_ref[0] = dpre
    head_ref[0] = feat[:, :ghost]
    tail_ref[0] = feat[:, atoms - ghost :]
    en = column(read_ref) * feat
    total = jnp.sum(en.reshape(ch // 8, 8, atoms), axis=0)
    en_ref[0] = total[:, :128] + total[:, 128:]


def edge_back(k, edge_tile, sink, yb_ref, m_ref, dy_ref, dlen_ref, chans, atoms):
    for a0 in range(0, atoms, 128):
        y = [yb_ref[k, l, :, a0 : a0 + 128] for l in range(NL)]
        y = [jnp.concatenate([v, v], axis=0) for v in y]
        acc = [jnp.zeros((8, 128), f32) for _ in range(NL + 1)]
        for c0 in range(0, chans, 16):
            e = edge_tile(k, c0, a0)
            de = None
            for l in range(NL):
                dm = m_ref[l, c0 : c0 + 16, a0 : a0 + 128]
                term = dm * y[l]
                de = term if de is None else de + term
                p = e * dm
                acc[l] = acc[l] + (p[:8] + p[8:])
            p = sink(k, c0, a0, de)
            acc[NL] = acc[NL] + (p[:8] + p[8:])
        for l in range(NL):
            dy_ref[0, l, k : k + 1, a0 : a0 + 128] = jnp.sum(acc[l], axis=0, keepdims=True)
        dlen_ref[0, k : k + 1, a0 : a0 + 128] = jnp.sum(acc[NL], axis=0, keepdims=True)


def second_kernel(
    head_ref, tail_ref, hlo_ref, hup_ref, idx_ref, geo_ref, a_ref, b_ref, mix_ref, read_ref,
    dfh_ref, dft_ref, dlo_ref, dup_ref, dy_ref, dlen_ref, en_ref,
    yb_ref, hf_ref, oh_ref, q_ref, rad_ref, radl_ref, m_ref, dq_ref,
):
    slots, atoms = idx_ref.shape[1:]
    ghost = hlo_ref.shape[2]
    nb, rh = a_ref.shape
    ch = b_ref.shape[1]
    extent = atoms + 2 * ghost
    parts = (hlo_ref, head_ref, tail_ref, hup_ref)
    for n, ref in enumerate(parts):
        hi, lo = split(ref[0])
        hf_ref[:ch, n * ghost : (n + 1) * ghost] = hi
        hf_ref[ch:, n * ghost : (n + 1) * ghost] = lo
    store_yb(yb_ref, [geo_ref[0, l] for l in range(NL)], slots, atoms)
    a_pack = pack_left(a_ref[...].T)
    b_pack = pack_left(b_ref[...].T)
    for k in range(slots):
        oh = one_hot(idx_ref[0, k : k + 1, :], extent)
        oh_ref[:, k * atoms : (k + 1) * atoms] = oh
        got = dot(hf_ref[...], oh)
        q_ref[k] = got[:ch] + got[ch:]
        basis, slope = basis_of(geo_ref[0, NL + 3, k : k + 1, :], nb)
        hid, ds = silu_parts(dot(a_pack, pack_right(basis)))
        rad_ref[k] = dot(b_pack, pack_right(hid))
        radl_ref[k] = dot(b_pack, pack_right(ds * dot(a_pack, pack_right(slope))))

    def edge_tile(k, c0, a0):
        cs = pl.ds(c0, 16)
        return rad_ref[k, cs, a0 : a0 + 128] * q_ref[k, cs, a0 : a0 + 128]

    moments_into(edge_tile, yb_ref, m_ref, ch, slots, atoms)
    inv = invariants_of(m_ref)
    mix = mix_ref[...]
    feat, dpre = silu_parts(dot(pack_left(mix.T), pack_right(inv)))
    en = column(read_ref) * feat
    total = jnp.sum(en.reshape(ch // 8, 8, atoms), axis=0)
    en_ref[0] = total[:, :128] + total[:, 128:]
    dpre = column(read_ref) * dpre
    dinv = dot(pack_left(mix), pack_right(dpre))
    moment_grads_into(m_ref, dinv, ch)

    def sink(k, c0, a0, de):
        cs = slice(c0, c0 + 16)
        ls = slice(a0, a0 + 128)
        hi, lo = split(de * rad_ref[k, cs, ls])
        ks = slice(k * atoms + a0, k * atoms + a0 + 128)
        dq_ref[cs, ks] = hi
        dq_ref[ch + c0 : ch + c0 + 16, ks] = lo
        return de * q_ref[k, cs, ls] * radl_ref[k, cs, ls]

    for k in range(slots):
        edge_back(k, edge_tile, sink, yb_ref, m_ref, dy_ref, dlen_ref, ch, atoms)
    back = dot_nt(dq_ref[...], oh_ref[...])
    back = back[:ch] + back[ch:]
    dlo_ref[0] = back[:, :ghost]
    dfh_ref[0] = back[:, ghost : 2 * ghost]
    dft_ref[0] = back[:, 2 * ghost : 3 * ghost]
    dup_ref[0] = back[:, 3 * ghost :]


def third_kernel(
    dfh_ref, dft_ref, rlo_ref, rup_ref, idx_ref, geo_ref, hid_ref, dsl_ref, mom_ref, dpre_ref,
    dy2_ref, dlen2_ref, b_ref, mix_ref, read_ref,
    own_ref, flo_ref, fup_ref,
    yb_ref, m_ref, dg_ref, dy_ref, dlen_ref, doff_ref,
):
    slots, atoms = idx_ref.shape[1:]
    ghost = rlo_ref.shape[2]
    rh, ch = b_ref.shape
    extent = atoms + 2 * ghost
    store_yb(yb_ref, [geo_ref[0, l] for l in range(NL)], slots, atoms)
    cot = jnp.concatenate([dfh_ref[0] + rlo_ref[0], dft_ref[0] + rup_ref[0]], axis=1)
    dpre = (cot + column(read_ref)) * dpre_ref[0]
    dinv = dot(pack_left(mix_ref[...]), pack_right(dpre))
    for l in range(NL):
        m_ref[l] = mom_ref[0, l]
    moment_grads_into(m_ref, dinv, ch)
    bt_pack = pack_left(b_ref[...])
    for l in range(NL):
        dg_ref[l] = dot(bt_pack, pack_right(m_ref[l]))

    def edge_tile(k, c0, a0):
        return hid_ref[0, k, pl.ds(c0, 16), a0 : a0 + 128]

    def sink(k, c0, a0, de):
        return de * dsl_ref[0, k, c0 : c0 + 16, a0 : a0 + 128]

    for k in range(slots):
        edge_back(k, edge_tile, sink, yb_ref, dg_ref, dy_ref, dlen_ref, rh, atoms)
    live = geo_ref[0, 0]
    dy = [live * (dy_ref[0, l] + dy2_ref[0, l]) for l in range(NL)]
    ux, uy, uz, length = [geo_ref[0, NL + n] for n in range(4)]
    dux = dy[1] + uy * dy[4] + uz * dy[6] + ux * dy[7]
    duy = dy[2] + ux * dy[4] + uz * dy[5] - uy * dy[7]
    duz = dy[3] + uy * dy[5] + ux * dy[6] + RT3 * uz * dy[8]
    radial = dlen_ref[0] + dlen2_ref[0] - (dux * ux + duy * uy + duz * uz) / length
    doff = [du / length + radial * u for du, u in ((dux, ux), (duy, uy), (duz, uz))]
    centre = jnp.concatenate([jnp.sum(d, axis=0, keepdims=True) for d in doff], axis=0)
    for x in range(3):
        doff_ref[x] = doff[x]
    back = jnp.zeros((16, extent), f32)
    pad = jnp.zeros((5, atoms), f32)
    for k in range(slots):
        rows = jnp.concatenate([doff_ref[x, k : k + 1, :] for x in range(3)] + [pad], axis=0)
        hi = rows.astype(bf16).astype(f32)
        both = jnp.concatenate([hi, rows - hi], axis=0).astype(bf16)
        back = back + dot_nt(both, one_hot(idx_ref[0, k : k + 1, :], extent))
    force = back[8:11] + back[:3]
    for n in range(own_ref.shape[1]):

        @pl.when(pl.program_id(0) == n)
        def _():
            own_ref[:, n, :] = centre - force[:, ghost : ghost + atoms]
            flo_ref[:, n, :] = -force[:, :ghost]
            fup_ref[:, n, :] = -force[:, ghost + atoms :]


def lane_row(values):
    lane = lax.broadcasted_iota(jnp.int32, (1, 128), 1)
    row = jnp.zeros((1, 128), f32)
    for n, v in enumerate(values):
        row = jnp.where(lane == n, v, row)
    return row


def total_of(x):
    return jnp.sum(jnp.sum(x, axis=1, keepdims=True), axis=0, keepdims=True)


def chain_of(pos_ref, before_ref, after_ref, start_ref, end_ref, chain):
    count = pos_ref.shape[1]
    me = lax.axis_index("image")
    before = jnp.where(me == 0, start_ref[...], before_ref[...])
    after = jnp.where(me == chain - 1, end_ref[...], after_ref[...])
    prev = [before] + [pos_ref[:, i, :] for i in range(count - 1)]
    nxt = [pos_ref[:, i, :] for i in range(1, count)] + [after]
    return prev, nxt


def partial_kernel(
    own_ref, rlo_ref, rup_ref, pos_ref, before_ref, after_ref, start_ref, end_ref,
    vel_ref, en1_ref, en2_ref, force_ref, send_ref, *, chain,
):
    count = pos_ref.shape[1]
    prev, nxt = chain_of(pos_ref, before_ref, after_ref, start_ref, end_ref, chain)
    values = []
    vel = jnp.zeros((1, 1), f32)
    for i in range(count):
        pos = pos_ref[:, i, :]
        force = own_ref[:, i, :] + jnp.concatenate([rlo_ref[:, i, :], rup_ref[:, i, :]], axis=1)
        force_ref[:, i, :] = force
        spread = nxt[i] - prev[i]
        ahead = nxt[i] - pos
        behind = pos - prev[i]
        values += [
            total_of(ahead * ahead),
            total_of(behind * behind),
            total_of(spread * spread),
            total_of(force * force),
            total_of(force * spread),
            total_of(en1_ref[i]) + total_of(en2_ref[i]),
        ]
        v = vel_ref[:, i, :]
        vel = vel + total_of(v * v)
    send_ref[...] = jnp.broadcast_to(lane_row(values + [vel]), send_ref.shape)


def final_kernel(
    got_ref, climb_ref, force_ref, pos_ref, before_ref, after_ref, start_ref, end_ref,
    vel_ref, neb_ref, vnext_ref, pnext_ref, en_ref,
    *, chain, slabs,
):
    count = pos_ref.shape[1]
    atoms = pos_ref.shape[2]
    me = lax.axis_index("image")
    prev, nxt = chain_of(pos_ref, before_ref, after_ref, start_ref, end_ref, chain)
    rows = [
        jnp.sum(got_ref[g * slabs : (g + 1) * slabs, :], axis=0, keepdims=True)
        for g in range(chain)
    ]
    table = jnp.concatenate(rows, axis=0)
    vel_sq = jnp.sum(table[:, 6 * count : 6 * count + 1], axis=0, keepdims=True)
    group = lax.broadcasted_iota(jnp.int32, (chain, 1), 0)
    force_sq = jnp.zeros((1, 1), f32)
    mine = []
    for i in range(count):
        ahead, behind, spread_sq, ff, fd, energy = [
            table[:, 6 * i + n : 6 * i + n + 1] for n in range(6)
        ]
        norm = 1.0 / jnp.sqrt(spread_sq + 1e-06)
        along = fd * norm
        climbing = jnp.where(group * count + i == climb_ref[0], 1.0, 0.0).astype(f32)
        spring = 5.0 * (jnp.sqrt(ahead) - jnp.sqrt(behind))
        coef = -(1.0 + climbing) * along + (1.0 - climbing) * spring
        scale = coef * norm
        part = ff + 2.0 * coef * along + scale * scale * spread_sq
        force_sq = force_sq + jnp.sum(part, axis=0, keepdims=True)
        here = group == me
        mine.append(jnp.sum(jnp.where(here, scale, 0.0), axis=0, keepdims=True))
        en_ref[i] = jnp.sum(jnp.where(here, energy, 0.0)) * (1.0 / (atoms * slabs))
    gain = 0.1 * jnp.sqrt(vel_sq / (force_sq + 1e-06))
    for i in range(count):
        neb = force_ref[:, i, :] + mine[i] * (nxt[i] - prev[i])
        neb_ref[:, i, :] = neb
        vnext = 0.9 * vel_ref[:, i, :] + gain * neb + 0.1 * neb
        vnext_ref[:, i, :] = vnext
        pnext_ref[:, i, :] = pos_ref[:, i, :] + 0.1 * vnext


def per_image(shape):
    rank = len(shape)
    return pl.BlockSpec((1,) + shape, lambda i: (i,) + (0,) * rank)


def whole(shape):
    rank = len(shape)
    return pl.BlockSpec(shape, lambda i: (0,) * rank)


def out(*shape):
    return jax.ShapeDtypeStruct(shape, f32)


VMEM = pl.BlockSpec(memory_space=pltpu.VMEM)
SMEM = pl.BlockSpec(memory_space=pltpu.SMEM)


def neighbours_of(cells, axis):
    count = lax.axis_size(axis)
    up = [(i, (i + 1) % count) for i in range(count)]
    down = [((i + 1) % count, i) for i in range(count)]
    to_below, to_above = cells
    return lax.ppermute(to_above, axis, up), lax.ppermute(to_below, axis, down)


def local(
    positions,
    velocity,
    start_state,
    end_state,
    neighbours,
    counts,
    climb_index,
    radial_a1,
    radial_b1,
    mix_first,
    read_first,
    radial_a2,
    radial_b2,
    mix_second,
    read_second,
):
    images, _, atoms = positions.shape
    slots = neighbours.shape[1]
    ghost = atoms // 2
    nb, rh = radial_a1.shape
    ch = radial_b1.shape[1]
    extent = atoms + 2 * ghost
    space = lax.axis_size("space")
    chain = lax.axis_size("image")
    big = pltpu.CompilerParams(dimension_semantics=("arbitrary",), vmem_limit_bytes=BIG_VMEM)
    small = pltpu.CompilerParams(vmem_limit_bytes=SMALL_VMEM)
    pos = positions.transpose(1, 0, 2)
    vel = velocity.transpose(1, 0, 2)

    plo, pup = neighbours_of((pos[:, :, :ghost], pos[:, :, ghost:]), "space")
    before = lax.ppermute(pos[:, images - 1], "image", [(i, i + 1) for i in range(chain - 1)])
    after = lax.ppermute(pos[:, 0], "image", [(i + 1, i) for i in range(chain - 1)])
    read1 = read_first.reshape(1, ch)
    read2 = read_second.reshape(1, ch)
    geo_n = NL + 4

    head, tail, geo, hid, dsl, mom, dpre, en1 = pl.pallas_call(
        first_kernel,
        grid=(images,),
        in_specs=[
            whole((3, images, atoms)),
            whole((3, images, ghost)),
            whole((3, images, ghost)),
            per_image((slots, atoms)),
            whole((images, atoms)),
            whole((nb, rh)),
            whole((rh, ch)),
            whole((3 * ch, ch)),
            whole((1, ch)),
        ],
        out_specs=[
            per_image((ch, ghost)),
            per_image((ch, ghost)),
            per_image((geo_n, slots, atoms)),
            per_image((slots, rh, atoms)),
            per_image((slots, rh, atoms)),
            per_image((NL, ch, atoms)),
            per_image((ch, atoms)),
            per_image((8, 128)),
        ],
        out_shape=[
            out(images, ch, ghost),
            out(images, ch, ghost),
            out(images, geo_n, slots, atoms),
            out(images, slots, rh, atoms),
            out(images, slots, rh, atoms),
            out(images, NL, ch, atoms),
            out(images, ch, atoms),
            out(images, 8, 128),
        ],
        scratch_shapes=[
            pltpu.VMEM((slots, NL, 8, atoms), f32),
            pltpu.VMEM((NL, rh, atoms), f32),
        ],
        compiler_params=big,
        name="first",
    )(pos, plo, pup, neighbours, counts, radial_a1, radial_b1, mix_first, read1)

    hlo, hup = neighbours_of((head, tail), "space")

    dfh, dft, dlo, dup, dy2, dlen2, en2 = pl.pallas_call(
        second_kernel,
        grid=(images,),
        in_specs=[per_image((ch, ghost))] * 4
        + [
            per_image((slots, atoms)),
            per_image((geo_n, slots, atoms)),
            whole((nb, rh)),
            whole((rh, ch)),
            whole((3 * ch, ch)),
            whole((1, ch)),
        ],
        out_specs=[per_image((ch, ghost))] * 4
        + [
            per_image((NL, slots, atoms)),
            per_image((slots, atoms)),
            per_image((8, 128)),
        ],
        out_shape=[out(images, ch, ghost)] * 4
        + [
            out(images, NL, slots, atoms),
            out(images, slots, atoms),
            out(images, 8, 128),
        ],
        scratch_shapes=[
            pltpu.VMEM((slots, NL, 8, atoms), f32),
            pltpu.VMEM((2 * ch, extent), bf16),
            pltpu.VMEM((extent, slots * atoms), bf16),
            pltpu.VMEM((slots, ch, atoms), f32),
            pltpu.VMEM((slots, ch, atoms), f32),
            pltpu.VMEM((slots, ch, atoms), f32),
            pltpu.VMEM((NL, ch, atoms), f32),
            pltpu.VMEM((2 * ch, slots * atoms), bf16),
        ],
        compiler_params=big,
        name="second",
    )(head, tail, hlo, hup, neighbours, geo, radial_a2, radial_b2, mix_second, read2)

    rlo, rup = neighbours_of((dlo, dup), "space")

    own, flo, fup = pl.pallas_call(
        third_kernel,
        grid=(images,),
        in_specs=[per_image((ch, ghost))] * 4
        + [
            per_image((slots, atoms)),
            per_image((geo_n, slots, atoms)),
            per_image((slots, rh, atoms)),
            per_image((slots, rh, atoms)),
            per_image((NL, ch, atoms)),
            per_image((ch, atoms)),
            per_image((NL, slots, atoms)),
            per_image((slots, atoms)),
            whole((rh, ch)),
            whole((3 * ch, ch)),
            whole((1, ch)),
        ],
        out_specs=[
            whole((3, images, atoms)),
            whole((3, images, ghost)),
            whole((3, images, ghost)),
        ],
        out_shape=[out(3, images, atoms), out(3, images, ghost), out(3, images, ghost)],
        scratch_shapes=[
            pltpu.VMEM((slots, NL, 8, atoms), f32),
            pltpu.VMEM((NL, ch, atoms), f32),
            pltpu.VMEM((NL, rh, atoms), f32),
            pltpu.VMEM((1, NL, slots, atoms), f32),
            pltpu.VMEM((1, slots, atoms), f32),
            pltpu.VMEM((3, slots, atoms), f32),
        ],
        compiler_params=big,
        name="third",
    )(
        dfh, dft, rlo, rup, neighbours, geo, hid, dsl, mom, dpre, dy2, dlen2,
        radial_b1, mix_first, read1,
    )

    glo, gup = neighbours_of((flo, fup), "space")

    rank = chain * space
    force, send = pl.pallas_call(
        functools.partial(partial_kernel, chain=chain),
        in_specs=[VMEM] * 11,
        out_specs=[VMEM] * 2,
        out_shape=[out(3, images, atoms), out(rank, 128)],
        compiler_params=small,
        name="partial",
    )(own, glo, gup, pos, before, after, start_state, end_state, vel, en1, en2)
    got = lax.all_to_all(
        send.reshape(rank, 1, 128), ("image", "space"), split_axis=0, concat_axis=0
    ).reshape(rank, 128)
    neb, vnext, pnext, energy = pl.pallas_call(
        functools.partial(final_kernel, chain=chain, slabs=space),
        in_specs=[VMEM, SMEM] + [VMEM] * 7,
        out_specs=[VMEM] * 3 + [SMEM],
        out_shape=[out(3, images, atoms)] * 3 + [out(images)],
        compiler_params=small,
        name="final",
    )(got, climb_index, force, pos, before, after, start_state, end_state, vel)
    return (
        neb.transpose(1, 0, 2),
        vnext.transpose(1, 0, 2),
        pnext.transpose(1, 0, 2),
        energy,
    )


def solution(mesh):
    in_specs = (
        P("image", None, "space"),
        P("image", None, "space"),
        P(None, "space"),
        P(None, "space"),
        P("image", None, "space"),
        P("image", "space"),
        P(),
        P(),
        P(),
        P(),
        P(),
        P(),
        P(),
        P(),
        P(),
    )
    out_specs = (
        P("image", None, "space"),
        P("image", None, "space"),
        P("image", None, "space"),
        P("image"),
    )
    return jax.shard_map(local, mesh=mesh, in_specs=in_specs, out_specs=out_specs, check_vma=False)
```

time: 120 us -> 103 us (0.86)
  Pallas kernels: 52 us -> 35.9 us
  local copies, waits for them, and re-layouts: 15 us -> 11.3 us
  waiting for transfers between devices: 10.1 us -> 13.1 us
    pallas_call x1, Pallas kernels: 30.3 us -> 23.2 us  [local(): pl.pallas_call(second_kernel, grid=(images,), in_specs=[per_image((ch, gh...]
    pallas_call x3, Pallas kernels: 11.4 us -> 6.43 us  [the longest x1 4.59 us: local(): pl.pallas_call(first_kernel, grid=(images,), in_specs=[whole((3, images,...]
    pallas_call x1, Pallas kernels: 10.3 us -> 6.25 us  [local(): pl.pallas_call(third_kernel, grid=(images,), in_specs=[per_image((ch, gho...]
    reshape x3 -> x0, local copies, waits for them, and re-layouts: 4.02 us -> none  [the longest x1 1.38 us: local(): read2 = read_second.reshape(ch, 1)]
    ppermute x4, waiting for transfers between devices: 1.19 us -> 4.18 us  [neighbours_of(): lax.ppermute(to_above, axis, up)]
    unnamed x31 -> x35, local copies, waits for them, and re-layouts: 8.98 us -> 11.3 us
    slice x2 -> x1, local copies, waits for them, and re-layouts: 1.31 us -> 0.01 us  [local(): plo, pup = neighbours_of((pos[:, :, :ghost], pos[:, :, ghost:]), 'space')]
  transfers between devices with their start and end apart: 11 -> 11, of which waited for: 2 -> 4; matrix products, arithmetic and copies ran while one was open for 5% -> 0% of each run, Pallas kernels for 9% -> 6%
where the time goes in v2:
time: 103 us
  starting transfers between devices  40.7 us (40%)
  Pallas kernels  35.9 us (35%)
  waiting for transfers between devices  13.1 us (13%)
  local copies, waits for them, and re-layouts  11.3 us (11%)
  between operations  1.58 us (2%)
    pallas_call x1, Pallas kernels, local(): pl.pallas_call(second_kernel, grid=(images,), in_specs=[per_image((ch, gh...  23.2 us
    ppermute x4, starting transfers between devices, neighbours_of(): lax.ppermute(to_below, axis, down)  19.4 us
    unnamed x35, local copies, waits for them, and re-layouts  11.3 us
    all_to_all x1, starting transfers between devices, local(): lax.all_to_all(send.reshape(rank, 1, 128), ('image', 'space'), split_axis...  10.5 us
    all_to_all x1, waiting for transfers between devices, local(): lax.all_to_all(send.reshape(rank, 1, 128), ('image', 'space'), split_axis...  8.94 us
    pallas_call x1, Pallas kernels, local(): pl.pallas_call(third_kernel, grid=(images,), in_specs=[per_image((ch, gho...  6.25 us
    ppermute x1, starting transfers between devices, local(): lax.ppermute(pos[:, images - 1], 'image', [(i, i + 1) for i in range(chai...  6.25 us
    pallas_call x1, Pallas kernels, local(): pl.pallas_call(first_kernel, grid=(images,), in_specs=[whole((3, images,...  4.59 us
  transfers between devices with their start and end apart: 11, of which 4 were waited for; matrix products, arithmetic and copies ran while one was open for 0% of the time, Pallas kernels for 6%

profile of v2, /device:TPU:1, one launch (start us, length us, event | category | flops | bytes accessed | tf_op | source)
XLA Modules:
  0.0 102.6 jit_solution(11561006598478702496)
XLA Ops:
  0.6 0.7 copy.33
  1.3 2.5 %collective-permute-start = (f32[3,2,128]{2,0,1:T(4,128)S(1)}, f32[3,2,128]{2,0,1:T(4,128)S(1)}, u32[]{:S(2)}, u32[]{:S(2)}) collective-permute-start(f32[3,2,128]{2,0,1:T(4,128)S(1)} %get-tuple-element.55), channel_id=1, source_target_pairs={{0,1},{1,2},{2,3},{3,4},{4,5},{5,6},{6,7},{7,8},{8,9},{9,10},{10,1... | collective-permute-start | bytes 9224 | tf_op jit(solution)/shard_map/ppermute | solution.py:458
  3.8 4.6 %collective-permute-start.1 = (f32[3,2,128]{2,0,1:T(4,128)S(1)}, f32[3,2,128]{2,0,1:T(4,128)S(1)}, u32[]{:S(2)}, u32[]{:S(2)}) collective-permute-start(f32[3,2,128]{2,0,1:T(4,128)S(1)} %get-tuple-element.54), channel_id=1, source_target_pairs={{1,0},{2,1},{3,2},{4,3},{5,4},{6,5},{7,6},{8,7},{9,8},{10,9},{11,1... | collective-permute-start | bytes 9224 | tf_op jit(solution)/shard_map/ppermute | solution.py:458
  8.4 0.9 collective-permute-done
  9.4 0.0 collective-permute-done.1
  9.4 0.0 copy-start
  9.4 0.9 copy-done
  10.3 0.0 copy-start.2
  10.3 0.8 copy-done.2
  11.1 0.8 copy-done.5
  11.8 0.7 copy-done.11
  12.5 0.7 copy-done.13
  13.2 0.7 copy-done.14
  13.8 4.6 %first.1 = (f32[2,128,128]{2,1,0:T(8,128)S(1)}, f32[2,128,128]{2,1,0:T(8,128)S(1)}, f32[2,13,16,256]{3,2,1,0:T(8,128)S(1)}, f32[2,16,64,256]{3,2,1,0:T(8,128)S(1...) custom-call(f32[3,2,256]{2,1,0:T(2,128)S(1)} %copy.26.pos_ref, ...), custom_call_target="tpu_custom_call" | custom-call | tf_op jit(solution)/shard_map/first/pallas_call | solution.py:498
  18.4 0.1 collective-permute-start.2
  18.5 4.9 %collective-permute-start.3 = (f32[2,128,128]{2,1,0:T(8,128)S(1)}, f32[2,128,128]{2,1,0:T(8,128)S(1)}, u32[]{:S(2)}, u32[]{:S(2)}) collective-permute-start(f32[2,128,128]{2,1,0:T(8,128)S(1)} %get-tuple-element.28.head_ref), channel_id=1, source_target_pairs={{1,0},{2,1},{3,2},{4,3},{5,4},{6,5},{7,6},{8,7},{9,8},{10,9},{11,1... | collective-permute-start | bytes 393224 | tf_op jit(solution)/shard_map/ppermute | solution.py:458
  23.4 2.3 %collective-permute-done.2.hlo_ref = f32[2,128,128]{2,1,0:T(8,128)S(1)} collective-permute-done((f32[2,128,128]{2,1,0:T(8,128)S(1)}, f32[2,128,128]{2,1,0:T(8,128)S(1)}, u32[]{:S(2)}, u32[]{:S(2)}) %collective-permute-start.2) | collective-permute-done | bytes 131104 | tf_op jit(solution)/shard_map/ppermute | solution.py:458
  25.7 0.0 collective-permute-done.3.hup_ref
  25.7 0.8 copy-done.3
  26.5 0.9 copy-done.4
  27.4 0.8 copy-done.7
  28.1 0.7 copy-done.12
  28.8 0.7 copy-done.16
  29.5 23.2 %second.1 = (f32[2,128,128]{2,1,0:T(8,128)S(1)}, f32[2,128,128]{2,1,0:T(8,128)S(1)}, f32[2,128,128]{2,1,0:T(8,128)S(1)}, f32[2,128,128]{2,1,0:T(8,128)S(1)}, f32...) custom-call(f32[2,128,128]{2,1,0:T(8,128)S(1)} %get-tuple-element.28.head_ref, ...), custom_call_target="tpu_custom_call" | custom-call | tf_op jit(solution)/shard_map/second/pallas_call | solution.py:542
  52.7 0.1 collective-permute-start.4
  52.8 5.1 %collective-permute-start.5 = (f32[2,128,128]{2,1,0:T(8,128)S(1)}, f32[2,128,128]{2,1,0:T(8,128)S(1)}, u32[]{:S(2)}, u32[]{:S(2)}) collective-permute-start(f32[2,128,128]{2,1,0:T(8,128)S(1)} %get-tuple-element.34), channel_id=1, source_target_pairs={{1,0},{2,1},{3,2},{4,3},{5,4},{6,5},{7,6},{8,7},{9,8},{10,9},{11,1... | collective-permute-start | bytes 393224 | tf_op jit(solution)/shard_map/ppermute | solution.py:458
  57.9 6.3 %collective-permute-start.8 = (f32[3,256]{1,0:T(4,128)S(1)}, f32[3,256]{1,0:T(4,128)S(1)}, u32[]{:S(2)}, u32[]{:S(2)}) collective-permute-start(f32[3,256]{1,0:T(4,128)S(1)} %get-tuple-element.53), channel_id=1, source_target_pairs={{0,16},{16,32},{32,48},{48,64},{64,80},{80,96},{96,112},{1,17},{17... | collective-permute-start | bytes 9224 | tf_op jit(solution)/shard_map/ppermute | solution.py:492
  64.2 1.9 %collective-permute-start.9 = (f32[3,256]{1,0:T(4,128)S(1)}, f32[3,256]{1,0:T(4,128)S(1)}, u32[]{:S(2)}, u32[]{:S(2)}) collective-permute-start(f32[3,256]{1,0:T(4,128)S(1)} %get-tuple-element.52), channel_id=1, source_target_pairs={{16,0},{32,16},{48,32},{64,48},{80,64},{96,80},{112,96},{17,1},{33... | collective-permute-start | bytes 9224 | tf_op jit(solution)/shard_map/ppermute | solution.py:493
  66.1 0.0 collective-permute-done.4.rlo_ref
  66.1 0.0 collective-permute-done.5.rup_ref
  66.1 0.0 copy-start.1
  66.1 0.9 copy-done.1
  67.0 0.8 copy-done.6
  67.8 0.7 copy-done.15
  68.5 6.3 %third.1 = (f32[3,2,256]{2,1,0:T(2,128)S(1)}, f32[3,2,128]{2,1,0:T(2,128)S(1)}, f32[3,2,128]{2,1,0:T(2,128)S(1)}) custom-call(f32[2,128,128]{2,1,0:T(8,128)S(1)} %get-tuple-element.31.dfh_ref, f32[2,128,128]{2,1,0:T(8,128)S(1)} %get-tuple-element.32.dft_ref, f32[2,128,128]{2,1,0:T(8,128)S(1)} %collective-permute-done.4.rlo_ref, ...), custom_call_target="tpu_custom_call" | custom-call | tf_op jit(solution)/shard_map/third/pallas_call | solution.py:582
  74.7 0.1 collective-permute-start.6
  74.8 4.8 %collective-permute-start.7 = (f32[3,2,128]{2,1,0:T(2,128)S(1)}, f32[3,2,128]{2,1,0:T(2,128)S(1)}, u32[]{:S(2)}, u32[]{:S(2)}) collective-permute-start(f32[3,2,128]{2,1,0:T(2,128)S(1)} %get-tuple-element.43), channel_id=1, source_target_pairs={{1,0},{2,1},{3,2},{4,3},{5,4},{6,5},{7,6},{8,7},{9,8},{10,9},{11,1... | collective-permute-start | bytes 9224 | tf_op jit(solution)/shard_map/ppermute | solution.py:458
  79.6 0.0 collective-permute-done.8.before_ref
  79.6 0.0 collective-permute-done.9.after_ref
  79.6 1.0 collective-permute-done.6.rlo_ref
  80.6 0.0 collective-permute-done.7.rup_ref
  80.6 0.0 copy-done.8
  80.6 0.0 copy-done.9
  80.6 0.0 copy-done.10
  80.6 0.7 partial.1
  81.3 10.5 %all-to-all-start = ((f32[128,1,128]{2,1,0:T(1,128)}), f32[128,1,128]{2,1,0:T(1,128)S(1)}, u32[]{:S(2)}, u32[]{:S(2)}) async-start(f32[128,1,128]{2,1,0:T(1,128)} %bitcast.7), calls=%async_computation | async-start | bytes 131072 | tf_op jit(solution)/shard_map/all_to_all | solution.py:631
  92.4 8.9 %all-to-all-done = f32[128,1,128]{2,1,0:T(1,128)S(1)} async-done(((f32[128,1,128]{2,1,0:T(1,128)}), f32[128,1,128]{2,1,0:T(1,128)S(1)}, u32[]{:S(2)}, u32[]{:S(2)}) %all-to-all-start) | async-done | bytes 65568 | tf_op jit(solution)/shard_map/all_to_all | solution.py:631
  101.4 1.1 %final.1 = (f32[3,2,256]{2,1,0:T(2,128)}, f32[3,2,256]{2,1,0:T(2,128)}, f32[3,2,256]{2,1,0:T(2,128)}, f32[2]{0:T(128)}) custom-call(f32[128,128]{1,0:T(8,128)S(1)} %bitcast.17, s32[1]{0:T(128)S(6)} %copy.34.climb_ref, f32[3,2,256]{2,1,0:T(2,128)S(1)} %get-tuple-element.47.force_ref, f32[3,2,256]{2,1,0:T(2,128)S(1)} %copy.26.pos_ref, ...), custom_call_target="tpu_custom_call" | custom-call | tf_op jit(solution)/shard_map/final/pallas_call | solution.py:634
  (19 shorter events, 0.0 us)
Async XLA Ops:
  1.3 8.0 %collective-permute-start = (f32[3,2,128]{2,0,1:T(4,128)S(1)}, f32[3,2,128]{2,0,1:T(4,128)S(1)}, u32[]{:S(2)}, u32[]{:S(2)}) collective-permute-start(f32[3,2,128]{2,0,1:T(4,128)S(1)} %get-tuple-element.55), channel_id=1, source_target_pairs={{0,1},{1,2},{2,3},{3,4},{4,5},{5,6},{6,7},{7,8},{8,9},{9,10},{10,1... | collective-permute-start | bytes 9224 | tf_op jit(solution)/shard_map/ppermute | solution.py:458
  3.8 5.6 %collective-permute-start.1 = (f32[3,2,128]{2,0,1:T(4,128)S(1)}, f32[3,2,128]{2,0,1:T(4,128)S(1)}, u32[]{:S(2)}, u32[]{:S(2)}) collective-permute-start(f32[3,2,128]{2,0,1:T(4,128)S(1)} %get-tuple-element.54), channel_id=1, source_target_pairs={{1,0},{2,1},{3,2},{4,3},{5,4},{6,5},{7,6},{8,7},{9,8},{10,9},{11,1... | collective-permute-start | bytes 9224 | tf_op jit(solution)/shard_map/ppermute | solution.py:458
  9.4 0.9 copy-start
  10.3 0.8 copy-start.2
  11.1 0.8 copy-start.5
  11.8 0.7 copy-start.11
  12.5 0.7 copy-start.13
  13.2 0.7 copy-start.14
  18.4 7.3 %collective-permute-start.2 = (f32[2,128,128]{2,1,0:T(8,128)S(1)}, f32[2,128,128]{2,1,0:T(8,128)S(1)}, u32[]{:S(2)}, u32[]{:S(2)}) collective-permute-start(f32[2,128,128]{2,1,0:T(8,128)S(1)} %get-tuple-element.29.tail_ref), channel_id=1, source_target_pairs={{0,1},{1,2},{2,3},{3,4},{4,5},{5,6},{6,7},{7,8},{8,9},{9,10},{10,1... | collective-permute-start | bytes 393224 | tf_op jit(solution)/shard_map/ppermute | solution.py:458
  18.5 7.2 %collective-permute-start.3 = (f32[2,128,128]{2,1,0:T(8,128)S(1)}, f32[2,128,128]{2,1,0:T(8,128)S(1)}, u32[]{:S(2)}, u32[]{:S(2)}) collective-permute-start(f32[2,128,128]{2,1,0:T(8,128)S(1)} %get-tuple-element.28.head_ref), channel_id=1, source_target_pairs={{1,0},{2,1},{3,2},{4,3},{5,4},{6,5},{7,6},{8,7},{9,8},{10,9},{11,1... | collective-permute-start | bytes 393224 | tf_op jit(solution)/shard_map/ppermute | solution.py:458
  25.7 0.8 copy-start.3
  26.5 0.9 copy-start.4
  27.4 0.8 copy-start.7
  28.1 0.7 copy-start.12
  28.8 0.7 copy-start.16
  52.7 13.4 %collective-permute-start.4 = (f32[2,128,128]{2,1,0:T(8,128)S(1)}, f32[2,128,128]{2,1,0:T(8,128)S(1)}, u32[]{:S(2)}, u32[]{:S(2)}) collective-permute-start(f32[2,128,128]{2,1,0:T(8,128)S(1)} %get-tuple-element.33), channel_id=1, source_target_pairs={{0,1},{1,2},{2,3},{3,4},{4,5},{5,6},{6,7},{7,8},{8,9},{9,10},{10,1... | collective-permute-start | bytes 393224 | tf_op jit(solution)/shard_map/ppermute | solution.py:458
  52.8 13.3 %collective-permute-start.5 = (f32[2,128,128]{2,1,0:T(8,128)S(1)}, f32[2,128,128]{2,1,0:T(8,128)S(1)}, u32[]{:S(2)}, u32[]{:S(2)}) collective-permute-start(f32[2,128,128]{2,1,0:T(8,128)S(1)} %get-tuple-element.34), channel_id=1, source_target_pairs={{1,0},{2,1},{3,2},{4,3},{5,4},{6,5},{7,6},{8,7},{9,8},{10,9},{11,1... | collective-permute-start | bytes 393224 | tf_op jit(solution)/shard_map/ppermute | solution.py:458
  57.9 21.7 %collective-permute-start.8 = (f32[3,256]{1,0:T(4,128)S(1)}, f32[3,256]{1,0:T(4,128)S(1)}, u32[]{:S(2)}, u32[]{:S(2)}) collective-permute-start(f32[3,256]{1,0:T(4,128)S(1)} %get-tuple-element.53), channel_id=1, source_target_pairs={{0,16},{16,32},{32,48},{48,64},{64,80},{80,96},{96,112},{1,17},{17... | collective-permute-start | bytes 9224 | tf_op jit(solution)/shard_map/ppermute | solution.py:492
  64.2 15.4 %collective-permute-start.9 = (f32[3,256]{1,0:T(4,128)S(1)}, f32[3,256]{1,0:T(4,128)S(1)}, u32[]{:S(2)}, u32[]{:S(2)}) collective-permute-start(f32[3,256]{1,0:T(4,128)S(1)} %get-tuple-element.52), channel_id=1, source_target_pairs={{16,0},{32,16},{48,32},{64,48},{80,64},{96,80},{112,96},{17,1},{33... | collective-permute-start | bytes 9224 | tf_op jit(solution)/shard_map/ppermute | solution.py:493
  66.1 0.9 copy-start.1
  67.0 0.8 copy-start.6
  67.8 0.7 copy-start.15
  68.4 12.1 %copy-start.8 = (f32[2,3,256]{2,0,1:T(2,128)S(1)}, f32[2,3,256]{2,0,1:T(2,128)}, u32[]{:S(2)}) copy-start(f32[2,3,256]{2,0,1:T(2,128)} %param.16) | copy-start | bytes 18436
  68.5 12.1 %copy-start.9 = (f32[3,256]{1,0:T(4,128)S(1)}, f32[3,256]{1,0:T(4,128)}, u32[]{:S(2)}) copy-start(f32[3,256]{1,0:T(4,128)} %start_ref.3) | copy-start | bytes 9220
  68.5 12.1 %copy-start.10 = (f32[3,256]{1,0:T(4,128)S(1)}, f32[3,256]{1,0:T(4,128)}, u32[]{:S(2)}) copy-start(f32[3,256]{1,0:T(4,128)} %end_ref.3) | copy-start | bytes 9220
  74.7 5.8 %collective-permute-start.6 = (f32[3,2,128]{2,1,0:T(2,128)S(1)}, f32[3,2,128]{2,1,0:T(2,128)S(1)}, u32[]{:S(2)}, u32[]{:S(2)}) collective-permute-start(f32[3,2,128]{2,1,0:T(2,128)S(1)} %get-tuple-element.42), channel_id=1, source_target_pairs={{0,1},{1,2},{2,3},{3,4},{4,5},{5,6},{6,7},{7,8},{8,9},{9,10},{10,1... | collective-permute-start | bytes 9224 | tf_op jit(solution)/shard_map/ppermute | solution.py:458
  74.8 5.8 %collective-permute-start.7 = (f32[3,2,128]{2,1,0:T(2,128)S(1)}, f32[3,2,128]{2,1,0:T(2,128)S(1)}, u32[]{:S(2)}, u32[]{:S(2)}) collective-permute-start(f32[3,2,128]{2,1,0:T(2,128)S(1)} %get-tuple-element.43), channel_id=1, source_target_pairs={{1,0},{2,1},{3,2},{4,3},{5,4},{6,5},{7,6},{8,7},{9,8},{10,9},{11,1... | collective-permute-start | bytes 9224 | tf_op jit(solution)/shard_map/ppermute | solution.py:458
  81.3 20.1 %all-to-all-start = ((f32[128,1,128]{2,1,0:T(1,128)}), f32[128,1,128]{2,1,0:T(1,128)S(1)}, u32[]{:S(2)}, u32[]{:S(2)}) async-start(f32[128,1,128]{2,1,0:T(1,128)} %bitcast.7), calls=%async_computation | async-start | bytes 131072 | tf_op jit(solution)/shard_map/all_to_all | solution.py:631

commit v3 on v2

v3 whole, which is shorter than its diff:
```python
import functools
import math

import jax
import jax.numpy as jnp
from jax import lax
from jax.experimental import pallas as pl
from jax.experimental.pallas import tpu as pltpu
from jax.sharding import PartitionSpec as P

f32 = jnp.float32
bf16 = jnp.bfloat16
RT3 = math.sqrt(3.0)
NL = 9
BIG_VMEM = 24 << 20
SMALL_VMEM = 4 << 20


def split(x):
    hi = x.astype(bf16)
    lo = (x - hi.astype(f32)).astype(bf16)
    return hi, lo


def dot(a, b):
    return lax.dot_general(a, b, (((1,), (0,)), ((), ())), preferred_element_type=f32)


def dot_nt(a, b):
    return lax.dot_general(a, b, (((1,), (1,)), ((), ())), preferred_element_type=f32)


def pack_left(w):
    hi, lo = split(w)
    return jnp.concatenate([hi, hi, lo], axis=1)


def pack_right(x):
    hi, lo = split(x)
    return jnp.concatenate([hi, lo, hi], axis=0)


def one_hot(row, extent):
    step = 256
    wide = (step, row.shape[1])
    ids = lax.broadcasted_iota(jnp.int32, wide, 0).astype(f32).astype(bf16)
    zero, one = jnp.zeros(wide, bf16), jnp.ones(wide, bf16)
    parts = []
    for first in range(0, extent, step):
        here = jnp.broadcast_to((row - first).astype(f32), wide).astype(bf16)
        parts.append(jnp.where(ids == here, one, zero))
    return jnp.concatenate(parts, axis=0)


def lane_gather(row, idx):
    slots, atoms = idx.shape
    extent = row.shape[1]
    lane = idx & 127
    tile = idx >> 7
    blocks = [jnp.broadcast_to(row[:, t : t + 128], (8, 128)) for t in range(0, extent, 128)]
    out_rows = []
    for s0 in range(0, slots, 8):
        cells = []
        for a0 in range(0, atoms, 128):
            at = lane[s0 : s0 + 8, a0 : a0 + 128]
            which = tile[s0 : s0 + 8, a0 : a0 + 128]
            got = None
            for t, block in enumerate(blocks):
                v = jnp.take_along_axis(block, at, axis=1, mode="promise_in_bounds")
                got = v if got is None else jnp.where(which == t, v, got)
            cells.append(got)
        out_rows.append(jnp.concatenate(cells, axis=1))
    return jnp.concatenate(out_rows, axis=0)


def pick(block, i, axis):
    n = block.shape[axis]
    got = lax.index_in_dim(block, 0, axis, keepdims=False)
    for m in range(1, n):
        got = jnp.where(i == m, lax.index_in_dim(block, m, axis, keepdims=False), got)
    return got


def silu_parts(z):
    s = 0.5 + 0.5 * jnp.tanh(0.5 * z)
    h = z * s
    return h, s + h * (1.0 - s)


def basis_of(row):
    nb = 8
    centres = 0.5 * lax.broadcasted_iota(jnp.int32, (nb, row.shape[1]), 0).astype(f32)
    spread = row - centres
    basis = jnp.exp(-2.0 * spread * spread)
    return basis, -4.0 * spread * basis


def moments_into(edge_tile, yb_ref, m_ref, chans, slots, atoms):
    def tile(t, carry):
        c0 = pl.multiple_of(t * 16, 16)
        for a0 in range(0, atoms, 128):
            acc = [jnp.zeros((16, 128), f32) for _ in range(NL)]
            for k in range(slots):
                e = edge_tile(k, c0, a0)
                acc[0] = acc[0] + e
                for l in range(1, NL):
                    y = yb_ref[k, l - 1, :, a0 : a0 + 128]
                    acc[l] = acc[l] + e * jnp.concatenate([y, y], axis=0)
            for l in range(NL):
                m_ref[l, pl.ds(c0, 16), a0 : a0 + 128] = acc[l]
        return carry

    lax.fori_loop(0, chans // 16, tile, 0)


def store_yb(yb_ref, angular, slots, atoms):
    for k in range(slots):
        for l in range(NL - 1):
            yb_ref[k, l] = jnp.broadcast_to(angular[l][k : k + 1], (8, atoms))


def invariants_of(m_ref):
    m = [m_ref[l] for l in range(NL)]
    one = m[1] * m[1] + m[2] * m[2] + m[3] * m[3]
    two = m[4] * m[4] + m[5] * m[5] + m[6] * m[6] + m[7] * m[7] + m[8] * m[8]
    return jnp.concatenate([m[0], one, two], axis=0)


def moment_grads_into(m_ref, dinv, chans):
    m_ref[0] = dinv[:chans]
    d1 = 2.0 * dinv[chans : 2 * chans]
    d2 = 2.0 * dinv[2 * chans :]
    for l in range(1, NL):
        m_ref[l] = m_ref[l] * (d1 if l < 4 else d2)


def prep_kernel(*refs):
    n = 10
    hbm, outs, bufs, sems = refs[:n], refs[n : n + 13], refs[n + 13 : -1], refs[-1]
    (
        idx_out, cnt_out, a1_out, b1_out, m1t_out, m1_out, b1t_out, r1_out,
        a2_out, b2_out, m2t_out, m2_out, r2_out,
    ) = outs
    a1, b1, m1, r1, a2, b2, m2, r2 = bufs
    targets = (idx_out, cnt_out) + bufs
    copies = [pltpu.make_async_copy(h, t, sems.at[q]) for q, (h, t) in enumerate(zip(hbm, targets))]
    for c in copies:
        c.start()
    for c in copies:
        c.wait()
    a1_out[...] = pack_left(a1[...].T)
    b1_out[...] = pack_left(b1[...].T)
    m1t_out[...] = pack_left(m1[...].T)
    m1_out[...] = pack_left(m1[...])
    b1t_out[...] = pack_left(b1[...])
    r1_out[...] = jnp.broadcast_to(r1[...], r1_out.shape[::-1]).T
    a2_out[...] = pack_left(a2[...].T)
    b2_out[...] = pack_left(b2[...].T)
    m2t_out[...] = pack_left(m2[...].T)
    m2_out[...] = pack_left(m2[...])
    r2_out[...] = jnp.broadcast_to(r2[...], r2_out.shape[::-1]).T


def energy_rows(read_ref, feat):
    ch, atoms = feat.shape
    read = read_ref[...]
    en = jnp.concatenate([read] * (atoms // 128), axis=1) * feat
    total = jnp.sum(en.reshape(ch // 8, 8, atoms), axis=0)
    return sum(total[:, a0 : a0 + 128] for a0 in range(0, atoms, 128))


def wide(read_ref, atoms):
    return jnp.concatenate([read_ref[...]] * (atoms // 128), axis=1)


def each_image(body):
    def kernel(*refs, images):
        def step(i, carry):
            body(i, *refs)
            return carry

        lax.fori_loop(0, images, step, 0)

    return kernel


@each_image
def first_kernel(
    i, pos_ref, plo_ref, pup_ref, before_ref, after_ref, idx_ref, cnt_ref, a_ref, b_ref, mixt_ref,
    read_ref, head_ref, tail_ref, geo_ref, hid_ref, dsl_ref, mom_ref, dpre_ref, en_ref,
    yb_ref, g_ref,
):
    slots, atoms = idx_ref.shape[1:]
    ghost = plo_ref.shape[2]
    idx = idx_ref[i]
    pos = pick(pos_ref[...], i, 1)
    plo = pick(plo_ref[...], i, 1)
    pup = pick(pup_ref[...], i, 1)
    ext = jnp.concatenate([plo, pos, pup], axis=1)
    off = [lane_gather(ext[x : x + 1], idx) - pos[x : x + 1] for x in range(3)]
    length = jnp.sqrt(off[0] * off[0] + off[1] * off[1] + off[2] * off[2] + 1.0)
    ux, uy, uz = [o / length for o in off]
    ids = lax.broadcasted_iota(jnp.int32, (slots, atoms), 0)
    cnt = pick(cnt_ref[...][None], i, 1)
    live = jnp.where(ids < cnt, 1.0 / slots, 0.0).astype(f32)
    angular = [
        ux,
        uy,
        uz,
        ux * uy,
        uy * uz,
        ux * uz,
        0.5 * (ux * ux - uy * uy),
        (3.0 * uz * uz - 1.0) / (2.0 * RT3),
    ]
    for l in range(NL - 1):
        geo_ref[i, l] = angular[l]
    geo_ref[i, NL - 1] = length
    geo_ref[i, NL] = live
    store_yb(yb_ref, angular, slots, atoms)
    for k in range(slots):
        basis, slope = basis_of(length[k : k + 1])
        hid, ds = silu_parts(dot(a_ref[...], pack_right(basis)))
        row = live[k : k + 1]
        hid_ref[i, k] = hid * row
        dsl_ref[i, k] = ds * row * dot(a_ref[...], pack_right(slope))

    def hid_tile(k, c0, a0):
        return hid_ref[i, k, pl.ds(c0, 16), a0 : a0 + 128]

    moments_into(hid_tile, yb_ref, g_ref, hid_ref.shape[2], slots, atoms)
    for l in range(NL):
        mom_ref[i, l] = dot(b_ref[...], pack_right(g_ref[l]))
    inv = invariants_of(mom_ref.at[i])
    feat, dpre = silu_parts(dot(mixt_ref[...], pack_right(inv)))
    dpre_ref[i] = dpre
    head_ref[i] = feat[:, :ghost]
    tail_ref[i] = feat[:, atoms - ghost :]
    en_ref[i] = energy_rows(read_ref, feat)


def edge_back(k, edge_tile, sink, yb_ref, m_ref, dy_ref, dlen_ref, chans, atoms):
    for a0 in range(0, atoms, 128):
        y = [yb_ref[k, l, :, a0 : a0 + 128] for l in range(NL - 1)]
        y = [jnp.concatenate([v, v], axis=0) for v in y]
        acc = [jnp.zeros((8, 128), f32) for _ in range(NL)]
        for c0 in range(0, chans, 16):
            e = edge_tile(k, c0, a0)
            de = m_ref[0, c0 : c0 + 16, a0 : a0 + 128]
            for l in range(1, NL):
                dm = m_ref[l, c0 : c0 + 16, a0 : a0 + 128]
                de = de + dm * y[l - 1]
                p = e * dm
                acc[l] = acc[l] + (p[:8] + p[8:])
            p = sink(k, c0, a0, de)
            acc[0] = acc[0] + (p[:8] + p[8:])
        for l in range(1, NL):
            dy_ref[l - 1, k : k + 1, a0 : a0 + 128] = jnp.sum(acc[l], axis=0, keepdims=True)
        dlen_ref[k : k + 1, a0 : a0 + 128] = jnp.sum(acc[0], axis=0, keepdims=True)


@each_image
def second_kernel(
    i, head_ref, tail_ref, hlo_ref, hup_ref, idx_ref, geo_ref, a_ref, b_ref, mixt_ref, mix_ref,
    read_ref, dfh_ref, dft_ref, dlo_ref, dup_ref, dy_ref, dlen_ref, en_ref,
    yb_ref, hf_ref, oh_ref, q_ref, rad_ref, radl_ref, m_ref, dq_ref,
):
    slots, atoms = idx_ref.shape[1:]
    ghost = hlo_ref.shape[2]
    ch = hlo_ref.shape[1]
    extent = atoms + 2 * ghost
    for n, ref in enumerate((hlo_ref, head_ref, tail_ref, hup_ref)):
        hi, lo = split(ref[i])
        hf_ref[:ch, n * ghost : (n + 1) * ghost] = hi
        hf_ref[ch:, n * ghost : (n + 1) * ghost] = lo
    store_yb(yb_ref, [geo_ref[i, l] for l in range(NL - 1)], slots, atoms)
    for k in range(slots):
        oh = one_hot(idx_ref[i, k : k + 1, :], extent)
        oh_ref[:, k * atoms : (k + 1) * atoms] = oh
        got = dot(hf_ref[...], oh)
        q_ref[k] = got[:ch] + got[ch:]
        basis, slope = basis_of(geo_ref[i, NL - 1, k : k + 1, :])
        row = geo_ref[i, NL, k : k + 1, :]
        hid, ds = silu_parts(dot(a_ref[...], pack_right(basis)))
        rad_ref[k] = dot(b_ref[...], pack_right(hid * row))
        dsl = ds * row * dot(a_ref[...], pack_right(slope))
        radl_ref[k] = dot(b_ref[...], pack_right(dsl))

    def edge_tile(k, c0, a0):
        cs = pl.ds(c0, 16)
        return rad_ref[k, cs, a0 : a0 + 128] * q_ref[k, cs, a0 : a0 + 128]

    moments_into(edge_tile, yb_ref, m_ref, ch, slots, atoms)
    inv = invariants_of(m_ref)
    feat, dpre = silu_parts(dot(mixt_ref[...], pack_right(inv)))
    en_ref[i] = energy_rows(read_ref, feat)
    dinv = dot(mix_ref[...], pack_right(wide(read_ref, atoms) * dpre))
    moment_grads_into(m_ref, dinv, ch)

    def sink(k, c0, a0, de):
        cs = slice(c0, c0 + 16)
        ls = slice(a0, a0 + 128)
        hi, lo = split(de * rad_ref[k, cs, ls])
        ks = slice(k * atoms + a0, k * atoms + a0 + 128)
        dq_ref[cs, ks] = hi
        dq_ref[ch + c0 : ch + c0 + 16, ks] = lo
        return de * q_ref[k, cs, ls] * radl_ref[k, cs, ls]

    for k in range(slots):
        edge_back(k, edge_tile, sink, yb_ref, m_ref, dy_ref.at[i], dlen_ref.at[i], ch, atoms)
    back = dot_nt(dq_ref[...], oh_ref[...])
    back = back[:ch] + back[ch:]
    dlo_ref[i] = back[:, :ghost]
    dfh_ref[i] = back[:, ghost : 2 * ghost]
    dft_ref[i] = back[:, 2 * ghost : 3 * ghost]
    dup_ref[i] = back[:, 3 * ghost :]


@each_image
def third_kernel(
    i, dfh_ref, dft_ref, rlo_ref, rup_ref, idx_ref, geo_ref, hid_ref, dsl_ref, mom_ref, dpre_ref,
    dy2_ref, dlen2_ref, bt_ref, mix_ref, read_ref,
    own_ref, flo_ref, fup_ref,
    yb_ref, m_ref, dg_ref, dy_ref, dlen_ref, doff_ref,
):
    slots, atoms = idx_ref.shape[1:]
    ch, ghost = rlo_ref.shape[1:]
    rh = hid_ref.shape[2]
    extent = atoms + 2 * ghost
    store_yb(yb_ref, [geo_ref[i, l] for l in range(NL - 1)], slots, atoms)
    cot = jnp.concatenate([dfh_ref[i] + rlo_ref[i], dft_ref[i] + rup_ref[i]], axis=1)
    dpre = (cot + wide(read_ref, atoms)) * dpre_ref[i]
    dinv = dot(mix_ref[...], pack_right(dpre))
    for l in range(NL):
        m_ref[l] = mom_ref[i, l]
    moment_grads_into(m_ref, dinv, ch)
    for l in range(NL):
        dg_ref[l] = dot(bt_ref[...], pack_right(m_ref[l]))

    def edge_tile(k, c0, a0):
        return hid_ref[i, k, pl.ds(c0, 16), a0 : a0 + 128]

    def sink(k, c0, a0, de):
        return de * dsl_ref[i, k, c0 : c0 + 16, a0 : a0 + 128]

    for k in range(slots):
        edge_back(k, edge_tile, sink, yb_ref, dg_ref, dy_ref, dlen_ref, rh, atoms)
    dy = [None] + [dy_ref[l] + dy2_ref[i, l] for l in range(NL - 1)]
    ux, uy, uz = [geo_ref[i, n] for n in range(3)]
    length = geo_ref[i, NL - 1]
    dux = dy[1] + uy * dy[4] + uz * dy[6] + ux * dy[7]
    duy = dy[2] + ux * dy[4] + uz * dy[5] - uy * dy[7]
    duz = dy[3] + uy * dy[5] + ux * dy[6] + RT3 * uz * dy[8]
    radial = dlen_ref[...] + dlen2_ref[i] - (dux * ux + duy * uy + duz * uz) / length
    doff = [du / length + radial * u for du, u in ((dux, ux), (duy, uy), (duz, uz))]
    centre = jnp.concatenate([jnp.sum(d, axis=0, keepdims=True) for d in doff], axis=0)
    for x in range(3):
        doff_ref[x] = doff[x]
    back = jnp.zeros((16, extent), f32)
    pad = jnp.zeros((5, atoms), f32)
    for k in range(slots):
        rows = jnp.concatenate([doff_ref[x, k : k + 1, :] for x in range(3)] + [pad], axis=0)
        hi = rows.astype(bf16).astype(f32)
        both = jnp.concatenate([hi, rows - hi], axis=0).astype(bf16)
        back = back + dot_nt(both, one_hot(idx_ref[i, k : k + 1, :], extent))
    force = back[8:11] + back[:3]
    for n in range(own_ref.shape[1]):

        @pl.when(i == n)
        def _():
            own_ref[:, n, :] = centre - force[:, ghost : ghost + atoms]
            flo_ref[:, n, :] = -force[:, :ghost]
            fup_ref[:, n, :] = -force[:, ghost + atoms :]


def lane_row(values):
    lane = lax.broadcasted_iota(jnp.int32, (1, 128), 1)
    row = jnp.zeros((1, 128), f32)
    for n, v in enumerate(values):
        row = jnp.where(lane == n, v, row)
    return row


def total_of(x):
    return jnp.sum(jnp.sum(x, axis=1, keepdims=True), axis=0, keepdims=True)


def chain_of(pos_ref, before_ref, after_ref, start_ref, end_ref, chain):
    count = pos_ref.shape[1]
    me = lax.axis_index("image")
    before = jnp.where(me == 0, start_ref[...], before_ref[...])
    after = jnp.where(me == chain - 1, end_ref[...], after_ref[...])
    prev = [before] + [pos_ref[:, i, :] for i in range(count - 1)]
    nxt = [pos_ref[:, i, :] for i in range(1, count)] + [after]
    return prev, nxt


def partial_kernel(
    own_ref, rlo_ref, rup_ref, pos_ref, before_ref, after_ref, start_ref, end_ref,
    vel_ref, en1_ref, en2_ref, climb_ref, force_ref, send_ref, *, chain,
):
    count = pos_ref.shape[1]
    prev, nxt = chain_of(pos_ref, before_ref, after_ref, start_ref, end_ref, chain)
    values = []
    vel = jnp.zeros((1, 1), f32)
    for i in range(count):
        pos = pos_ref[:, i, :]
        force = own_ref[:, i, :] + jnp.concatenate([rlo_ref[:, i, :], rup_ref[:, i, :]], axis=1)
        force_ref[:, i, :] = force
        spread = nxt[i] - prev[i]
        ahead = nxt[i] - pos
        behind = pos - prev[i]
        values += [
            total_of(ahead * ahead),
            total_of(behind * behind),
            total_of(spread * spread),
            total_of(force * force),
            total_of(force * spread),
            total_of(en1_ref[i]) + total_of(en2_ref[i]),
        ]
        v = vel_ref[:, i, :]
        vel = vel + total_of(v * v)
    send_ref[...] = jnp.broadcast_to(lane_row(values + [vel, climb_ref[0].astype(f32)]), send_ref.shape)


def final_kernel(
    got_ref, force_ref, pos_ref, before_ref, after_ref, start_ref, end_ref,
    vel_ref, neb_ref, vnext_ref, pnext_ref, en_ref,
    *, chain, slabs,
):
    count = pos_ref.shape[1]
    atoms = pos_ref.shape[2]
    me = lax.axis_index("image")
    prev, nxt = chain_of(pos_ref, before_ref, after_ref, start_ref, end_ref, chain)
    rows = [
        jnp.sum(got_ref[g * slabs : (g + 1) * slabs, :], axis=0, keepdims=True)
        for g in range(chain)
    ]
    table = jnp.concatenate(rows, axis=0)
    climb = got_ref[0:1, 6 * count + 1 : 6 * count + 2]
    vel_sq = jnp.sum(table[:, 6 * count : 6 * count + 1], axis=0, keepdims=True)
    group = lax.broadcasted_iota(jnp.int32, (chain, 1), 0)
    force_sq = jnp.zeros((1, 1), f32)
    mine = []
    for i in range(count):
        ahead, behind, spread_sq, ff, fd, energy = [
            table[:, 6 * i + n : 6 * i + n + 1] for n in range(6)
        ]
        norm = 1.0 / jnp.sqrt(spread_sq + 1e-06)
        along = fd * norm
        climbing = jnp.where((group * count + i).astype(f32) == climb, 1.0, 0.0).astype(f32)
        spring = 5.0 * (jnp.sqrt(ahead) - jnp.sqrt(behind))
        coef = -(1.0 + climbing) * along + (1.0 - climbing) * spring
        scale = coef * norm
        part = ff + 2.0 * coef * along + scale * scale * spread_sq
        force_sq = force_sq + jnp.sum(part, axis=0, keepdims=True)
        here = group == me
        mine.append(jnp.sum(jnp.where(here, scale, 0.0), axis=0, keepdims=True))
        en_ref[i] = jnp.sum(jnp.where(here, energy, 0.0)) * (1.0 / (atoms * slabs))
    gain = 0.1 * jnp.sqrt(vel_sq / (force_sq + 1e-06))
    for i in range(count):
        neb = force_ref[:, i, :] + mine[i] * (nxt[i] - prev[i])
        neb_ref[:, i, :] = neb
        vnext = 0.9 * vel_ref[:, i, :] + gain * neb + 0.1 * neb
        vnext_ref[:, i, :] = vnext
        pnext_ref[:, i, :] = pos_ref[:, i, :] + 0.1 * vnext


def out(*shape):
    return jax.ShapeDtypeStruct(shape, f32)


def half(*shape):
    return jax.ShapeDtypeStruct(shape, bf16)


ANY = pl.BlockSpec(memory_space=pl.ANY)
VMEM = pl.BlockSpec(memory_space=pltpu.VMEM)
SMEM = pl.BlockSpec(memory_space=pltpu.SMEM)


def neighbours_of(cells, axis):
    count = lax.axis_size(axis)
    up = [(i, (i + 1) % count) for i in range(count)]
    down = [((i + 1) % count, i) for i in range(count)]
    to_below, to_above = cells
    return lax.ppermute(to_above, axis, up), lax.ppermute(to_below, axis, down)


def local(
    positions,
    velocity,
    start_state,
    end_state,
    neighbours,
    counts,
    climb_index,
    radial_a1,
    radial_b1,
    mix_first,
    read_first,
    radial_a2,
    radial_b2,
    mix_second,
    read_second,
):
    images, _, atoms = positions.shape
    slots = neighbours.shape[1]
    ghost = atoms // 2
    nb, rh = radial_a1.shape
    ch = radial_b1.shape[1]
    extent = atoms + 2 * ghost
    space = lax.axis_size("space")
    chain = lax.axis_size("image")
    params = pltpu.CompilerParams(vmem_limit_bytes=BIG_VMEM)
    small = pltpu.CompilerParams(vmem_limit_bytes=SMALL_VMEM)
    pos = positions.transpose(1, 0, 2)
    vel = velocity.transpose(1, 0, 2)

    plo, pup = neighbours_of((pos[:, :, :ghost], pos[:, :, ghost:]), "space")
    before = lax.ppermute(pos[:, images - 1], "image", [(i, i + 1) for i in range(chain - 1)])
    after = lax.ppermute(pos[:, 0], "image", [(i + 1, i) for i in range(chain - 1)])
    weights = (
        radial_a1, radial_b1, mix_first, read_first.reshape(1, ch),
        radial_a2, radial_b2, mix_second, read_second.reshape(1, ch),
    )
    idx, cnt, a1, b1, m1t, m1, b1t, r1, a2, b2, m2t, m2, r2 = pl.pallas_call(
        prep_kernel,
        in_specs=[pl.BlockSpec(memory_space=pltpu.HBM)] * 10,
        out_specs=[VMEM] * 13,
        out_shape=[
            jax.ShapeDtypeStruct(neighbours.shape, jnp.int32),
            jax.ShapeDtypeStruct(counts.shape, jnp.int32),
            half(rh, 3 * nb),
            half(ch, 3 * rh),
            half(ch, 9 * ch),
            half(3 * ch, 3 * ch),
            half(rh, 3 * ch),
            out(ch, 128),
            half(rh, 3 * nb),
            half(ch, 3 * rh),
            half(ch, 9 * ch),
            half(3 * ch, 3 * ch),
            out(ch, 128),
        ],
        scratch_shapes=[pltpu.VMEM(w.shape, f32) for w in weights]
        + [pltpu.SemaphoreType.DMA((10,))],
        compiler_params=small,
        cost_estimate=pl.CostEstimate(flops=4000000, bytes_accessed=4000000, transcendentals=0),
        name="prep",
    )(neighbours, counts, *weights)
    geo_n = NL + 1

    head, tail, geo, hid, dsl, mom, dpre, en1 = pl.pallas_call(
        functools.partial(first_kernel, images=images),
        in_specs=[VMEM] * 3 + [ANY] * 2 + [VMEM] * 6,
        out_specs=[VMEM] * 8,
        out_shape=[
            out(images, ch, ghost),
            out(images, ch, ghost),
            out(images, geo_n, slots, atoms),
            out(images, slots, rh, atoms),
            out(images, slots, rh, atoms),
            out(images, NL, ch, atoms),
            out(images, ch, atoms),
            out(images, 8, 128),
        ],
        scratch_shapes=[
            pltpu.VMEM((slots, NL - 1, 8, atoms), f32),
            pltpu.VMEM((NL, rh, atoms), f32),
        ],
        compiler_params=params,
        name="first",
    )(pos, plo, pup, before, after, idx, cnt, a1, b1, m1t, r1)

    hlo, hup = neighbours_of((head, tail), "space")

    dfh, dft, dlo, dup, dy2, dlen2, en2 = pl.pallas_call(
        functools.partial(second_kernel, images=images),
        in_specs=[VMEM] * 11,
        out_specs=[VMEM] * 7,
        out_shape=[out(images, ch, ghost)] * 4
        + [
            out(images, NL - 1, slots, atoms),
            out(images, slots, atoms),
            out(images, 8, 128),
        ],
        scratch_shapes=[
            pltpu.VMEM((slots, NL - 1, 8, atoms), f32),
            pltpu.VMEM((2 * ch, extent), bf16),
            pltpu.VMEM((extent, slots * atoms), bf16),
            pltpu.VMEM((slots, ch, atoms), f32),
            pltpu.VMEM((slots, ch, atoms), f32),
            pltpu.VMEM((slots, ch, atoms), f32),
            pltpu.VMEM((NL, ch, atoms), f32),
            pltpu.VMEM((2 * ch, slots * atoms), bf16),
        ],
        compiler_params=params,
        name="second",
    )(head, tail, hlo, hup, idx, geo, a2, b2, m2t, m2, r2)

    rlo, rup = neighbours_of((dlo, dup), "space")

    own, flo, fup = pl.pallas_call(
        functools.partial(third_kernel, images=images),
        in_specs=[VMEM] * 15,
        out_specs=[VMEM] * 3,
        out_shape=[out(3, images, atoms), out(3, images, ghost), out(3, images, ghost)],
        scratch_shapes=[
            pltpu.VMEM((slots, NL - 1, 8, atoms), f32),
            pltpu.VMEM((NL, ch, atoms), f32),
            pltpu.VMEM((NL, rh, atoms), f32),
            pltpu.VMEM((NL - 1, slots, atoms), f32),
            pltpu.VMEM((slots, atoms), f32),
            pltpu.VMEM((3, slots, atoms), f32),
        ],
        compiler_params=params,
        name="third",
    )(dfh, dft, rlo, rup, idx, geo, hid, dsl, mom, dpre, dy2, dlen2, b1t, m1, r1)

    glo, gup = neighbours_of((flo, fup), "space")

    rank = chain * space
    force, send = pl.pallas_call(
        functools.partial(partial_kernel, chain=chain),
        in_specs=[VMEM] * 11 + [SMEM],
        out_specs=[VMEM] * 2,
        out_shape=[out(3, images, atoms), out(rank, 128)],
        compiler_params=small,
        name="partial",
    )(own, glo, gup, pos, before, after, start_state, end_state, vel, en1, en2, climb_index)
    got = lax.all_to_all(
        send.reshape(rank, 1, 128), ("image", "space"), split_axis=0, concat_axis=0
    ).reshape(rank, 128)
    neb, vnext, pnext, energy = pl.pallas_call(
        functools.partial(final_kernel, chain=chain, slabs=space),
        in_specs=[VMEM] * 8,
        out_specs=[VMEM] * 3 + [SMEM],
        out_shape=[out(3, images, atoms)] * 3 + [out(images)],
        compiler_params=small,
        name="final",
    )(got, force, pos, before, after, start_state, end_state, vel)
    return (
        neb.transpose(1, 0, 2),
        vnext.transpose(1, 0, 2),
        pnext.transpose(1, 0, 2),
        energy,
    )


def solution(mesh):
    in_specs = (
        P("image", None, "space"),
        P("image", None, "space"),
        P(None, "space"),
        P(None, "space"),
        P("image", None, "space"),
        P("image", "space"),
        P(),
        P(),
        P(),
        P(),
        P(),
        P(),
        P(),
        P(),
        P(),
    )
    out_specs = (
        P("image", None, "space"),
        P("image", None, "space"),
        P("image", None, "space"),
        P("image"),
    )
    return jax.shard_map(local, mesh=mesh, in_specs=in_specs, out_specs=out_specs, check_vma=False)
```

time: 103 us -> 101 us (0.981)
  blocking collectives: 0 us -> 21.1 us
  starting transfers between devices: 40.7 us -> 28 us
  waiting for transfers between devices: 13.1 us -> 5.73 us
  local copies, waits for them, and re-layouts: 11.3 us -> 8.21 us
    all_to_all x0 -> x1, blocking collectives: none -> 21.1 us  [local(): lax.all_to_all(send.reshape(rank, 1, 128), ('image', 'space'), split_axis...]
    all_to_all x1 -> x0, starting transfers between devices: 10.5 us -> none  [local(): lax.all_to_all(send.reshape(rank, 1, 128), ('image', 'space'), split_axis...]
    all_to_all x1 -> x0, waiting for transfers between devices: 8.94 us -> none  [local(): lax.all_to_all(send.reshape(rank, 1, 128), ('image', 'space'), split_axis...]
    unnamed x35 -> x27, local copies, waits for them, and re-layouts: 11.3 us -> 8.19 us
    ppermute x1, starting transfers between devices: 6.25 us -> 3.95 us  [local(): lax.ppermute(pos[:, images - 1], 'image', [(i, i + 1) for i in range(chai...]
    ppermute x4, waiting for transfers between devices: 4.18 us -> 5.72 us  [neighbours_of(): lax.ppermute(to_above, axis, up)]
    pallas_call x3 -> x4, Pallas kernels: 34.1 us -> 34.1 us  [the longest x1 22.7 us: local(): pl.pallas_call(functools.partial(second_kernel, images=images), in_specs=...]
  transfers between devices with their start and end apart: 11 -> 10, of which waited for: 4 -> 3; matrix products, arithmetic and copies ran while one was open for 0% -> 0% of each run, Pallas kernels for 6% -> 1%
where the time goes in v3:
time: 101 us; the launch traced here: 100 us
  Pallas kernels  35.3 us (35%)
  starting transfers between devices  28 us (28%)
  blocking collectives  21.1 us (21%)
  local copies, waits for them, and re-layouts  8.21 us (8%)
  waiting for transfers between devices  5.73 us (6%)
  between operations  1.62 us (2%)
    pallas_call x1, Pallas kernels, local(): pl.pallas_call(functools.partial(second_kernel, images=images), in_specs=...  22.7 us
    all_to_all x1, blocking collectives, local(): lax.all_to_all(send.reshape(rank, 1, 128), ('image', 'space'), split_axis...  21.1 us
    ppermute x4, starting transfers between devices, neighbours_of(): lax.ppermute(to_below, axis, down)  19.4 us
    unnamed x27, local copies, waits for them, and re-layouts  8.19 us
    pallas_call x1, Pallas kernels, local(): pl.pallas_call(functools.partial(third_kernel, images=images), in_specs=[...  5.86 us
    ppermute x4, waiting for transfers between devices, neighbours_of(): lax.ppermute(to_above, axis, up)  5.72 us
    pallas_call x1, Pallas kernels, local(): pl.pallas_call(functools.partial(first_kernel, images=images), in_specs=[...  4.18 us
    ppermute x1, starting transfers between devices, local(): lax.ppermute(pos[:, images - 1], 'image', [(i, i + 1) for i in range(chai...  3.95 us
  transfers between devices with their start and end apart: 10, of which 3 were waited for; matrix products, arithmetic and copies ran while one was open for 0% of the time, Pallas kernels for 1%

profile of v3, /device:TPU:1, one launch (start us, length us, event | category | flops | bytes accessed | tf_op | source)
XLA Modules:
  0.0 100.0 jit_solution(8878738437383313196)
XLA Ops:
  0.6 0.7 copy.33
  1.3 2.5 %collective-permute-start = (f32[3,2,128]{2,0,1:T(4,128)S(1)}, f32[3,2,128]{2,0,1:T(4,128)S(1)}, u32[]{:S(2)}, u32[]{:S(2)}) collective-permute-start(f32[3,2,128]{2,0,1:T(4,128)S(1)} %get-tuple-element.81), channel_id=1, source_target_pairs={{0,1},{1,2},{2,3},{3,4},{4,5},{5,6},{6,7},{7,8},{8,9},{9,10},{10,1... | collective-permute-start | bytes 9224 | tf_op jit(solution)/shard_map/ppermute | solution.py:487
  3.8 4.6 %collective-permute-start.1 = (f32[3,2,128]{2,0,1:T(4,128)S(1)}, f32[3,2,128]{2,0,1:T(4,128)S(1)}, u32[]{:S(2)}, u32[]{:S(2)}) collective-permute-start(f32[3,2,128]{2,0,1:T(4,128)S(1)} %get-tuple-element.80), channel_id=1, source_target_pairs={{1,0},{2,1},{3,2},{4,3},{5,4},{6,5},{7,6},{8,7},{9,8},{10,9},{11,1... | collective-permute-start | bytes 9224 | tf_op jit(solution)/shard_map/ppermute | solution.py:487
  8.4 3.9 %collective-permute-start.2 = (f32[3,256]{1,0:T(4,128)S(1)}, f32[3,256]{1,0:T(4,128)S(1)}, u32[]{:S(2)}, u32[]{:S(2)}) collective-permute-start(f32[3,256]{1,0:T(4,128)S(1)} %get-tuple-element.79), channel_id=1, source_target_pairs={{0,16},{16,32},{32,48},{48,64},{64,80},{80,96},{96,112},{1,17},{17... | collective-permute-start | bytes 9224 | tf_op jit(solution)/shard_map/ppermute | solution.py:521
  12.4 1.9 %collective-permute-start.3 = (f32[3,256]{1,0:T(4,128)S(1)}, f32[3,256]{1,0:T(4,128)S(1)}, u32[]{:S(2)}, u32[]{:S(2)}) collective-permute-start(f32[3,256]{1,0:T(4,128)S(1)} %get-tuple-element.78), channel_id=1, source_target_pairs={{16,0},{32,16},{48,32},{64,48},{80,64},{96,80},{112,96},{17,1},{33... | collective-permute-start | bytes 9224 | tf_op jit(solution)/shard_map/ppermute | solution.py:522
  14.3 0.0 copy-start
  14.3 0.9 copy-done
  15.3 0.0 copy-start.1
  15.3 0.9 copy-done.1
  16.2 0.0 copy-start.2
  16.2 0.8 copy-done.2
  16.9 0.0 copy-start.3
  16.9 0.8 copy-done.3
  17.7 0.0 copy-start.4
  17.7 0.8 copy-done.4
  18.5 0.0 copy-start.8
  18.5 0.7 copy-done.8
  19.1 0.0 copy-start.9
  19.1 0.7 copy-done.9
  19.8 0.7 copy-done.10
  20.5 0.7 copy-done.11
  21.2 0.7 copy-done.12
  21.8 1.4 %prep.1 = (s32[2,16,256]{2,1,0:T(8,128)S(1)}, s32[2,256]{1,0:T(2,128)S(1)}, bf16[64,24]{1,0:T(8,128)(2,1)S(1)}, bf16[128,192]{1,0:T(8,128)(2,1)S(1)}, bf16[128,1...) custom-call(s32[2,16,256]{2,1,0:T(8,128)S(1)} %copy-done.2, ...), custom_call_target="tpu_custom_call" | custom-call | flops 4000000 | bytes 4000000 | tf_op jit(solution)/shard_map/prep/pallas_call | solution.py:527
  23.2 0.0 collective-permute-done
  23.2 0.0 collective-permute-done.1
  23.2 0.0 collective-permute-done.2.refs_3_.before_ref
  23.2 0.0 collective-permute-done.3.refs_4_.after_ref
  23.3 4.2 %first.1 = (f32[2,128,128]{2,1,0:T(8,128)S(1)}, f32[2,128,128]{2,1,0:T(8,128)S(1)}, f32[2,10,16,256]{3,2,1,0:T(8,128)S(1)}, f32[2,16,64,256]{3,2,1,0:T(8,128)S(1...) custom-call(f32[3,2,256]{2,1,0:T(2,128)S(1)} %copy.26.refs_0_.pos_re, ...), custom_call_target="tpu_custom_call" | custom-call | tf_op jit(solution)/shard_map/first/pallas_call | solution.py:554
  27.4 0.1 collective-permute-start.4
  27.5 4.8 %collective-permute-start.5 = (f32[2,128,128]{2,1,0:T(8,128)S(1)}, f32[2,128,128]{2,1,0:T(8,128)S(1)}, u32[]{:S(2)}, u32[]{:S(2)}) collective-permute-start(f32[2,128,128]{2,1,0:T(8,128)S(1)} %get-tuple-element.47.refs_0_), channel_id=1, source_target_pairs={{1,0},{2,1},{3,2},{4,3},{5,4},{6,5},{7,6},{8,7},{9,8},{10,9},{11,1... | collective-permute-start | bytes 393224 | tf_op jit(solution)/shard_map/ppermute | solution.py:487
  32.3 2.4 %collective-permute-done.4.refs_2_ = f32[2,128,128]{2,1,0:T(8,128)S(1)} collective-permute-done((f32[2,128,128]{2,1,0:T(8,128)S(1)}, f32[2,128,128]{2,1,0:T(8,128)S(1)}, u32[]{:S(2)}, u32[]{:S(2)}) %collective-permute-start.4) | collective-permute-done | bytes 131104 | tf_op jit(solution)/shard_map/ppermute | solution.py:487
  34.6 0.0 collective-permute-done.5.refs_3_
  34.7 22.7 %second.1 = (f32[2,128,128]{2,1,0:T(8,128)S(1)}, f32[2,128,128]{2,1,0:T(8,128)S(1)}, f32[2,128,128]{2,1,0:T(8,128)S(1)}, f32[2,128,128]{2,1,0:T(8,128)S(1)}, f32...) custom-call(f32[2,128,128]{2,1,0:T(8,128)S(1)} %get-tuple-element.47.refs_0_, ...), custom_call_target="tpu_custom_call" | custom-call | tf_op jit(solution)/shard_map/second/pallas_call | solution.py:578
  57.3 0.1 collective-permute-start.6
  57.4 4.8 %collective-permute-start.7 = (f32[2,128,128]{2,1,0:T(8,128)S(1)}, f32[2,128,128]{2,1,0:T(8,128)S(1)}, u32[]{:S(2)}, u32[]{:S(2)}) collective-permute-start(f32[2,128,128]{2,1,0:T(8,128)S(1)} %get-tuple-element.58), channel_id=1, source_target_pairs={{1,0},{2,1},{3,2},{4,3},{5,4},{6,5},{7,6},{8,7},{9,8},{10,9},{11,1... | collective-permute-start | bytes 393224 | tf_op jit(solution)/shard_map/ppermute | solution.py:487
  62.3 3.1 %collective-permute-done.6.refs_2_ = f32[2,128,128]{2,1,0:T(8,128)S(1)} collective-permute-done((f32[2,128,128]{2,1,0:T(8,128)S(1)}, f32[2,128,128]{2,1,0:T(8,128)S(1)}, u32[]{:S(2)}, u32[]{:S(2)}) %collective-permute-start.6) | collective-permute-done | bytes 131104 | tf_op jit(solution)/shard_map/ppermute | solution.py:487
  65.4 0.0 collective-permute-done.7.refs_3_
  65.4 5.9 %third.1 = (f32[3,2,256]{2,1,0:T(2,128)S(1)}, f32[3,2,128]{2,1,0:T(2,128)S(1)}, f32[3,2,128]{2,1,0:T(2,128)S(1)}) custom-call(f32[2,128,128]{2,1,0:T(8,128)S(1)} %get-tuple-element.55.refs_0_, f32[2,128,128]{2,1,0:T(8,128)S(1)} %get-tuple-element.56.refs_1_, f32[2,128,128]{2,1,0:T(8,128)S(1)} %collective-permute-done.6.refs_2_, ...), custom_call_target="tpu_custom_call" | custom-call | tf_op jit(solution)/shard_map/third/pallas_call | solution.py:604
  71.2 0.1 collective-permute-start.8
  71.3 5.2 %collective-permute-start.9 = (f32[3,2,128]{2,1,0:T(2,128)S(1)}, f32[3,2,128]{2,1,0:T(2,128)S(1)}, u32[]{:S(2)}, u32[]{:S(2)}) collective-permute-start(f32[3,2,128]{2,1,0:T(2,128)S(1)} %get-tuple-element.69), channel_id=1, source_target_pairs={{1,0},{2,1},{3,2},{4,3},{5,4},{6,5},{7,6},{8,7},{9,8},{10,9},{11,1... | collective-permute-start | bytes 9224 | tf_op jit(solution)/shard_map/ppermute | solution.py:487
  77.2 0.3 collective-permute-done.8.rlo_ref
  77.4 0.0 collective-permute-done.9.rup_ref
  77.4 0.0 copy-done.5
  77.4 0.0 copy-done.6
  77.4 0.0 copy-done.7
  77.5 0.1 partial.1
  77.6 21.1 %all_to_all.5 = f32[128,1,128]{2,1,0:T(1,128)S(1)} all-to-all(f32[128,1,128]{2,1,0:T(1,128)S(1)} %bitcast.18), channel_id=1, replica_groups=mesh['image'=8,'space'=16] {'image','space'}, dimensions={0} | all-to-all | bytes 131072 | tf_op jit(solution)/shard_map/all_to_all | solution.py:632
  98.7 1.1 %final.1 = (f32[3,2,256]{2,1,0:T(2,128)}, f32[3,2,256]{2,1,0:T(2,128)}, f32[3,2,256]{2,1,0:T(2,128)}, f32[2]{0:T(128)}) custom-call(f32[128,128]{1,0:T(8,128)S(1)} %bitcast.17, f32[3,2,256]{2,1,0:T(2,128)S(1)} %get-tuple-element.73.force_ref, f32[3,2,256]{2,1,0:T(2,128)S(1)} %copy.26.refs_0_.pos_ref, f32[3,256]{1,0:T(4,128)S(1)} %collective-permute-done.2.refs_3_.before_ref, ...), custom_call_target="tpu_custom_call" | custom-call | tf_op jit(solution)/shard_map/final/pallas_call | solution.py:635
  (11 shorter events, 0.0 us)
Async XLA Ops:
  1.3 21.9 %collective-permute-start = (f32[3,2,128]{2,0,1:T(4,128)S(1)}, f32[3,2,128]{2,0,1:T(4,128)S(1)}, u32[]{:S(2)}, u32[]{:S(2)}) collective-permute-start(f32[3,2,128]{2,0,1:T(4,128)S(1)} %get-tuple-element.81), channel_id=1, source_target_pairs={{0,1},{1,2},{2,3},{3,4},{4,5},{5,6},{6,7},{7,8},{8,9},{9,10},{10,1... | collective-permute-start | bytes 9224 | tf_op jit(solution)/shard_map/ppermute | solution.py:487
  3.8 19.4 %collective-permute-start.1 = (f32[3,2,128]{2,0,1:T(4,128)S(1)}, f32[3,2,128]{2,0,1:T(4,128)S(1)}, u32[]{:S(2)}, u32[]{:S(2)}) collective-permute-start(f32[3,2,128]{2,0,1:T(4,128)S(1)} %get-tuple-element.80), channel_id=1, source_target_pairs={{1,0},{2,1},{3,2},{4,3},{5,4},{6,5},{7,6},{8,7},{9,8},{10,9},{11,1... | collective-permute-start | bytes 9224 | tf_op jit(solution)/shard_map/ppermute | solution.py:487
  8.4 14.8 %collective-permute-start.2 = (f32[3,256]{1,0:T(4,128)S(1)}, f32[3,256]{1,0:T(4,128)S(1)}, u32[]{:S(2)}, u32[]{:S(2)}) collective-permute-start(f32[3,256]{1,0:T(4,128)S(1)} %get-tuple-element.79), channel_id=1, source_target_pairs={{0,16},{16,32},{32,48},{48,64},{64,80},{80,96},{96,112},{1,17},{17... | collective-permute-start | bytes 9224 | tf_op jit(solution)/shard_map/ppermute | solution.py:521
  12.4 10.9 %collective-permute-start.3 = (f32[3,256]{1,0:T(4,128)S(1)}, f32[3,256]{1,0:T(4,128)S(1)}, u32[]{:S(2)}, u32[]{:S(2)}) collective-permute-start(f32[3,256]{1,0:T(4,128)S(1)} %get-tuple-element.78), channel_id=1, source_target_pairs={{16,0},{32,16},{48,32},{64,48},{80,64},{96,80},{112,96},{17,1},{33... | collective-permute-start | bytes 9224 | tf_op jit(solution)/shard_map/ppermute | solution.py:522
  14.3 0.9 copy-start
  15.3 0.9 copy-start.1
  16.2 0.8 copy-start.2
  16.9 0.8 copy-start.3
  17.7 0.8 copy-start.4
  18.5 0.7 copy-start.8
  19.1 0.7 copy-start.9
  19.8 0.7 copy-start.10
  20.5 0.7 copy-start.11
  21.2 0.7 copy-start.12
  27.4 7.2 %collective-permute-start.4 = (f32[2,128,128]{2,1,0:T(8,128)S(1)}, f32[2,128,128]{2,1,0:T(8,128)S(1)}, u32[]{:S(2)}, u32[]{:S(2)}) collective-permute-start(f32[2,128,128]{2,1,0:T(8,128)S(1)} %get-tuple-element.48.refs_1_), channel_id=1, source_target_pairs={{0,1},{1,2},{2,3},{3,4},{4,5},{5,6},{6,7},{7,8},{8,9},{9,10},{10,1... | collective-permute-start | bytes 393224 | tf_op jit(solution)/shard_map/ppermute | solution.py:487
  27.5 7.1 %collective-permute-start.5 = (f32[2,128,128]{2,1,0:T(8,128)S(1)}, f32[2,128,128]{2,1,0:T(8,128)S(1)}, u32[]{:S(2)}, u32[]{:S(2)}) collective-permute-start(f32[2,128,128]{2,1,0:T(8,128)S(1)} %get-tuple-element.47.refs_0_), channel_id=1, source_target_pairs={{1,0},{2,1},{3,2},{4,3},{5,4},{6,5},{7,6},{8,7},{9,8},{10,9},{11,1... | collective-permute-start | bytes 393224 | tf_op jit(solution)/shard_map/ppermute | solution.py:487
  57.3 8.0 %collective-permute-start.6 = (f32[2,128,128]{2,1,0:T(8,128)S(1)}, f32[2,128,128]{2,1,0:T(8,128)S(1)}, u32[]{:S(2)}, u32[]{:S(2)}) collective-permute-start(f32[2,128,128]{2,1,0:T(8,128)S(1)} %get-tuple-element.57), channel_id=1, source_target_pairs={{0,1},{1,2},{2,3},{3,4},{4,5},{5,6},{6,7},{7,8},{8,9},{9,10},{10,1... | collective-permute-start | bytes 393224 | tf_op jit(solution)/shard_map/ppermute | solution.py:487
  57.4 8.0 %collective-permute-start.7 = (f32[2,128,128]{2,1,0:T(8,128)S(1)}, f32[2,128,128]{2,1,0:T(8,128)S(1)}, u32[]{:S(2)}, u32[]{:S(2)}) collective-permute-start(f32[2,128,128]{2,1,0:T(8,128)S(1)} %get-tuple-element.58), channel_id=1, source_target_pairs={{1,0},{2,1},{3,2},{4,3},{5,4},{6,5},{7,6},{8,7},{9,8},{10,9},{11,1... | collective-permute-start | bytes 393224 | tf_op jit(solution)/shard_map/ppermute | solution.py:487
  65.4 12.1 %copy-start.5 = (f32[2,3,256]{2,0,1:T(2,128)S(1)}, f32[2,3,256]{2,0,1:T(2,128)}, u32[]{:S(2)}) copy-start(f32[2,3,256]{2,0,1:T(2,128)} %param.16) | copy-start | bytes 18436
  65.4 12.1 %copy-start.6 = (f32[3,256]{1,0:T(4,128)S(1)}, f32[3,256]{1,0:T(4,128)}, u32[]{:S(2)}) copy-start(f32[3,256]{1,0:T(4,128)} %start_ref.3) | copy-start | bytes 9220
  65.4 12.1 %copy-start.7 = (f32[3,256]{1,0:T(4,128)S(1)}, f32[3,256]{1,0:T(4,128)}, u32[]{:S(2)}) copy-start(f32[3,256]{1,0:T(4,128)} %end_ref.3) | copy-start | bytes 9220
  71.2 6.2 %collective-permute-start.8 = (f32[3,2,128]{2,1,0:T(2,128)S(1)}, f32[3,2,128]{2,1,0:T(2,128)S(1)}, u32[]{:S(2)}, u32[]{:S(2)}) collective-permute-start(f32[3,2,128]{2,1,0:T(2,128)S(1)} %get-tuple-element.68), channel_id=1, source_target_pairs={{0,1},{1,2},{2,3},{3,4},{4,5},{5,6},{6,7},{7,8},{8,9},{9,10},{10,1... | collective-permute-start | bytes 9224 | tf_op jit(solution)/shard_map/ppermute | solution.py:487
  71.3 6.1 %collective-permute-start.9 = (f32[3,2,128]{2,1,0:T(2,128)S(1)}, f32[3,2,128]{2,1,0:T(2,128)S(1)}, u32[]{:S(2)}, u32[]{:S(2)}) collective-permute-start(f32[3,2,128]{2,1,0:T(2,128)S(1)} %get-tuple-element.69), channel_id=1, source_target_pairs={{1,0},{2,1},{3,2},{4,3},{5,4},{6,5},{7,6},{8,7},{9,8},{10,9},{11,1... | collective-permute-start | bytes 9224 | tf_op jit(solution)/shard_map/ppermute | solution.py:487

commit v4 on v3

--- a/solution.py
+++ b/solution.py
@@ -12,7 +12,7 @@
 bf16 = jnp.bfloat16
 RT3 = math.sqrt(3.0)
 NL = 9
-BIG_VMEM = 24 << 20
+BIG_VMEM = 16 << 20
 SMALL_VMEM = 4 << 20
 
 
@@ -134,31 +134,40 @@
         m_ref[l] = m_ref[l] * (d1 if l < 4 else d2)
 
 
-def prep_kernel(*refs):
-    n = 10
-    hbm, outs, bufs, sems = refs[:n], refs[n : n + 13], refs[n + 13 : -1], refs[-1]
-    (
-        idx_out, cnt_out, a1_out, b1_out, m1t_out, m1_out, b1t_out, r1_out,
-        a2_out, b2_out, m2t_out, m2_out, r2_out,
-    ) = outs
-    a1, b1, m1, r1, a2, b2, m2, r2 = bufs
-    targets = (idx_out, cnt_out) + bufs
-    copies = [pltpu.make_async_copy(h, t, sems.at[q]) for q, (h, t) in enumerate(zip(hbm, targets))]
-    for c in copies:
-        c.start()
-    for c in copies:
-        c.wait()
-    a1_out[...] = pack_left(a1[...].T)
-    b1_out[...] = pack_left(b1[...].T)
-    m1t_out[...] = pack_left(m1[...].T)
-    m1_out[...] = pack_left(m1[...])
-    b1t_out[...] = pack_left(b1[...])
-    r1_out[...] = jnp.broadcast_to(r1[...], r1_out.shape[::-1]).T
-    a2_out[...] = pack_left(a2[...].T)
-    b2_out[...] = pack_left(b2[...].T)
-    m2t_out[...] = pack_left(m2[...].T)
-    m2_out[...] = pack_left(m2[...])
-    r2_out[...] = jnp.broadcast_to(r2[...], r2_out.shape[::-1]).T
+def joined(parts):
+    rows = []
+    for w in parts:
+        rows.append(jnp.pad(w, ((0, -w.shape[0] % 8), (0, 128 - w.shape[1]))))
+    return jnp.concatenate(rows, axis=0)
+
+
+def prep_kernel(
+    all_ref, idx_ref, cnt_ref, idx_out, cnt_out, a1_out, b1_out, m1t_out, m1_out, b1t_out, r1_out,
+    a2_out, b2_out, m2t_out, m2_out, r2_out,
+):
+    idx_out[...] = idx_ref[...]
+    cnt_out[...] = cnt_ref[...]
+    nb = a1_out.shape[1] // 3
+    rh = a1_out.shape[0]
+    ch = b1_out.shape[0]
+    at = 0
+    for a_out, b_out, bt_out, mt_out, m_out, r_out in (
+        (a1_out, b1_out, b1t_out, m1t_out, m1_out, r1_out),
+        (a2_out, b2_out, None, m2t_out, m2_out, r2_out),
+    ):
+        a_out[...] = pack_left(all_ref[at : at + nb, :].T[:rh])
+        at += nb
+        b = all_ref[at : at + rh, :]
+        b_out[...] = pack_left(b.T)
+        if bt_out is not None:
+            bt_out[...] = pack_left(b)
+        at += rh
+        m = all_ref[at : at + 3 * ch, :]
+        mt_out[...] = pack_left(m.T)
+        m_out[...] = pack_left(m)
+        at += 3 * ch
+        r_out[...] = jnp.broadcast_to(all_ref[at : at + 1, :], r_out.shape[::-1]).T
+        at += 8
 
 
 def energy_rows(read_ref, feat):
@@ -260,10 +269,21 @@
 
 
 @each_image
+def radial_kernel(i, geo_ref, a_ref, b_ref, rad_ref, radl_ref):
+    for k in range(rad_ref.shape[1]):
+        basis, slope = basis_of(geo_ref[i, NL - 1, k : k + 1, :])
+        row = geo_ref[i, NL, k : k + 1, :]
+        hid, ds = silu_parts(dot(a_ref[...], pack_right(basis)))
+        rad_ref[i, k] = dot(b_ref[...], pack_right(hid * row))
+        dsl = ds * row * dot(a_ref[...], pack_right(slope))
+        radl_ref[i, k] = dot(b_ref[...], pack_right(dsl))
+
+
+@each_image
 def second_kernel(
-    i, head_ref, tail_ref, hlo_ref, hup_ref, idx_ref, geo_ref, a_ref, b_ref, mixt_ref, mix_ref,
-    read_ref, dfh_ref, dft_ref, dlo_ref, dup_ref, dy_ref, dlen_ref, en_ref,
-    yb_ref, hf_ref, oh_ref, q_ref, rad_ref, radl_ref, m_ref, dq_ref,
+    i, head_ref, tail_ref, hlo_ref, hup_ref, idx_ref, geo_ref, rad_ref, radl_ref, mixt_ref,
+    mix_ref, read_ref, dfh_ref, dft_ref, dlo_ref, dup_ref, dlen_ref, en_ref, q_ref, m_ref,
+    yb_ref, hf_ref, oh_ref, dq_ref,
 ):
     slots, atoms = idx_ref.shape[1:]
     ghost = hlo_ref.shape[2]
@@ -278,42 +298,60 @@
         oh = one_hot(idx_ref[i, k : k + 1, :], extent)
         oh_ref[:, k * atoms : (k + 1) * atoms] = oh
         got = dot(hf_ref[...], oh)
-        q_ref[k] = got[:ch] + got[ch:]
-        basis, slope = basis_of(geo_ref[i, NL - 1, k : k + 1, :])
-        row = geo_ref[i, NL, k : k + 1, :]
-        hid, ds = silu_parts(dot(a_ref[...], pack_right(basis)))
-        rad_ref[k] = dot(b_ref[...], pack_right(hid * row))
-        dsl = ds * row * dot(a_ref[...], pack_right(slope))
-        radl_ref[k] = dot(b_ref[...], pack_right(dsl))
+        q_ref[i, k] = got[:ch] + got[ch:]
 
     def edge_tile(k, c0, a0):
         cs = pl.ds(c0, 16)
-        return rad_ref[k, cs, a0 : a0 + 128] * q_ref[k, cs, a0 : a0 + 128]
-
-    moments_into(edge_tile, yb_ref, m_ref, ch, slots, atoms)
-    inv = invariants_of(m_ref)
+        return rad_ref[i, k, cs, a0 : a0 + 128] * q_ref[i, k, cs, a0 : a0 + 128]
+
+    m = m_ref.at[i]
+    moments_into(edge_tile, yb_ref, m, ch, slots, atoms)
+    inv = invariants_of(m)
     feat, dpre = silu_parts(dot(mixt_ref[...], pack_right(inv)))
     en_ref[i] = energy_rows(read_ref, feat)
     dinv = dot(mix_ref[...], pack_right(wide(read_ref, atoms) * dpre))
-    moment_grads_into(m_ref, dinv, ch)
-
-    def sink(k, c0, a0, de):
-        cs = slice(c0, c0 + 16)
-        ls = slice(a0, a0 + 128)
-        hi, lo = split(de * rad_ref[k, cs, ls])
-        ks = slice(k * atoms + a0, k * atoms + a0 + 128)
-        dq_ref[cs, ks] = hi
-        dq_ref[ch + c0 : ch + c0 + 16, ks] = lo
-        return de * q_ref[k, cs, ls] * radl_ref[k, cs, ls]
-
+    moment_grads_into(m, dinv, ch)
     for k in range(slots):
-        edge_back(k, edge_tile, sink, yb_ref, m_ref, dy_ref.at[i], dlen_ref.at[i], ch, atoms)
+        for a0 in range(0, atoms, 128):
+            ls = slice(a0, a0 + 128)
+            y = [yb_ref[k, l, :, ls] for l in range(NL - 1)]
+            y = [jnp.concatenate([v, v], axis=0) for v in y]
+            acc = jnp.zeros((8, 128), f32)
+            ks = slice(k * atoms + a0, k * atoms + a0 + 128)
+            for c0 in range(0, ch, 16):
+                cs = slice(c0, c0 + 16)
+                de = m[0, cs, ls]
+                for l in range(1, NL):
+                    de = de + m[l, cs, ls] * y[l - 1]
+                hi, lo = split(de * rad_ref[i, k, cs, ls])
+                dq_ref[cs, ks] = hi
+                dq_ref[ch + c0 : ch + c0 + 16, ks] = lo
+                p = de * q_ref[i, k, cs, ls] * radl_ref[i, k, cs, ls]
+                acc = acc + (p[:8] + p[8:])
+            dlen_ref[i, k : k + 1, ls] = jnp.sum(acc, axis=0, keepdims=True)
     back = dot_nt(dq_ref[...], oh_ref[...])
     back = back[:ch] + back[ch:]
     dlo_ref[i] = back[:, :ghost]
     dfh_ref[i] = back[:, ghost : 2 * ghost]
     dft_ref[i] = back[:, 2 * ghost : 3 * ghost]
     dup_ref[i] = back[:, 3 * ghost :]
+
+
+@each_image
+def angular_kernel(i, rad_ref, q_ref, m_ref, dy_ref):
+    slots, ch, atoms = rad_ref.shape[1:]
+    for k in range(slots):
+        for a0 in range(0, atoms, 128):
+            ls = slice(a0, a0 + 128)
+            acc = [jnp.zeros((8, 128), f32) for _ in range(NL)]
+            for c0 in range(0, ch, 16):
+                cs = slice(c0, c0 + 16)
+                e = rad_ref[i, k, cs, ls] * q_ref[i, k, cs, ls]
+                for l in range(1, NL):
+                    p = e * m_ref[i, l, cs, ls]
+                    acc[l] = acc[l] + (p[:8] + p[8:])
+            for l in range(1, NL):
+                dy_ref[i, l - 1, k : k + 1, ls] = jnp.sum(acc[l], axis=0, keepdims=True)
 
 
 @each_image
@@ -526,7 +564,7 @@
     )
     idx, cnt, a1, b1, m1t, m1, b1t, r1, a2, b2, m2t, m2, r2 = pl.pallas_call(
         prep_kernel,
-        in_specs=[pl.BlockSpec(memory_space=pltpu.HBM)] * 10,
+        in_specs=[VMEM] * 3,
         out_specs=[VMEM] * 13,
         out_shape=[
             jax.ShapeDtypeStruct(neighbours.shape, jnp.int32),
@@ -543,12 +581,10 @@
             half(3 * ch, 3 * ch),
             out(ch, 128),
         ],
-        scratch_shapes=[pltpu.VMEM(w.shape, f32) for w in weights]
-        + [pltpu.SemaphoreType.DMA((10,))],
         compiler_params=small,
         cost_estimate=pl.CostEstimate(flops=4000000, bytes_accessed=4000000, transcendentals=0),
         name="prep",
-    )(neighbours, counts, *weights)
+    )(joined(weights), neighbours, counts)
     geo_n = NL + 1
 
     head, tail, geo, hid, dsl, mom, dpre, en1 = pl.pallas_call(
@@ -575,31 +611,46 @@
 
     hlo, hup = neighbours_of((head, tail), "space")
 
-    dfh, dft, dlo, dup, dy2, dlen2, en2 = pl.pallas_call(
+    rad, radl = pl.pallas_call(
+        functools.partial(radial_kernel, images=images),
+        in_specs=[VMEM] * 3,
+        out_specs=[VMEM] * 2,
+        out_shape=[out(images, slots, ch, atoms)] * 2,
+        compiler_params=small,
+        cost_estimate=pl.CostEstimate(flops=1 << 30, bytes_accessed=1 << 23, transcendentals=1 << 20),
+        name="radial",
+    )(geo, a2, b2)
+    dfh, dft, dlo, dup, dlen2, en2, q, dm = pl.pallas_call(
         functools.partial(second_kernel, images=images),
         in_specs=[VMEM] * 11,
-        out_specs=[VMEM] * 7,
+        out_specs=[VMEM] * 8,
         out_shape=[out(images, ch, ghost)] * 4
         + [
-            out(images, NL - 1, slots, atoms),
             out(images, slots, atoms),
             out(images, 8, 128),
+            out(images, slots, ch, atoms),
+            out(images, NL, ch, atoms),
         ],
         scratch_shapes=[
             pltpu.VMEM((slots, NL - 1, 8, atoms), f32),
             pltpu.VMEM((2 * ch, extent), bf16),
             pltpu.VMEM((extent, slots * atoms), bf16),
-            pltpu.VMEM((slots, ch, atoms), f32),
-            pltpu.VMEM((slots, ch, atoms), f32),
-            pltpu.VMEM((slots, ch, atoms), f32),
-            pltpu.VMEM((NL, ch, atoms), f32),
             pltpu.VMEM((2 * ch, slots * atoms), bf16),
         ],
         compiler_params=params,
         name="second",
-    )(head, tail, hlo, hup, idx, geo, a2, b2, m2t, m2, r2)
+    )(head, tail, hlo, hup, idx, geo, rad, radl, m2t, m2, r2)
 
     rlo, rup = neighbours_of((dlo, dup), "space")
+    dy2 = pl.pallas_call(
+        functools.partial(angular_kernel, images=images),
+        in_specs=[VMEM] * 3,
+        out_specs=VMEM,
+        out_shape=out(images, NL - 1, slots, atoms),
+        compiler_params=small,
+        cost_estimate=pl.CostEstimate(flops=1 << 30, bytes_accessed=1 << 23, transcendentals=0),
+        name="angular",
+    )(rad, q, dm)
 
     own, flo, fup = pl.pallas_call(
         functools.partial(third_kernel, images=images),

time: 101 us -> 94.8 us (0.939)
  waiting for transfers between devices: 5.73 us -> 0.48 us
    pallas_call x1, Pallas kernels: 22.7 us -> 13.3 us  [local(): pl.pallas_call(functools.partial(second_kernel, images=images), in_specs=...]
    pallas_call x1 -> x3, Pallas kernels: 1.36 us -> 10.6 us  [the longest x1 7.05 us: local(): pl.pallas_call(functools.partial(radial_kernel, images=images), in_specs=...]
    ppermute x4, waiting for transfers between devices: 5.72 us -> 0.46 us  [neighbours_of(): lax.ppermute(to_above, axis, up)]
    unnamed x27 -> x18, local copies, waits for them, and re-layouts: 8.19 us -> 7.58 us
  transfers between devices with their start and end apart: 10 -> 10, of which waited for: 3 -> 2; matrix products, arithmetic and copies ran while one was open for 0% -> 6% of each run, Pallas kernels for 1% -> 11%
where the time goes in v4:
time: 94.8 us; the launch traced here: 94.3 us
  Pallas kernels  35.4 us (37%)
  starting transfers between devices  27.7 us (29%)
  blocking collectives  20.8 us (22%)
  local copies, waits for them, and re-layouts  8.26 us (9%)
  between operations  1.63 us (2%)
    all_to_all x1, blocking collectives, local(): lax.all_to_all(send.reshape(rank, 1, 128), ('image', 'space'), split_axis...  20.8 us
    ppermute x4, starting transfers between devices, neighbours_of(): lax.ppermute(to_below, axis, down)  19.3 us
    pallas_call x1, Pallas kernels, local(): pl.pallas_call(functools.partial(second_kernel, images=images), in_specs=...  13.3 us
    unnamed x18, local copies, waits for them, and re-layouts  7.58 us
    pallas_call x1, Pallas kernels, local(): pl.pallas_call(functools.partial(radial_kernel, images=images), in_specs=...  7.05 us
    pallas_call x1, Pallas kernels, local(): pl.pallas_call(functools.partial(third_kernel, images=images), in_specs=[...  5.99 us
    ppermute x1, starting transfers between devices, local(): lax.ppermute(pos[:, images - 1], 'image', [(i, i + 1) for i in range(chai...  4.49 us
    pallas_call x1, Pallas kernels, local(): pl.pallas_call(functools.partial(first_kernel, images=images), in_specs=[...  4.36 us
  transfers between devices with their start and end apart: 10, of which 2 were waited for; matrix products, arithmetic and copies ran while one was open for 6% of the time, Pallas kernels for 11%

profile of v4, /device:TPU:1, one launch (start us, length us, event | category | flops | bytes accessed | tf_op | source)
XLA Modules:
  0.0 94.3 jit_solution(4975381480820145302)
XLA Ops:
  0.6 0.7 copy.33
  1.3 4.5 %collective-permute-start.2 = (f32[3,256]{1,0:T(4,128)S(1)}, f32[3,256]{1,0:T(4,128)S(1)}, u32[]{:S(2)}, u32[]{:S(2)}) collective-permute-start(f32[3,256]{1,0:T(4,128)S(1)} %get-tuple-element.85), channel_id=1, source_target_pairs={{0,16},{16,32},{32,48},{48,64},{64,80},{80,96},{96,112},{1,17},{17... | collective-permute-start | bytes 9224 | tf_op jit(solution)/shard_map/ppermute | solution.py:559
  5.8 1.9 %collective-permute-start.3 = (f32[3,256]{1,0:T(4,128)S(1)}, f32[3,256]{1,0:T(4,128)S(1)}, u32[]{:S(2)}, u32[]{:S(2)}) collective-permute-start(f32[3,256]{1,0:T(4,128)S(1)} %get-tuple-element.84), channel_id=1, source_target_pairs={{16,0},{32,16},{48,32},{64,48},{80,64},{96,80},{112,96},{17,1},{33... | collective-permute-start | bytes 9224 | tf_op jit(solution)/shard_map/ppermute | solution.py:560
  7.8 1.7 %collective-permute-start = (f32[3,2,128]{2,0,1:T(4,128)S(1)}, f32[3,2,128]{2,0,1:T(4,128)S(1)}, u32[]{:S(2)}, u32[]{:S(2)}) collective-permute-start(f32[3,2,128]{2,0,1:T(4,128)S(1)} %get-tuple-element.87), channel_id=1, source_target_pairs={{0,1},{1,2},{2,3},{3,4},{4,5},{5,6},{6,7},{7,8},{8,9},{9,10},{10,1... | collective-permute-start | bytes 9224 | tf_op jit(solution)/shard_map/ppermute | solution.py:525
  9.5 4.7 %collective-permute-start.1 = (f32[3,2,128]{2,0,1:T(4,128)S(1)}, f32[3,2,128]{2,0,1:T(4,128)S(1)}, u32[]{:S(2)}, u32[]{:S(2)}) collective-permute-start(f32[3,2,128]{2,0,1:T(4,128)S(1)} %get-tuple-element.86), channel_id=1, source_target_pairs={{1,0},{2,1},{3,2},{4,3},{5,4},{6,5},{7,6},{8,7},{9,8},{10,9},{11,1... | collective-permute-start | bytes 9224 | tf_op jit(solution)/shard_map/ppermute | solution.py:525
  14.1 0.7 constant_dynamic-update-slice_fusion.7
  14.8 0.8 constant_dynamic-update-slice_fusion.6
  15.6 0.9 constant_dynamic-update-slice_fusion.5
  16.5 0.7 constant_dynamic-update-slice_fusion.4
  17.2 0.7 constant_dynamic-update-slice_fusion.3
  17.9 0.8 constant_dynamic-update-slice_fusion.2
  18.6 0.9 constant_dynamic-update-slice_fusion.1
  19.6 0.7 constant_dynamic-update-slice_fusion.all_ref
  20.2 0.0 copy-start
  20.2 0.8 copy-done
  21.0 0.0 copy-start.4
  21.0 0.7 copy-done.4
  21.7 0.5 prep.1
  22.2 0.0 collective-permute-done
  22.2 0.0 collective-permute-done.1
  22.3 0.0 collective-permute-done.2.refs_3_.before_ref
  22.3 0.0 collective-permute-done.3.refs_4_.after_ref
  22.3 4.4 %first.1 = (f32[2,128,128]{2,1,0:T(8,128)S(1)}, f32[2,128,128]{2,1,0:T(8,128)S(1)}, f32[2,10,16,256]{3,2,1,0:T(8,128)S(1)}, f32[2,16,64,256]{3,2,1,0:T(8,128)S(1...) custom-call(f32[3,2,256]{2,1,0:T(2,128)S(1)} %copy.26.refs_0_.pos_re, ...), custom_call_target="tpu_custom_call" | custom-call | tf_op jit(solution)/shard_map/first/pallas_call | solution.py:590
  26.6 0.1 collective-permute-start.4
  26.7 4.8 %collective-permute-start.5 = (f32[2,128,128]{2,1,0:T(8,128)S(1)}, f32[2,128,128]{2,1,0:T(8,128)S(1)}, u32[]{:S(2)}, u32[]{:S(2)}) collective-permute-start(f32[2,128,128]{2,1,0:T(8,128)S(1)} %get-tuple-element.50.refs_0_), channel_id=1, source_target_pairs={{1,0},{2,1},{3,2},{4,3},{5,4},{6,5},{7,6},{8,7},{9,8},{10,9},{11,1... | collective-permute-start | bytes 393224 | tf_op jit(solution)/shard_map/ppermute | solution.py:525
  31.5 7.1 %radial.1 = (f32[2,16,128,256]{3,2,1,0:T(8,128)S(1)}, f32[2,16,128,256]{3,2,1,0:T(8,128)S(1)}) custom-call(f32[2,10,16,256]{3,2,1,0:T(8,128)S(1)} %get-tuple-element.52.refs_0_.refs_5_, bf16[64,24]{1,0:T(8,128)(2,1)S(1)} %get-tuple-element.53.refs_1_, bf16[128,192]{1,0:T(8,128)(2,1)S(1)} %get-tuple-element.54.refs_2_), custom_call_target="tpu_custom_call" | custom-call | flops 1073741824 | bytes 8388608 | tf_op jit(solution)/shard_map/radial/pallas_call | solution.py:614
  38.6 0.0 collective-permute-done.4.refs_2_
  38.6 0.0 collective-permute-done.5.refs_3_
  38.6 13.3 %second.1 = (f32[2,128,128]{2,1,0:T(8,128)S(1)}, f32[2,128,128]{2,1,0:T(8,128)S(1)}, f32[2,128,128]{2,1,0:T(8,128)S(1)}, f32[2,128,128]{2,1,0:T(8,128)S(1)}, f32...) custom-call(f32[2,128,128]{2,1,0:T(8,128)S(1)} %get-tuple-element.50, ...), custom_call_target="tpu_custom_call" | custom-call | tf_op jit(solution)/shard_map/second/pallas_call | solution.py:623
  51.8 0.1 collective-permute-start.6
  51.9 4.8 %collective-permute-start.7 = (f32[2,128,128]{2,1,0:T(8,128)S(1)}, f32[2,128,128]{2,1,0:T(8,128)S(1)}, u32[]{:S(2)}, u32[]{:S(2)}) collective-permute-start(f32[2,128,128]{2,1,0:T(8,128)S(1)} %get-tuple-element.63), channel_id=1, source_target_pairs={{1,0},{2,1},{3,2},{4,3},{5,4},{6,5},{7,6},{8,7},{9,8},{10,9},{11,1... | collective-permute-start | bytes 393224 | tf_op jit(solution)/shard_map/ppermute | solution.py:525
  56.7 3.0 %angular.1.refs_10_ = f32[2,8,16,256]{3,2,1,0:T(8,128)S(1)} custom-call(f32[2,16,128,256]{3,2,1,0:T(8,128)S(1)} %get-tuple-element.55.refs_6_.refs_0_, f32[2,16,128,256]{3,2,1,0:T(8,128)S(1)} %get-tuple-element.68.refs_1_, f32[2,9,128,256]{3,2,1,0:T(8,128)S(1)} %get-tuple-element.69.refs_2_), custom_call_target="tpu_custom_call" | custom-call | flops 1073741824 | bytes 8388608 | tf_op jit(solution)/shard_map/angular/pallas_call | solution.py:645
  59.7 0.2 collective-permute-done.6.refs_2_
  59.9 0.0 collective-permute-done.7.refs_3_
  59.9 0.0 copy-start.1
  59.9 0.0 copy-start.2
  59.9 0.0 copy-start.3
  59.9 6.0 %third.1 = (f32[3,2,256]{2,1,0:T(2,128)S(1)}, f32[3,2,128]{2,1,0:T(2,128)S(1)}, f32[3,2,128]{2,1,0:T(2,128)S(1)}) custom-call(f32[2,128,128]{2,1,0:T(8,128)S(1)} %get-tuple-element.60.refs_0_, f32[2,128,128]{2,1,0:T(8,128)S(1)} %get-tuple-element.61.refs_1_, f32[2,128,128]{2,1,0:T(8,128)S(1)} %collective-permute-done.6.refs_2_, ...), custom_call_target="tpu_custom_call" | custom-call | tf_op jit(solution)/shard_map/third/pallas_call | solution.py:655
  65.9 0.1 collective-permute-start.8
  66.0 5.1 %collective-permute-start.9 = (f32[3,2,128]{2,1,0:T(2,128)S(1)}, f32[3,2,128]{2,1,0:T(2,128)S(1)}, u32[]{:S(2)}, u32[]{:S(2)}) collective-permute-start(f32[3,2,128]{2,1,0:T(2,128)S(1)} %get-tuple-element.75), channel_id=1, source_target_pairs={{1,0},{2,1},{3,2},{4,3},{5,4},{6,5},{7,6},{8,7},{9,8},{10,9},{11,1... | collective-permute-start | bytes 9224 | tf_op jit(solution)/shard_map/ppermute | solution.py:525
  71.8 0.3 collective-permute-done.8.rlo_ref
  72.0 0.0 collective-permute-done.9.rup_ref
  72.0 0.0 copy-done.1
  72.0 0.0 copy-done.2
  72.0 0.0 copy-done.3
  72.0 0.1 partial.1
  72.2 20.8 %all_to_all.5 = f32[128,1,128]{2,1,0:T(1,128)S(1)} all-to-all(f32[128,1,128]{2,1,0:T(1,128)S(1)} %bitcast.18), channel_id=1, replica_groups=mesh['image'=8,'space'=16] {'image','space'}, dimensions={0} | all-to-all | bytes 131072 | tf_op jit(solution)/shard_map/all_to_all | solution.py:683
  93.0 1.1 %final.1 = (f32[3,2,256]{2,1,0:T(2,128)}, f32[3,2,256]{2,1,0:T(2,128)}, f32[3,2,256]{2,1,0:T(2,128)}, f32[2]{0:T(128)}) custom-call(f32[128,128]{1,0:T(8,128)S(1)} %bitcast.17, f32[3,2,256]{2,1,0:T(2,128)S(1)} %get-tuple-element.79.force_ref, f32[3,2,256]{2,1,0:T(2,128)S(1)} %copy.26.refs_0_.pos_ref, f32[3,256]{1,0:T(4,128)S(1)} %collective-permute-done.2.refs_3_.before_ref, ...), custom_call_target="tpu_custom_call" | custom-call | tf_op jit(solution)/shard_map/final/pallas_call | solution.py:686
  (5 shorter events, 0.0 us)
Async XLA Ops:
  1.3 20.9 %collective-permute-start.2 = (f32[3,256]{1,0:T(4,128)S(1)}, f32[3,256]{1,0:T(4,128)S(1)}, u32[]{:S(2)}, u32[]{:S(2)}) collective-permute-start(f32[3,256]{1,0:T(4,128)S(1)} %get-tuple-element.85), channel_id=1, source_target_pairs={{0,16},{16,32},{32,48},{48,64},{64,80},{80,96},{96,112},{1,17},{17... | collective-permute-start | bytes 9224 | tf_op jit(solution)/shard_map/ppermute | solution.py:559
  5.8 16.4 %collective-permute-start.3 = (f32[3,256]{1,0:T(4,128)S(1)}, f32[3,256]{1,0:T(4,128)S(1)}, u32[]{:S(2)}, u32[]{:S(2)}) collective-permute-start(f32[3,256]{1,0:T(4,128)S(1)} %get-tuple-element.84), channel_id=1, source_target_pairs={{16,0},{32,16},{48,32},{64,48},{80,64},{96,80},{112,96},{17,1},{33... | collective-permute-start | bytes 9224 | tf_op jit(solution)/shard_map/ppermute | solution.py:560
  7.8 14.5 %collective-permute-start = (f32[3,2,128]{2,0,1:T(4,128)S(1)}, f32[3,2,128]{2,0,1:T(4,128)S(1)}, u32[]{:S(2)}, u32[]{:S(2)}) collective-permute-start(f32[3,2,128]{2,0,1:T(4,128)S(1)} %get-tuple-element.87), channel_id=1, source_target_pairs={{0,1},{1,2},{2,3},{3,4},{4,5},{5,6},{6,7},{7,8},{8,9},{9,10},{10,1... | collective-permute-start | bytes 9224 | tf_op jit(solution)/shard_map/ppermute | solution.py:525
  9.5 12.8 %collective-permute-start.1 = (f32[3,2,128]{2,0,1:T(4,128)S(1)}, f32[3,2,128]{2,0,1:T(4,128)S(1)}, u32[]{:S(2)}, u32[]{:S(2)}) collective-permute-start(f32[3,2,128]{2,0,1:T(4,128)S(1)} %get-tuple-element.86), channel_id=1, source_target_pairs={{1,0},{2,1},{3,2},{4,3},{5,4},{6,5},{7,6},{8,7},{9,8},{10,9},{11,1... | collective-permute-start | bytes 9224 | tf_op jit(solution)/shard_map/ppermute | solution.py:525
  20.2 0.8 copy-start
  21.0 0.7 copy-start.4
  26.6 11.9 %collective-permute-start.4 = (f32[2,128,128]{2,1,0:T(8,128)S(1)}, f32[2,128,128]{2,1,0:T(8,128)S(1)}, u32[]{:S(2)}, u32[]{:S(2)}) collective-permute-start(f32[2,128,128]{2,1,0:T(8,128)S(1)} %get-tuple-element.51.refs_1_), channel_id=1, source_target_pairs={{0,1},{1,2},{2,3},{3,4},{4,5},{5,6},{6,7},{7,8},{8,9},{9,10},{10,1... | collective-permute-start | bytes 393224 | tf_op jit(solution)/shard_map/ppermute | solution.py:525
  26.7 11.8 %collective-permute-start.5 = (f32[2,128,128]{2,1,0:T(8,128)S(1)}, f32[2,128,128]{2,1,0:T(8,128)S(1)}, u32[]{:S(2)}, u32[]{:S(2)}) collective-permute-start(f32[2,128,128]{2,1,0:T(8,128)S(1)} %get-tuple-element.50.refs_0_), channel_id=1, source_target_pairs={{1,0},{2,1},{3,2},{4,3},{5,4},{6,5},{7,6},{8,7},{9,8},{10,9},{11,1... | collective-permute-start | bytes 393224 | tf_op jit(solution)/shard_map/ppermute | solution.py:525
  51.8 8.0 %collective-permute-start.6 = (f32[2,128,128]{2,1,0:T(8,128)S(1)}, f32[2,128,128]{2,1,0:T(8,128)S(1)}, u32[]{:S(2)}, u32[]{:S(2)}) collective-permute-start(f32[2,128,128]{2,1,0:T(8,128)S(1)} %get-tuple-element.62), channel_id=1, source_target_pairs={{0,1},{1,2},{2,3},{3,4},{4,5},{5,6},{6,7},{7,8},{8,9},{9,10},{10,1... | collective-permute-start | bytes 393224 | tf_op jit(solution)/shard_map/ppermute | solution.py:525
  51.9 8.0 %collective-permute-start.7 = (f32[2,128,128]{2,1,0:T(8,128)S(1)}, f32[2,128,128]{2,1,0:T(8,128)S(1)}, u32[]{:S(2)}, u32[]{:S(2)}) collective-permute-start(f32[2,128,128]{2,1,0:T(8,128)S(1)} %get-tuple-element.63), channel_id=1, source_target_pairs={{1,0},{2,1},{3,2},{4,3},{5,4},{6,5},{7,6},{8,7},{9,8},{10,9},{11,1... | collective-permute-start | bytes 393224 | tf_op jit(solution)/shard_map/ppermute | solution.py:525
  59.9 12.1 %copy-start.1 = (f32[2,3,256]{2,0,1:T(2,128)S(1)}, f32[2,3,256]{2,0,1:T(2,128)}, u32[]{:S(2)}) copy-start(f32[2,3,256]{2,0,1:T(2,128)} %param.16) | copy-start | bytes 18436
  59.9 12.1 %copy-start.2 = (f32[3,256]{1,0:T(4,128)S(1)}, f32[3,256]{1,0:T(4,128)}, u32[]{:S(2)}) copy-start(f32[3,256]{1,0:T(4,128)} %start_ref.3) | copy-start | bytes 9220
  59.9 12.1 %copy-start.3 = (f32[3,256]{1,0:T(4,128)S(1)}, f32[3,256]{1,0:T(4,128)}, u32[]{:S(2)}) copy-start(f32[3,256]{1,0:T(4,128)} %end_ref.3) | copy-start | bytes 9220
  65.9 6.1 %collective-permute-start.8 = (f32[3,2,128]{2,1,0:T(2,128)S(1)}, f32[3,2,128]{2,1,0:T(2,128)S(1)}, u32[]{:S(2)}, u32[]{:S(2)}) collective-permute-start(f32[3,2,128]{2,1,0:T(2,128)S(1)} %get-tuple-element.74), channel_id=1, source_target_pairs={{0,1},{1,2},{2,3},{3,4},{4,5},{5,6},{6,7},{7,8},{8,9},{9,10},{10,1... | collective-permute-start | bytes 9224 | tf_op jit(solution)/shard_map/ppermute | solution.py:525
  66.0 6.0 %collective-permute-start.9 = (f32[3,2,128]{2,1,0:T(2,128)S(1)}, f32[3,2,128]{2,1,0:T(2,128)S(1)}, u32[]{:S(2)}, u32[]{:S(2)}) collective-permute-start(f32[3,2,128]{2,1,0:T(2,128)S(1)} %get-tuple-element.75), channel_id=1, source_target_pairs={{1,0},{2,1},{3,2},{4,3},{5,4},{6,5},{7,6},{8,7},{9,8},{10,9},{11,1... | collective-permute-start | bytes 9224 | tf_op jit(solution)/shard_map/ppermute | solution.py:525

commit v5 on v4

--- a/solution.py
+++ b/solution.py
@@ -134,40 +134,31 @@
         m_ref[l] = m_ref[l] * (d1 if l < 4 else d2)
 
 
-def joined(parts):
-    rows = []
-    for w in parts:
-        rows.append(jnp.pad(w, ((0, -w.shape[0] % 8), (0, 128 - w.shape[1]))))
-    return jnp.concatenate(rows, axis=0)
-
-
-def prep_kernel(
-    all_ref, idx_ref, cnt_ref, idx_out, cnt_out, a1_out, b1_out, m1t_out, m1_out, b1t_out, r1_out,
-    a2_out, b2_out, m2t_out, m2_out, r2_out,
-):
-    idx_out[...] = idx_ref[...]
-    cnt_out[...] = cnt_ref[...]
-    nb = a1_out.shape[1] // 3
-    rh = a1_out.shape[0]
-    ch = b1_out.shape[0]
-    at = 0
-    for a_out, b_out, bt_out, mt_out, m_out, r_out in (
-        (a1_out, b1_out, b1t_out, m1t_out, m1_out, r1_out),
-        (a2_out, b2_out, None, m2t_out, m2_out, r2_out),
-    ):
-        a_out[...] = pack_left(all_ref[at : at + nb, :].T[:rh])
-        at += nb
-        b = all_ref[at : at + rh, :]
-        b_out[...] = pack_left(b.T)
-        if bt_out is not None:
-            bt_out[...] = pack_left(b)
-        at += rh
-        m = all_ref[at : at + 3 * ch, :]
-        mt_out[...] = pack_left(m.T)
-        m_out[...] = pack_left(m)
-        at += 3 * ch
-        r_out[...] = jnp.broadcast_to(all_ref[at : at + 1, :], r_out.shape[::-1]).T
-        at += 8
+def prep_kernel(*refs):
+    n = 10
+    hbm, outs, bufs, sems = refs[:n], refs[n : n + 13], refs[n + 13 : -1], refs[-1]
+    (
+        idx_out, cnt_out, a1_out, b1_out, m1t_out, m1_out, b1t_out, r1_out,
+        a2_out, b2_out, m2t_out, m2_out, r2_out,
+    ) = outs
+    a1, b1, m1, r1, a2, b2, m2, r2 = bufs
+    targets = (idx_out, cnt_out) + bufs
+    copies = [pltpu.make_async_copy(h, t, sems.at[q]) for q, (h, t) in enumerate(zip(hbm, targets))]
+    for c in copies:
+        c.start()
+    for c in copies:
+        c.wait()
+    a1_out[...] = pack_left(a1[...].T)
+    b1_out[...] = pack_left(b1[...].T)
+    m1t_out[...] = pack_left(m1[...].T)
+    m1_out[...] = pack_left(m1[...])
+    b1t_out[...] = pack_left(b1[...])
+    r1_out[...] = jnp.broadcast_to(r1[...], r1_out.shape[::-1]).T
+    a2_out[...] = pack_left(a2[...].T)
+    b2_out[...] = pack_left(b2[...].T)
+    m2t_out[...] = pack_left(m2[...].T)
+    m2_out[...] = pack_left(m2[...])
+    r2_out[...] = jnp.broadcast_to(r2[...], r2_out.shape[::-1]).T
 
 
 def energy_rows(read_ref, feat):
@@ -564,7 +555,7 @@
     )
     idx, cnt, a1, b1, m1t, m1, b1t, r1, a2, b2, m2t, m2, r2 = pl.pallas_call(
         prep_kernel,
-        in_specs=[VMEM] * 3,
+        in_specs=[pl.BlockSpec(memory_space=pltpu.HBM)] * 10,
         out_specs=[VMEM] * 13,
         out_shape=[
             jax.ShapeDtypeStruct(neighbours.shape, jnp.int32),
@@ -581,10 +572,12 @@
             half(3 * ch, 3 * ch),
             out(ch, 128),
         ],
+        scratch_shapes=[pltpu.VMEM(w.shape, f32) for w in weights]
+        + [pltpu.SemaphoreType.DMA((10,))],
         compiler_params=small,
         cost_estimate=pl.CostEstimate(flops=4000000, bytes_accessed=4000000, transcendentals=0),
         name="prep",
-    )(joined(weights), neighbours, counts)
+    )(*[pltpu.with_memory_space_constraint(w, pltpu.HBM) for w in (neighbours, counts) + weights])
     geo_n = NL + 1
 
     head, tail, geo, hid, dsl, mom, dpre, en1 = pl.pallas_call(

time: 94.8 us -> 88.6 us (0.935)
  local copies, waits for them, and re-layouts: 8.26 us -> 0.73 us
  Pallas kernels: 35.4 us -> 36.7 us
    unnamed x18 -> x7, local copies, waits for them, and re-layouts: 7.58 us -> 0.71 us
    pallas_call x1, Pallas kernels: 0.53 us -> 1.82 us  [local(): pl.pallas_call(prep_kernel, in_specs=[pl.BlockSpec(memory_space=pltpu.HBM...]
    ppermute x1, waiting for transfers between devices: 0.01 us -> 1.1 us  [local(): lax.ppermute(pos[:, 0], 'image', [(i + 1, i) for i in range(chain - 1)])]
  transfers between devices with their start and end apart: 10 -> 10, of which waited for: 2 -> 2; matrix products, arithmetic and copies ran while one was open for 6% -> 0% of each run, Pallas kernels for 11% -> 13%
where the time goes in v5:
time: 88.6 us; the launch traced here: 88.4 us
  Pallas kernels  36.7 us (41%)
  starting transfers between devices  27.7 us (31%)
  blocking collectives  20.2 us (23%)
  between operations  1.65 us (2%)
  waiting for transfers between devices  1.37 us (2%)
    all_to_all x1, blocking collectives, local(): lax.all_to_all(send.reshape(rank, 1, 128), ('image', 'space'), split_axis...  20.2 us
    ppermute x4, starting transfers between devices, neighbours_of(): lax.ppermute(to_below, axis, down)  19.2 us
    pallas_call x1, Pallas kernels, local(): pl.pallas_call(functools.partial(second_kernel, images=images), in_specs=...  13.3 us
    pallas_call x1, Pallas kernels, local(): pl.pallas_call(functools.partial(radial_kernel, images=images), in_specs=...  7.05 us
    pallas_call x1, Pallas kernels, local(): pl.pallas_call(functools.partial(third_kernel, images=images), in_specs=[...  5.99 us
    pallas_call x1, Pallas kernels, local(): pl.pallas_call(functools.partial(first_kernel, images=images), in_specs=[...  4.35 us
    ppermute x1, starting transfers between devices, local(): lax.ppermute(pos[:, images - 1], 'image', [(i, i + 1) for i in range(chai...  3.95 us
    pallas_call x1, Pallas kernels, local(): pl.pallas_call(functools.partial(angular_kernel, images=images), in_specs...  2.98 us
  transfers between devices with their start and end apart: 10, of which 2 were waited for; matrix products, arithmetic and copies ran while one was open for 0% of the time, Pallas kernels for 13%

profile of v5, /device:TPU:1, one launch (start us, length us, event | category | flops | bytes accessed | tf_op | source)
XLA Modules:
  0.0 88.4 jit_solution(12458771940866448396)
XLA Ops:
  0.6 0.7 copy.33
  1.3 2.5 %collective-permute-start = (f32[3,2,128]{2,0,1:T(4,128)S(1)}, f32[3,2,128]{2,0,1:T(4,128)S(1)}, u32[]{:S(2)}, u32[]{:S(2)}) collective-permute-start(f32[3,2,128]{2,0,1:T(4,128)S(1)} %get-tuple-element.87), channel_id=1, source_target_pairs={{0,1},{1,2},{2,3},{3,4},{4,5},{5,6},{6,7},{7,8},{8,9},{9,10},{10,1... | collective-permute-start | bytes 9224 | tf_op jit(solution)/shard_map/ppermute | solution.py:516
  3.8 4.6 %collective-permute-start.1 = (f32[3,2,128]{2,0,1:T(4,128)S(1)}, f32[3,2,128]{2,0,1:T(4,128)S(1)}, u32[]{:S(2)}, u32[]{:S(2)}) collective-permute-start(f32[3,2,128]{2,0,1:T(4,128)S(1)} %get-tuple-element.86), channel_id=1, source_target_pairs={{1,0},{2,1},{3,2},{4,3},{5,4},{6,5},{7,6},{8,7},{9,8},{10,9},{11,1... | collective-permute-start | bytes 9224 | tf_op jit(solution)/shard_map/ppermute | solution.py:516
  8.4 3.9 %collective-permute-start.2 = (f32[3,256]{1,0:T(4,128)S(1)}, f32[3,256]{1,0:T(4,128)S(1)}, u32[]{:S(2)}, u32[]{:S(2)}) collective-permute-start(f32[3,256]{1,0:T(4,128)S(1)} %get-tuple-element.85), channel_id=1, source_target_pairs={{0,16},{16,32},{32,48},{48,64},{64,80},{80,96},{96,112},{1,17},{17... | collective-permute-start | bytes 9224 | tf_op jit(solution)/shard_map/ppermute | solution.py:550
  12.4 1.9 %collective-permute-start.3 = (f32[3,256]{1,0:T(4,128)S(1)}, f32[3,256]{1,0:T(4,128)S(1)}, u32[]{:S(2)}, u32[]{:S(2)}) collective-permute-start(f32[3,256]{1,0:T(4,128)S(1)} %get-tuple-element.84), channel_id=1, source_target_pairs={{16,0},{32,16},{48,32},{64,48},{80,64},{96,80},{112,96},{17,1},{33... | collective-permute-start | bytes 9224 | tf_op jit(solution)/shard_map/ppermute | solution.py:551
  14.3 1.8 %prep.1 = (s32[2,16,256]{2,1,0:T(8,128)S(1)}, s32[2,256]{1,0:T(2,128)S(1)}, bf16[64,24]{1,0:T(8,128)(2,1)S(1)}, bf16[128,192]{1,0:T(8,128)(2,1)S(1)}, bf16[128,1...) custom-call(s32[2,16,256]{2,1,0:T(8,128)} %refs_0_.1, ...), custom_call_target="tpu_custom_call" | custom-call | flops 4000000 | bytes 4000000 | tf_op jit(solution)/shard_map/prep/pallas_call | solution.py:556
  16.2 0.0 collective-permute-done
  16.2 0.0 collective-permute-done.1
  16.2 0.0 collective-permute-done.2.refs_3_.before_ref
  16.2 1.1 %collective-permute-done.3.refs_4_.after_ref = f32[3,256]{1,0:T(4,128)S(1)} collective-permute-done((f32[3,256]{1,0:T(4,128)S(1)}, f32[3,256]{1,0:T(4,128)S(1)}, u32[]{:S(2)}, u32[]{:S(2)}) %collective-permute-start.3) | collective-permute-done | bytes 3104 | tf_op jit(solution)/shard_map/ppermute | solution.py:551
  17.3 4.4 %first.1 = (f32[2,128,128]{2,1,0:T(8,128)S(1)}, f32[2,128,128]{2,1,0:T(8,128)S(1)}, f32[2,10,16,256]{3,2,1,0:T(8,128)S(1)}, f32[2,16,64,256]{3,2,1,0:T(8,128)S(1...) custom-call(f32[3,2,256]{2,1,0:T(2,128)S(1)} %copy.26.refs_0_.pos_re, ...), custom_call_target="tpu_custom_call" | custom-call | tf_op jit(solution)/shard_map/first/pallas_call | solution.py:583
  21.7 0.1 collective-permute-start.4
  21.7 4.8 %collective-permute-start.5 = (f32[2,128,128]{2,1,0:T(8,128)S(1)}, f32[2,128,128]{2,1,0:T(8,128)S(1)}, u32[]{:S(2)}, u32[]{:S(2)}) collective-permute-start(f32[2,128,128]{2,1,0:T(8,128)S(1)} %get-tuple-element.50.refs_0_), channel_id=1, source_target_pairs={{1,0},{2,1},{3,2},{4,3},{5,4},{6,5},{7,6},{8,7},{9,8},{10,9},{11,1... | collective-permute-start | bytes 393224 | tf_op jit(solution)/shard_map/ppermute | solution.py:516
  26.5 7.1 %radial.1 = (f32[2,16,128,256]{3,2,1,0:T(8,128)S(1)}, f32[2,16,128,256]{3,2,1,0:T(8,128)S(1)}) custom-call(f32[2,10,16,256]{3,2,1,0:T(8,128)S(1)} %get-tuple-element.52.refs_0_.refs_5_, bf16[64,24]{1,0:T(8,128)(2,1)S(1)} %get-tuple-element.53.refs_1_, bf16[128,192]{1,0:T(8,128)(2,1)S(1)} %get-tuple-element.54.refs_2_), custom_call_target="tpu_custom_call" | custom-call | flops 1073741824 | bytes 8388608 | tf_op jit(solution)/shard_map/radial/pallas_call | solution.py:607
  33.6 0.0 collective-permute-done.4.refs_2_
  33.6 0.0 collective-permute-done.5.refs_3_
  33.6 13.3 %second.1 = (f32[2,128,128]{2,1,0:T(8,128)S(1)}, f32[2,128,128]{2,1,0:T(8,128)S(1)}, f32[2,128,128]{2,1,0:T(8,128)S(1)}, f32[2,128,128]{2,1,0:T(8,128)S(1)}, f32...) custom-call(f32[2,128,128]{2,1,0:T(8,128)S(1)} %get-tuple-element.50, ...), custom_call_target="tpu_custom_call" | custom-call | tf_op jit(solution)/shard_map/second/pallas_call | solution.py:616
  46.9 0.1 collective-permute-start.6
  46.9 4.8 %collective-permute-start.7 = (f32[2,128,128]{2,1,0:T(8,128)S(1)}, f32[2,128,128]{2,1,0:T(8,128)S(1)}, u32[]{:S(2)}, u32[]{:S(2)}) collective-permute-start(f32[2,128,128]{2,1,0:T(8,128)S(1)} %get-tuple-element.63), channel_id=1, source_target_pairs={{1,0},{2,1},{3,2},{4,3},{5,4},{6,5},{7,6},{8,7},{9,8},{10,9},{11,1... | collective-permute-start | bytes 393224 | tf_op jit(solution)/shard_map/ppermute | solution.py:516
  51.7 3.0 %angular.1.refs_10_ = f32[2,8,16,256]{3,2,1,0:T(8,128)S(1)} custom-call(f32[2,16,128,256]{3,2,1,0:T(8,128)S(1)} %get-tuple-element.55.refs_6_.refs_0_, f32[2,16,128,256]{3,2,1,0:T(8,128)S(1)} %get-tuple-element.68.refs_1_, f32[2,9,128,256]{3,2,1,0:T(8,128)S(1)} %get-tuple-element.69.refs_2_), custom_call_target="tpu_custom_call" | custom-call | flops 1073741824 | bytes 8388608 | tf_op jit(solution)/shard_map/angular/pallas_call | solution.py:638
  54.7 0.0 collective-permute-done.6.refs_2_
  54.7 0.0 collective-permute-done.7.refs_3_
  54.7 0.0 copy-start
  54.7 0.0 copy-start.1
  54.7 0.0 copy-start.2
  54.8 6.0 %third.1 = (f32[3,2,256]{2,1,0:T(2,128)S(1)}, f32[3,2,128]{2,1,0:T(2,128)S(1)}, f32[3,2,128]{2,1,0:T(2,128)S(1)}) custom-call(f32[2,128,128]{2,1,0:T(8,128)S(1)} %get-tuple-element.60.refs_0_, f32[2,128,128]{2,1,0:T(8,128)S(1)} %get-tuple-element.61.refs_1_, f32[2,128,128]{2,1,0:T(8,128)S(1)} %collective-permute-done.6.refs_2_, ...), custom_call_target="tpu_custom_call" | custom-call | tf_op jit(solution)/shard_map/third/pallas_call | solution.py:648
  60.8 0.1 collective-permute-start.8
  60.8 5.0 %collective-permute-start.9 = (f32[3,2,128]{2,1,0:T(2,128)S(1)}, f32[3,2,128]{2,1,0:T(2,128)S(1)}, u32[]{:S(2)}, u32[]{:S(2)}) collective-permute-start(f32[3,2,128]{2,1,0:T(2,128)S(1)} %get-tuple-element.75), channel_id=1, source_target_pairs={{1,0},{2,1},{3,2},{4,3},{5,4},{6,5},{7,6},{8,7},{9,8},{10,9},{11,1... | collective-permute-start | bytes 9224 | tf_op jit(solution)/shard_map/ppermute | solution.py:516
  66.5 0.3 collective-permute-done.8.rlo_ref
  66.8 0.0 collective-permute-done.9.rup_ref
  66.8 0.0 copy-done
  66.8 0.0 copy-done.1
  66.8 0.0 copy-done.2
  66.8 0.1 partial.1
  66.9 20.2 %all_to_all.5 = f32[128,1,128]{2,1,0:T(1,128)S(1)} all-to-all(f32[128,1,128]{2,1,0:T(1,128)S(1)} %bitcast.18), channel_id=1, replica_groups=mesh['image'=8,'space'=16] {'image','space'}, dimensions={0} | all-to-all | bytes 131072 | tf_op jit(solution)/shard_map/all_to_all | solution.py:676
  87.1 1.1 %final.1 = (f32[3,2,256]{2,1,0:T(2,128)}, f32[3,2,256]{2,1,0:T(2,128)}, f32[3,2,256]{2,1,0:T(2,128)}, f32[2]{0:T(128)}) custom-call(f32[128,128]{1,0:T(8,128)S(1)} %bitcast.17, f32[3,2,256]{2,1,0:T(2,128)S(1)} %get-tuple-element.79.force_ref, f32[3,2,256]{2,1,0:T(2,128)S(1)} %copy.26.refs_0_.pos_ref, f32[3,256]{1,0:T(4,128)S(1)} %collective-permute-done.2.refs_3_.before_ref, ...), custom_call_target="tpu_custom_call" | custom-call | tf_op jit(solution)/shard_map/final/pallas_call | solution.py:679
  (5 shorter events, 0.0 us)
Async XLA Ops:
  1.3 14.8 %collective-permute-start = (f32[3,2,128]{2,0,1:T(4,128)S(1)}, f32[3,2,128]{2,0,1:T(4,128)S(1)}, u32[]{:S(2)}, u32[]{:S(2)}) collective-permute-start(f32[3,2,128]{2,0,1:T(4,128)S(1)} %get-tuple-element.87), channel_id=1, source_target_pairs={{0,1},{1,2},{2,3},{3,4},{4,5},{5,6},{6,7},{7,8},{8,9},{9,10},{10,1... | collective-permute-start | bytes 9224 | tf_op jit(solution)/shard_map/ppermute | solution.py:516
  3.8 12.4 %collective-permute-start.1 = (f32[3,2,128]{2,0,1:T(4,128)S(1)}, f32[3,2,128]{2,0,1:T(4,128)S(1)}, u32[]{:S(2)}, u32[]{:S(2)}) collective-permute-start(f32[3,2,128]{2,0,1:T(4,128)S(1)} %get-tuple-element.86), channel_id=1, source_target_pairs={{1,0},{2,1},{3,2},{4,3},{5,4},{6,5},{7,6},{8,7},{9,8},{10,9},{11,1... | collective-permute-start | bytes 9224 | tf_op jit(solution)/shard_map/ppermute | solution.py:516
  8.4 7.8 %collective-permute-start.2 = (f32[3,256]{1,0:T(4,128)S(1)}, f32[3,256]{1,0:T(4,128)S(1)}, u32[]{:S(2)}, u32[]{:S(2)}) collective-permute-start(f32[3,256]{1,0:T(4,128)S(1)} %get-tuple-element.85), channel_id=1, source_target_pairs={{0,16},{16,32},{32,48},{48,64},{64,80},{80,96},{96,112},{1,17},{17... | collective-permute-start | bytes 9224 | tf_op jit(solution)/shard_map/ppermute | solution.py:550
  12.4 4.9 %collective-permute-start.3 = (f32[3,256]{1,0:T(4,128)S(1)}, f32[3,256]{1,0:T(4,128)S(1)}, u32[]{:S(2)}, u32[]{:S(2)}) collective-permute-start(f32[3,256]{1,0:T(4,128)S(1)} %get-tuple-element.84), channel_id=1, source_target_pairs={{16,0},{32,16},{48,32},{64,48},{80,64},{96,80},{112,96},{17,1},{33... | collective-permute-start | bytes 9224 | tf_op jit(solution)/shard_map/ppermute | solution.py:551
  21.7 11.9 %collective-permute-start.4 = (f32[2,128,128]{2,1,0:T(8,128)S(1)}, f32[2,128,128]{2,1,0:T(8,128)S(1)}, u32[]{:S(2)}, u32[]{:S(2)}) collective-permute-start(f32[2,128,128]{2,1,0:T(8,128)S(1)} %get-tuple-element.51.refs_1_), channel_id=1, source_target_pairs={{0,1},{1,2},{2,3},{3,4},{4,5},{5,6},{6,7},{7,8},{8,9},{9,10},{10,1... | collective-permute-start | bytes 393224 | tf_op jit(solution)/shard_map/ppermute | solution.py:516
  21.7 11.8 %collective-permute-start.5 = (f32[2,128,128]{2,1,0:T(8,128)S(1)}, f32[2,128,128]{2,1,0:T(8,128)S(1)}, u32[]{:S(2)}, u32[]{:S(2)}) collective-permute-start(f32[2,128,128]{2,1,0:T(8,128)S(1)} %get-tuple-element.50.refs_0_), channel_id=1, source_target_pairs={{1,0},{2,1},{3,2},{4,3},{5,4},{6,5},{7,6},{8,7},{9,8},{10,9},{11,1... | collective-permute-start | bytes 393224 | tf_op jit(solution)/shard_map/ppermute | solution.py:516
  46.9 7.8 %collective-permute-start.6 = (f32[2,128,128]{2,1,0:T(8,128)S(1)}, f32[2,128,128]{2,1,0:T(8,128)S(1)}, u32[]{:S(2)}, u32[]{:S(2)}) collective-permute-start(f32[2,128,128]{2,1,0:T(8,128)S(1)} %get-tuple-element.62), channel_id=1, source_target_pairs={{0,1},{1,2},{2,3},{3,4},{4,5},{5,6},{6,7},{7,8},{8,9},{9,10},{10,1... | collective-permute-start | bytes 393224 | tf_op jit(solution)/shard_map/ppermute | solution.py:516
  46.9 7.8 %collective-permute-start.7 = (f32[2,128,128]{2,1,0:T(8,128)S(1)}, f32[2,128,128]{2,1,0:T(8,128)S(1)}, u32[]{:S(2)}, u32[]{:S(2)}) collective-permute-start(f32[2,128,128]{2,1,0:T(8,128)S(1)} %get-tuple-element.63), channel_id=1, source_target_pairs={{1,0},{2,1},{3,2},{4,3},{5,4},{6,5},{7,6},{8,7},{9,8},{10,9},{11,1... | collective-permute-start | bytes 393224 | tf_op jit(solution)/shard_map/ppermute | solution.py:516
  54.7 12.0 %copy-start = (f32[2,3,256]{2,0,1:T(2,128)S(1)}, f32[2,3,256]{2,0,1:T(2,128)}, u32[]{:S(2)}) copy-start(f32[2,3,256]{2,0,1:T(2,128)} %param.16) | copy-start | bytes 18436
  54.7 12.0 %copy-start.1 = (f32[3,256]{1,0:T(4,128)S(1)}, f32[3,256]{1,0:T(4,128)}, u32[]{:S(2)}) copy-start(f32[3,256]{1,0:T(4,128)} %start_ref.3) | copy-start | bytes 9220
  54.7 12.0 %copy-start.2 = (f32[3,256]{1,0:T(4,128)S(1)}, f32[3,256]{1,0:T(4,128)}, u32[]{:S(2)}) copy-start(f32[3,256]{1,0:T(4,128)} %end_ref.3) | copy-start | bytes 9220
  60.8 6.0 %collective-permute-start.8 = (f32[3,2,128]{2,1,0:T(2,128)S(1)}, f32[3,2,128]{2,1,0:T(2,128)S(1)}, u32[]{:S(2)}, u32[]{:S(2)}) collective-permute-start(f32[3,2,128]{2,1,0:T(2,128)S(1)} %get-tuple-element.74), channel_id=1, source_target_pairs={{0,1},{1,2},{2,3},{3,4},{4,5},{5,6},{6,7},{7,8},{8,9},{9,10},{10,1... | collective-permute-start | bytes 9224 | tf_op jit(solution)/shard_map/ppermute | solution.py:516
  60.8 5.9 %collective-permute-start.9 = (f32[3,2,128]{2,1,0:T(2,128)S(1)}, f32[3,2,128]{2,1,0:T(2,128)S(1)}, u32[]{:S(2)}, u32[]{:S(2)}) collective-permute-start(f32[3,2,128]{2,1,0:T(2,128)S(1)} %get-tuple-element.75), channel_id=1, source_target_pairs={{1,0},{2,1},{3,2},{4,3},{5,4},{6,5},{7,6},{8,7},{9,8},{10,9},{11,1... | collective-permute-start | bytes 9224 | tf_op jit(solution)/shard_map/ppermute | solution.py:516

commit v6 on v5

--- a/solution.py
+++ b/solution.py
@@ -12,6 +12,9 @@
 bf16 = jnp.bfloat16
 RT3 = math.sqrt(3.0)
 NL = 9
+GROUP_FIRST = 2
+GROUP = 8
+PULL = 4
 BIG_VMEM = 16 << 20
 SMALL_VMEM = 4 << 20
 
@@ -159,6 +162,18 @@
     m2t_out[...] = pack_left(m2[...].T)
     m2_out[...] = pack_left(m2[...])
     r2_out[...] = jnp.broadcast_to(r2[...], r2_out.shape[::-1]).T
+
+
+def lanes(parts):
+    return jnp.concatenate(parts, axis=1)
+
+
+def hidden_of(a_ref, rows, lives):
+    pairs = [basis_of(row) for row in rows]
+    hid, ds = silu_parts(dot(a_ref[...], lanes([pack_right(p[0]) for p in pairs])))
+    back = dot(a_ref[...], lanes([pack_right(p[1]) for p in pairs]))
+    live = lanes(lives)
+    return hid * live, ds * live * back
 
 
 def energy_rows(read_ref, feat):
@@ -218,12 +233,15 @@
     geo_ref[i, NL - 1] = length
     geo_ref[i, NL] = live
     store_yb(yb_ref, angular, slots, atoms)
-    for k in range(slots):
-        basis, slope = basis_of(length[k : k + 1])
-        hid, ds = silu_parts(dot(a_ref[...], pack_right(basis)))
-        row = live[k : k + 1]
-        hid_ref[i, k] = hid * row
-        dsl_ref[i, k] = ds * row * dot(a_ref[...], pack_right(slope))
+    for k0 in range(0, slots, GROUP_FIRST):
+        ks = range(k0, k0 + GROUP_FIRST)
+        hid, dsl = hidden_of(
+            a_ref, [length[k : k + 1] for k in ks], [live[k : k + 1] for k in ks]
+        )
+        for k in ks:
+            at = slice((k - k0) * atoms, (k - k0 + 1) * atoms)
+            hid_ref[i, k] = hid[:, at]
+            dsl_ref[i, k] = dsl[:, at]
 
     def hid_tile(k, c0, a0):
         return hid_ref[i, k, pl.ds(c0, 16), a0 : a0 + 128]
@@ -261,13 +279,20 @@
 
 @each_image
 def radial_kernel(i, geo_ref, a_ref, b_ref, rad_ref, radl_ref):
-    for k in range(rad_ref.shape[1]):
-        basis, slope = basis_of(geo_ref[i, NL - 1, k : k + 1, :])
-        row = geo_ref[i, NL, k : k + 1, :]
-        hid, ds = silu_parts(dot(a_ref[...], pack_right(basis)))
-        rad_ref[i, k] = dot(b_ref[...], pack_right(hid * row))
-        dsl = ds * row * dot(a_ref[...], pack_right(slope))
-        radl_ref[i, k] = dot(b_ref[...], pack_right(dsl))
+    slots, _, atoms = rad_ref.shape[1:]
+    for k0 in range(0, slots, GROUP):
+        ks = range(k0, k0 + GROUP)
+        hid, dsl = hidden_of(
+            a_ref,
+            [geo_ref[i, NL - 1, k : k + 1, :] for k in ks],
+            [geo_ref[i, NL, k : k + 1, :] for k in ks],
+        )
+        rad = dot(b_ref[...], pack_right(hid))
+        radl = dot(b_ref[...], pack_right(dsl))
+        for k in ks:
+            at = slice((k - k0) * atoms, (k - k0 + 1) * atoms)
+            rad_ref[i, k] = rad[:, at]
+            radl_ref[i, k] = radl[:, at]
 
 
 @each_image
@@ -285,11 +310,14 @@
         hf_ref[:ch, n * ghost : (n + 1) * ghost] = hi
         hf_ref[ch:, n * ghost : (n + 1) * ghost] = lo
     store_yb(yb_ref, [geo_ref[i, l] for l in range(NL - 1)], slots, atoms)
-    for k in range(slots):
-        oh = one_hot(idx_ref[i, k : k + 1, :], extent)
-        oh_ref[:, k * atoms : (k + 1) * atoms] = oh
-        got = dot(hf_ref[...], oh)
-        q_ref[i, k] = got[:ch] + got[ch:]
+    for k0 in range(0, slots, PULL):
+        at = slice(k0 * atoms, (k0 + PULL) * atoms)
+        for k in range(k0, k0 + PULL):
+            oh_ref[:, k * atoms : (k + 1) * atoms] = one_hot(idx_ref[i, k : k + 1, :], extent)
+        got = dot(hf_ref[...], oh_ref[:, at])
+        got = got[:ch] + got[ch:]
+        for k in range(k0, k0 + PULL):
+            q_ref[i, k] = got[:, (k - k0) * atoms : (k - k0 + 1) * atoms]
 
     def edge_tile(k, c0, a0):
         cs = pl.ds(c0, 16)

time: 88.6 us -> 85.3 us (0.963)
  Pallas kernels: 36.7 us -> 32.7 us
    pallas_call x1, Pallas kernels: 7.05 us -> 3.01 us  [local(): pl.pallas_call(functools.partial(radial_kernel, images=images), in_specs=...]
  transfers between devices with their start and end apart: 10 -> 10, of which waited for: 2 -> 4; matrix products, arithmetic and copies ran while one was open for 0% -> 0% of each run, Pallas kernels for 13% -> 9%
where the time goes in v6:
time: 85.3 us; the launch traced here: 85 us
  Pallas kernels  32.7 us (38%)
  starting transfers between devices  28.1 us (33%)
  blocking collectives  20.2 us (24%)
  waiting for transfers between devices  1.67 us (2%)
  between operations  1.61 us (2%)
    all_to_all x1, blocking collectives, local(): lax.all_to_all(send.reshape(rank, 1, 128), ('image', 'space'), split_axis...  20.2 us
    ppermute x4, starting transfers between devices, neighbours_of(): lax.ppermute(to_below, axis, down)  19.6 us
    pallas_call x1, Pallas kernels, local(): pl.pallas_call(functools.partial(second_kernel, images=images), in_specs=...  13.2 us
    pallas_call x1, Pallas kernels, local(): pl.pallas_call(functools.partial(third_kernel, images=images), in_specs=[...  5.98 us
    pallas_call x1, Pallas kernels, local(): pl.pallas_call(functools.partial(first_kernel, images=images), in_specs=[...  4.4 us
    ppermute x1, starting transfers between devices, local(): lax.ppermute(pos[:, images - 1], 'image', [(i, i + 1) for i in range(chai...  3.95 us
    pallas_call x1, Pallas kernels, local(): pl.pallas_call(functools.partial(radial_kernel, images=images), in_specs=...  3.01 us
    pallas_call x1, Pallas kernels, local(): pl.pallas_call(functools.partial(angular_kernel, images=images), in_specs...  2.98 us
  transfers between devices with their start and end apart: 10, of which 4 were waited for; matrix products, arithmetic and copies ran while one was open for 0% of the time, Pallas kernels for 9%

profile of v6, /device:TPU:1, one launch (start us, length us, event | category | flops | bytes accessed | tf_op | source)
XLA Modules:
  0.0 85.0 jit_solution(4920602108903623827)
XLA Ops:
  0.6 0.7 copy.33
  1.3 2.5 %collective-permute-start = (f32[3,2,128]{2,0,1:T(4,128)S(1)}, f32[3,2,128]{2,0,1:T(4,128)S(1)}, u32[]{:S(2)}, u32[]{:S(2)}) collective-permute-start(f32[3,2,128]{2,0,1:T(4,128)S(1)} %get-tuple-element.87), channel_id=1, source_target_pairs={{0,1},{1,2},{2,3},{3,4},{4,5},{5,6},{6,7},{7,8},{8,9},{9,10},{10,1... | collective-permute-start | bytes 9224 | tf_op jit(solution)/shard_map/ppermute | solution.py:544
  3.8 4.6 %collective-permute-start.1 = (f32[3,2,128]{2,0,1:T(4,128)S(1)}, f32[3,2,128]{2,0,1:T(4,128)S(1)}, u32[]{:S(2)}, u32[]{:S(2)}) collective-permute-start(f32[3,2,128]{2,0,1:T(4,128)S(1)} %get-tuple-element.86), channel_id=1, source_target_pairs={{1,0},{2,1},{3,2},{4,3},{5,4},{6,5},{7,6},{8,7},{9,8},{10,9},{11,1... | collective-permute-start | bytes 9224 | tf_op jit(solution)/shard_map/ppermute | solution.py:544
  8.4 3.9 %collective-permute-start.2 = (f32[3,256]{1,0:T(4,128)S(1)}, f32[3,256]{1,0:T(4,128)S(1)}, u32[]{:S(2)}, u32[]{:S(2)}) collective-permute-start(f32[3,256]{1,0:T(4,128)S(1)} %get-tuple-element.85), channel_id=1, source_target_pairs={{0,16},{16,32},{32,48},{48,64},{64,80},{80,96},{96,112},{1,17},{17... | collective-permute-start | bytes 9224 | tf_op jit(solution)/shard_map/ppermute | solution.py:578
  12.4 1.9 %collective-permute-start.3 = (f32[3,256]{1,0:T(4,128)S(1)}, f32[3,256]{1,0:T(4,128)S(1)}, u32[]{:S(2)}, u32[]{:S(2)}) collective-permute-start(f32[3,256]{1,0:T(4,128)S(1)} %get-tuple-element.84), channel_id=1, source_target_pairs={{16,0},{32,16},{48,32},{64,48},{80,64},{96,80},{112,96},{17,1},{33... | collective-permute-start | bytes 9224 | tf_op jit(solution)/shard_map/ppermute | solution.py:579
  14.3 1.8 %prep.1 = (s32[2,16,256]{2,1,0:T(8,128)S(1)}, s32[2,256]{1,0:T(2,128)S(1)}, bf16[64,24]{1,0:T(8,128)(2,1)S(1)}, bf16[128,192]{1,0:T(8,128)(2,1)S(1)}, bf16[128,1...) custom-call(s32[2,16,256]{2,1,0:T(8,128)} %refs_0_.1, ...), custom_call_target="tpu_custom_call" | custom-call | flops 4000000 | bytes 4000000 | tf_op jit(solution)/shard_map/prep/pallas_call | solution.py:584
  16.2 0.0 collective-permute-done
  16.2 0.0 collective-permute-done.1
  16.2 0.0 collective-permute-done.2.refs_3_.before_ref
  16.2 1.1 %collective-permute-done.3.refs_4_.after_ref = f32[3,256]{1,0:T(4,128)S(1)} collective-permute-done((f32[3,256]{1,0:T(4,128)S(1)}, f32[3,256]{1,0:T(4,128)S(1)}, u32[]{:S(2)}, u32[]{:S(2)}) %collective-permute-start.3) | collective-permute-done | bytes 3104 | tf_op jit(solution)/shard_map/ppermute | solution.py:579
  17.3 4.4 %first.1 = (f32[2,128,128]{2,1,0:T(8,128)S(1)}, f32[2,128,128]{2,1,0:T(8,128)S(1)}, f32[2,10,16,256]{3,2,1,0:T(8,128)S(1)}, f32[2,16,64,256]{3,2,1,0:T(8,128)S(1...) custom-call(f32[3,2,256]{2,1,0:T(2,128)S(1)} %copy.26.refs_0_.pos_re, ...), custom_call_target="tpu_custom_call" | custom-call | tf_op jit(solution)/shard_map/first/pallas_call | solution.py:611
  21.7 0.1 collective-permute-start.4
  21.8 4.8 %collective-permute-start.5 = (f32[2,128,128]{2,1,0:T(8,128)S(1)}, f32[2,128,128]{2,1,0:T(8,128)S(1)}, u32[]{:S(2)}, u32[]{:S(2)}) collective-permute-start(f32[2,128,128]{2,1,0:T(8,128)S(1)} %get-tuple-element.50.refs_0_), channel_id=1, source_target_pairs={{1,0},{2,1},{3,2},{4,3},{5,4},{6,5},{7,6},{8,7},{9,8},{10,9},{11,1... | collective-permute-start | bytes 393224 | tf_op jit(solution)/shard_map/ppermute | solution.py:544
  26.6 3.0 %radial.1 = (f32[2,16,128,256]{3,2,1,0:T(8,128)S(1)}, f32[2,16,128,256]{3,2,1,0:T(8,128)S(1)}) custom-call(f32[2,10,16,256]{3,2,1,0:T(8,128)S(1)} %get-tuple-element.52.refs_0_.refs_5_, bf16[64,24]{1,0:T(8,128)(2,1)S(1)} %get-tuple-element.53.refs_1_, bf16[128,192]{1,0:T(8,128)(2,1)S(1)} %get-tuple-element.54.refs_2_), custom_call_target="tpu_custom_call" | custom-call | flops 1073741824 | bytes 8388608 | tf_op jit(solution)/shard_map/radial/pallas_call | solution.py:635
  29.6 0.0 collective-permute-done.4.refs_2_
  29.6 0.0 collective-permute-done.5.refs_3_
  29.6 13.2 %second.1 = (f32[2,128,128]{2,1,0:T(8,128)S(1)}, f32[2,128,128]{2,1,0:T(8,128)S(1)}, f32[2,128,128]{2,1,0:T(8,128)S(1)}, f32[2,128,128]{2,1,0:T(8,128)S(1)}, f32...) custom-call(f32[2,128,128]{2,1,0:T(8,128)S(1)} %get-tuple-element.50, ...), custom_call_target="tpu_custom_call" | custom-call | tf_op jit(solution)/shard_map/second/pallas_call | solution.py:644
  42.8 0.1 collective-permute-start.6
  42.9 4.8 %collective-permute-start.7 = (f32[2,128,128]{2,1,0:T(8,128)S(1)}, f32[2,128,128]{2,1,0:T(8,128)S(1)}, u32[]{:S(2)}, u32[]{:S(2)}) collective-permute-start(f32[2,128,128]{2,1,0:T(8,128)S(1)} %get-tuple-element.63), channel_id=1, source_target_pairs={{1,0},{2,1},{3,2},{4,3},{5,4},{6,5},{7,6},{8,7},{9,8},{10,9},{11,1... | collective-permute-start | bytes 393224 | tf_op jit(solution)/shard_map/ppermute | solution.py:544
  47.7 3.0 %angular.1.refs_10_ = f32[2,8,16,256]{3,2,1,0:T(8,128)S(1)} custom-call(f32[2,16,128,256]{3,2,1,0:T(8,128)S(1)} %get-tuple-element.55.refs_6_.refs_0_, f32[2,16,128,256]{3,2,1,0:T(8,128)S(1)} %get-tuple-element.68.refs_1_, f32[2,9,128,256]{3,2,1,0:T(8,128)S(1)} %get-tuple-element.69.refs_2_), custom_call_target="tpu_custom_call" | custom-call | flops 1073741824 | bytes 8388608 | tf_op jit(solution)/shard_map/angular/pallas_call | solution.py:666
  50.7 0.1 collective-permute-done.6.refs_2_
  50.8 0.2 collective-permute-done.7.refs_3_
  51.0 0.0 copy-start
  51.0 0.0 copy-start.1
  51.0 0.0 copy-start.2
  51.0 6.0 %third.1 = (f32[3,2,256]{2,1,0:T(2,128)S(1)}, f32[3,2,128]{2,1,0:T(2,128)S(1)}, f32[3,2,128]{2,1,0:T(2,128)S(1)}) custom-call(f32[2,128,128]{2,1,0:T(8,128)S(1)} %get-tuple-element.60.refs_0_, f32[2,128,128]{2,1,0:T(8,128)S(1)} %get-tuple-element.61.refs_1_, f32[2,128,128]{2,1,0:T(8,128)S(1)} %collective-permute-done.6.refs_2_, ...), custom_call_target="tpu_custom_call" | custom-call | tf_op jit(solution)/shard_map/third/pallas_call | solution.py:676
  57.0 0.1 collective-permute-start.8
  57.1 5.4 %collective-permute-start.9 = (f32[3,2,128]{2,1,0:T(2,128)S(1)}, f32[3,2,128]{2,1,0:T(2,128)S(1)}, u32[]{:S(2)}, u32[]{:S(2)}) collective-permute-start(f32[3,2,128]{2,1,0:T(2,128)S(1)} %get-tuple-element.75), channel_id=1, source_target_pairs={{1,0},{2,1},{3,2},{4,3},{5,4},{6,5},{7,6},{8,7},{9,8},{10,9},{11,1... | collective-permute-start | bytes 9224 | tf_op jit(solution)/shard_map/ppermute | solution.py:544
  63.1 0.3 collective-permute-done.8.rlo_ref
  63.4 0.0 collective-permute-done.9.rup_ref
  63.4 0.0 copy-done
  63.4 0.0 copy-done.1
  63.4 0.0 copy-done.2
  63.4 0.1 partial.1
  63.5 20.2 %all_to_all.5 = f32[128,1,128]{2,1,0:T(1,128)S(1)} all-to-all(f32[128,1,128]{2,1,0:T(1,128)S(1)} %bitcast.18), channel_id=1, replica_groups=mesh['image'=8,'space'=16] {'image','space'}, dimensions={0} | all-to-all | bytes 131072 | tf_op jit(solution)/shard_map/all_to_all | solution.py:704
  83.8 1.1 %final.1 = (f32[3,2,256]{2,1,0:T(2,128)}, f32[3,2,256]{2,1,0:T(2,128)}, f32[3,2,256]{2,1,0:T(2,128)}, f32[2]{0:T(128)}) custom-call(f32[128,128]{1,0:T(8,128)S(1)} %bitcast.17, f32[3,2,256]{2,1,0:T(2,128)S(1)} %get-tuple-element.79.force_ref, f32[3,2,256]{2,1,0:T(2,128)S(1)} %copy.26.refs_0_.pos_ref, f32[3,256]{1,0:T(4,128)S(1)} %collective-permute-done.2.refs_3_.before_ref, ...), custom_call_target="tpu_custom_call" | custom-call | tf_op jit(solution)/shard_map/final/pallas_call | solution.py:707
  (5 shorter events, 0.0 us)
Async XLA Ops:
  1.3 14.8 %collective-permute-start = (f32[3,2,128]{2,0,1:T(4,128)S(1)}, f32[3,2,128]{2,0,1:T(4,128)S(1)}, u32[]{:S(2)}, u32[]{:S(2)}) collective-permute-start(f32[3,2,128]{2,0,1:T(4,128)S(1)} %get-tuple-element.87), channel_id=1, source_target_pairs={{0,1},{1,2},{2,3},{3,4},{4,5},{5,6},{6,7},{7,8},{8,9},{9,10},{10,1... | collective-permute-start | bytes 9224 | tf_op jit(solution)/shard_map/ppermute | solution.py:544
  3.8 12.4 %collective-permute-start.1 = (f32[3,2,128]{2,0,1:T(4,128)S(1)}, f32[3,2,128]{2,0,1:T(4,128)S(1)}, u32[]{:S(2)}, u32[]{:S(2)}) collective-permute-start(f32[3,2,128]{2,0,1:T(4,128)S(1)} %get-tuple-element.86), channel_id=1, source_target_pairs={{1,0},{2,1},{3,2},{4,3},{5,4},{6,5},{7,6},{8,7},{9,8},{10,9},{11,1... | collective-permute-start | bytes 9224 | tf_op jit(solution)/shard_map/ppermute | solution.py:544
  8.4 7.8 %collective-permute-start.2 = (f32[3,256]{1,0:T(4,128)S(1)}, f32[3,256]{1,0:T(4,128)S(1)}, u32[]{:S(2)}, u32[]{:S(2)}) collective-permute-start(f32[3,256]{1,0:T(4,128)S(1)} %get-tuple-element.85), channel_id=1, source_target_pairs={{0,16},{16,32},{32,48},{48,64},{64,80},{80,96},{96,112},{1,17},{17... | collective-permute-start | bytes 9224 | tf_op jit(solution)/shard_map/ppermute | solution.py:578
  12.4 4.9 %collective-permute-start.3 = (f32[3,256]{1,0:T(4,128)S(1)}, f32[3,256]{1,0:T(4,128)S(1)}, u32[]{:S(2)}, u32[]{:S(2)}) collective-permute-start(f32[3,256]{1,0:T(4,128)S(1)} %get-tuple-element.84), channel_id=1, source_target_pairs={{16,0},{32,16},{48,32},{64,48},{80,64},{96,80},{112,96},{17,1},{33... | collective-permute-start | bytes 9224 | tf_op jit(solution)/shard_map/ppermute | solution.py:579
  21.7 7.9 %collective-permute-start.4 = (f32[2,128,128]{2,1,0:T(8,128)S(1)}, f32[2,128,128]{2,1,0:T(8,128)S(1)}, u32[]{:S(2)}, u32[]{:S(2)}) collective-permute-start(f32[2,128,128]{2,1,0:T(8,128)S(1)} %get-tuple-element.51.refs_1_), channel_id=1, source_target_pairs={{0,1},{1,2},{2,3},{3,4},{4,5},{5,6},{6,7},{7,8},{8,9},{9,10},{10,1... | collective-permute-start | bytes 393224 | tf_op jit(solution)/shard_map/ppermute | solution.py:544
  21.8 7.8 %collective-permute-start.5 = (f32[2,128,128]{2,1,0:T(8,128)S(1)}, f32[2,128,128]{2,1,0:T(8,128)S(1)}, u32[]{:S(2)}, u32[]{:S(2)}) collective-permute-start(f32[2,128,128]{2,1,0:T(8,128)S(1)} %get-tuple-element.50.refs_0_), channel_id=1, source_target_pairs={{1,0},{2,1},{3,2},{4,3},{5,4},{6,5},{7,6},{8,7},{9,8},{10,9},{11,1... | collective-permute-start | bytes 393224 | tf_op jit(solution)/shard_map/ppermute | solution.py:544
  42.8 8.0 %collective-permute-start.6 = (f32[2,128,128]{2,1,0:T(8,128)S(1)}, f32[2,128,128]{2,1,0:T(8,128)S(1)}, u32[]{:S(2)}, u32[]{:S(2)}) collective-permute-start(f32[2,128,128]{2,1,0:T(8,128)S(1)} %get-tuple-element.62), channel_id=1, source_target_pairs={{0,1},{1,2},{2,3},{3,4},{4,5},{5,6},{6,7},{7,8},{8,9},{9,10},{10,1... | collective-permute-start | bytes 393224 | tf_op jit(solution)/shard_map/ppermute | solution.py:544
  42.9 8.1 %collective-permute-start.7 = (f32[2,128,128]{2,1,0:T(8,128)S(1)}, f32[2,128,128]{2,1,0:T(8,128)S(1)}, u32[]{:S(2)}, u32[]{:S(2)}) collective-permute-start(f32[2,128,128]{2,1,0:T(8,128)S(1)} %get-tuple-element.63), channel_id=1, source_target_pairs={{1,0},{2,1},{3,2},{4,3},{5,4},{6,5},{7,6},{8,7},{9,8},{10,9},{11,1... | collective-permute-start | bytes 393224 | tf_op jit(solution)/shard_map/ppermute | solution.py:544
  51.0 12.4 %copy-start = (f32[2,3,256]{2,0,1:T(2,128)S(1)}, f32[2,3,256]{2,0,1:T(2,128)}, u32[]{:S(2)}) copy-start(f32[2,3,256]{2,0,1:T(2,128)} %param.16) | copy-start | bytes 18436
  51.0 12.4 %copy-start.1 = (f32[3,256]{1,0:T(4,128)S(1)}, f32[3,256]{1,0:T(4,128)}, u32[]{:S(2)}) copy-start(f32[3,256]{1,0:T(4,128)} %start_ref.3) | copy-start | bytes 9220
  51.0 12.4 %copy-start.2 = (f32[3,256]{1,0:T(4,128)S(1)}, f32[3,256]{1,0:T(4,128)}, u32[]{:S(2)}) copy-start(f32[3,256]{1,0:T(4,128)} %end_ref.3) | copy-start | bytes 9220
  57.0 6.4 %collective-permute-start.8 = (f32[3,2,128]{2,1,0:T(2,128)S(1)}, f32[3,2,128]{2,1,0:T(2,128)S(1)}, u32[]{:S(2)}, u32[]{:S(2)}) collective-permute-start(f32[3,2,128]{2,1,0:T(2,128)S(1)} %get-tuple-element.74), channel_id=1, source_target_pairs={{0,1},{1,2},{2,3},{3,4},{4,5},{5,6},{6,7},{7,8},{8,9},{9,10},{10,1... | collective-permute-start | bytes 9224 | tf_op jit(solution)/shard_map/ppermute | solution.py:544
  57.1 6.3 %collective-permute-start.9 = (f32[3,2,128]{2,1,0:T(2,128)S(1)}, f32[3,2,128]{2,1,0:T(2,128)S(1)}, u32[]{:S(2)}, u32[]{:S(2)}) collective-permute-start(f32[3,2,128]{2,1,0:T(2,128)S(1)} %get-tuple-element.75), channel_id=1, source_target_pairs={{1,0},{2,1},{3,2},{4,3},{5,4},{6,5},{7,6},{8,7},{9,8},{10,9},{11,1... | collective-permute-start | bytes 9224 | tf_op jit(solution)/shard_map/ppermute | solution.py:544

commit v7 on v6

--- a/solution.py
+++ b/solution.py
@@ -202,10 +202,11 @@
 @each_image
 def first_kernel(
     i, pos_ref, plo_ref, pup_ref, before_ref, after_ref, idx_ref, cnt_ref, a_ref, b_ref, mixt_ref,
-    read_ref, head_ref, tail_ref, geo_ref, hid_ref, dsl_ref, mom_ref, dpre_ref, en_ref,
-    yb_ref, g_ref,
+    read_ref, head_ref, tail_ref, geo_ref, hid_ref, dsl_ref, mom_ref, dpre_ref, en_ref, ybs_ref,
+    g_ref,
 ):
     slots, atoms = idx_ref.shape[1:]
+    yb_ref = ybs_ref.at[i]
     ghost = plo_ref.shape[2]
     idx = idx_ref[i]
     pos = pick(pos_ref[...], i, 1)
@@ -278,8 +279,12 @@
 
 
 @each_image
-def radial_kernel(i, geo_ref, a_ref, b_ref, rad_ref, radl_ref):
+def radial_kernel(i, idx_ref, geo_ref, a_ref, b_ref, rad_ref, radl_ref, oh_ref):
     slots, _, atoms = rad_ref.shape[1:]
+    for k in range(slots):
+        oh_ref[i, :, k * atoms : (k + 1) * atoms] = one_hot(
+            idx_ref[i, k : k + 1, :], oh_ref.shape[1]
+        )
     for k0 in range(0, slots, GROUP):
         ks = range(k0, k0 + GROUP)
         hid, dsl = hidden_of(
@@ -297,23 +302,21 @@
 
 @each_image
 def second_kernel(
-    i, head_ref, tail_ref, hlo_ref, hup_ref, idx_ref, geo_ref, rad_ref, radl_ref, mixt_ref,
+    i, head_ref, tail_ref, hlo_ref, hup_ref, ybs_ref, ohs_ref, rad_ref, radl_ref, mixt_ref,
     mix_ref, read_ref, dfh_ref, dft_ref, dlo_ref, dup_ref, dlen_ref, en_ref, q_ref, m_ref,
-    yb_ref, hf_ref, oh_ref, dq_ref,
+    hf_ref, dq_ref,
 ):
-    slots, atoms = idx_ref.shape[1:]
+    slots, _, atoms = rad_ref.shape[1:]
     ghost = hlo_ref.shape[2]
     ch = hlo_ref.shape[1]
-    extent = atoms + 2 * ghost
+    yb_ref = ybs_ref.at[i]
+    oh_ref = ohs_ref.at[i]
     for n, ref in enumerate((hlo_ref, head_ref, tail_ref, hup_ref)):
         hi, lo = split(ref[i])
         hf_ref[:ch, n * ghost : (n + 1) * ghost] = hi
         hf_ref[ch:, n * ghost : (n + 1) * ghost] = lo
-    store_yb(yb_ref, [geo_ref[i, l] for l in range(NL - 1)], slots, atoms)
     for k0 in range(0, slots, PULL):
         at = slice(k0 * atoms, (k0 + PULL) * atoms)
-        for k in range(k0, k0 + PULL):
-            oh_ref[:, k * atoms : (k + 1) * atoms] = one_hot(idx_ref[i, k : k + 1, :], extent)
         got = dot(hf_ref[...], oh_ref[:, at])
         got = got[:ch] + got[ch:]
         for k in range(k0, k0 + PULL):
@@ -375,16 +378,15 @@
 
 @each_image
 def third_kernel(
-    i, dfh_ref, dft_ref, rlo_ref, rup_ref, idx_ref, geo_ref, hid_ref, dsl_ref, mom_ref, dpre_ref,
+    i, dfh_ref, dft_ref, rlo_ref, rup_ref, ybs_ref, ohs_ref, geo_ref, hid_ref, dsl_ref, mom_ref, dpre_ref,
     dy2_ref, dlen2_ref, bt_ref, mix_ref, read_ref,
     own_ref, flo_ref, fup_ref,
-    yb_ref, m_ref, dg_ref, dy_ref, dlen_ref, doff_ref,
+    m_ref, dg_ref, dy_ref, dlen_ref, doff_ref,
 ):
-    slots, atoms = idx_ref.shape[1:]
+    slots, rh, atoms = hid_ref.shape[1:]
     ch, ghost = rlo_ref.shape[1:]
-    rh = hid_ref.shape[2]
-    extent = atoms + 2 * ghost
-    store_yb(yb_ref, [geo_ref[i, l] for l in range(NL - 1)], slots, atoms)
+    extent = ohs_ref.shape[1]
+    yb_ref = ybs_ref.at[i]
     cot = jnp.concatenate([dfh_ref[i] + rlo_ref[i], dft_ref[i] + rup_ref[i]], axis=1)
     dpre = (cot + wide(read_ref, atoms)) * dpre_ref[i]
     dinv = dot(mix_ref[...], pack_right(dpre))
@@ -419,7 +421,7 @@
         rows = jnp.concatenate([doff_ref[x, k : k + 1, :] for x in range(3)] + [pad], axis=0)
         hi = rows.astype(bf16).astype(f32)
         both = jnp.concatenate([hi, rows - hi], axis=0).astype(bf16)
-        back = back + dot_nt(both, one_hot(idx_ref[i, k : k + 1, :], extent))
+        back = back + dot_nt(both, ohs_ref[i, :, k * atoms : (k + 1) * atoms])
     force = back[8:11] + back[:3]
     for n in range(own_ref.shape[1]):
 
@@ -608,10 +610,10 @@
     )(*[pltpu.with_memory_space_constraint(w, pltpu.HBM) for w in (neighbours, counts) + weights])
     geo_n = NL + 1
 
-    head, tail, geo, hid, dsl, mom, dpre, en1 = pl.pallas_call(
+    head, tail, geo, hid, dsl, mom, dpre, en1, yb = pl.pallas_call(
         functools.partial(first_kernel, images=images),
         in_specs=[VMEM] * 3 + [ANY] * 2 + [VMEM] * 6,
-        out_specs=[VMEM] * 8,
+        out_specs=[VMEM] * 9,
         out_shape=[
             out(images, ch, ghost),
             out(images, ch, ghost),
@@ -621,26 +623,24 @@
             out(images, NL, ch, atoms),
             out(images, ch, atoms),
             out(images, 8, 128),
+            out(images, slots, NL - 1, 8, atoms),
         ],
-        scratch_shapes=[
-            pltpu.VMEM((slots, NL - 1, 8, atoms), f32),
-            pltpu.VMEM((NL, rh, atoms), f32),
-        ],
+        scratch_shapes=[pltpu.VMEM((NL, rh, atoms), f32)],
         compiler_params=params,
         name="first",
     )(pos, plo, pup, before, after, idx, cnt, a1, b1, m1t, r1)
 
     hlo, hup = neighbours_of((head, tail), "space")
 
-    rad, radl = pl.pallas_call(
+    rad, radl, oh = pl.pallas_call(
         functools.partial(radial_kernel, images=images),
-        in_specs=[VMEM] * 3,
-        out_specs=[VMEM] * 2,
-        out_shape=[out(images, slots, ch, atoms)] * 2,
+        in_specs=[VMEM] * 4,
+        out_specs=[VMEM] * 3,
+        out_shape=[out(images, slots, ch, atoms)] * 2 + [half(images, extent, slots * atoms)],
         compiler_params=small,
         cost_estimate=pl.CostEstimate(flops=1 << 30, bytes_accessed=1 << 23, transcendentals=1 << 20),
         name="radial",
-    )(geo, a2, b2)
+    )(idx, geo, a2, b2)
     dfh, dft, dlo, dup, dlen2, en2, q, dm = pl.pallas_call(
         functools.partial(second_kernel, images=images),
         in_specs=[VMEM] * 11,
@@ -653,14 +653,12 @@
             out(images, NL, ch, atoms),
         ],
         scratch_shapes=[
-            pltpu.VMEM((slots, NL - 1, 8, atoms), f32),
             pltpu.VMEM((2 * ch, extent), bf16),
-            pltpu.VMEM((extent, slots * atoms), bf16),
             pltpu.VMEM((2 * ch, slots * atoms), bf16),
         ],
         compiler_params=params,
         name="second",
-    )(head, tail, hlo, hup, idx, geo, rad, radl, m2t, m2, r2)
+    )(head, tail, hlo, hup, yb, oh, rad, radl, m2t, m2, r2)
 
     rlo, rup = neighbours_of((dlo, dup), "space")
     dy2 = pl.pallas_call(
@@ -675,11 +673,10 @@
 
     own, flo, fup = pl.pallas_call(
         functools.partial(third_kernel, images=images),
-        in_specs=[VMEM] * 15,
+        in_specs=[VMEM] * 16,
         out_specs=[VMEM] * 3,
         out_shape=[out(3, images, atoms), out(3, images, ghost), out(3, images, ghost)],
         scratch_shapes=[
-            pltpu.VMEM((slots, NL - 1, 8, atoms), f32),
             pltpu.VMEM((NL, ch, atoms), f32),
             pltpu.VMEM((NL, rh, atoms), f32),
             pltpu.VMEM((NL - 1, slots, atoms), f32),
@@ -688,7 +685,7 @@
         ],
         compiler_params=params,
         name="third",
-    )(dfh, dft, rlo, rup, idx, geo, hid, dsl, mom, dpre, dy2, dlen2, b1t, m1, r1)
+    )(dfh, dft, rlo, rup, yb, oh, geo, hid, dsl, mom, dpre, dy2, dlen2, b1t, m1, r1)
 
     glo, gup = neighbours_of((flo, fup), "space")
 

time: 85.3 us -> 85.7 us (level)
  Pallas kernels: 32.7 us -> 33.8 us
    pallas_call x1, Pallas kernels: 3.01 us -> 4.38 us  [local(): pl.pallas_call(functools.partial(radial_kernel, images=images), in_specs=...]
  transfers between devices with their start and end apart: 10 -> 10, of which waited for: 4 -> 2; matrix products, arithmetic and copies ran while one was open for 0% -> 0% of each run, Pallas kernels for 9% -> 11%
where the time goes in v7:
time: 85.7 us; the launch traced here: 85.5 us
  Pallas kernels  33.8 us (39%)
  starting transfers between devices  27.7 us (32%)
  blocking collectives  20.2 us (24%)
  between operations  1.65 us (2%)
  waiting for transfers between devices  1.37 us (2%)
    all_to_all x1, blocking collectives, local(): lax.all_to_all(send.reshape(rank, 1, 128), ('image', 'space'), split_axis...  20.2 us
    ppermute x4, starting transfers between devices, neighbours_of(): lax.ppermute(to_below, axis, down)  19.2 us
    pallas_call x1, Pallas kernels, local(): pl.pallas_call(functools.partial(second_kernel, images=images), in_specs=...  13.2 us
    pallas_call x1, Pallas kernels, local(): pl.pallas_call(functools.partial(third_kernel, images=images), in_specs=[...  5.96 us
    pallas_call x1, Pallas kernels, local(): pl.pallas_call(functools.partial(radial_kernel, images=images), in_specs=...  4.38 us
    pallas_call x1, Pallas kernels, local(): pl.pallas_call(functools.partial(first_kernel, images=images), in_specs=[...  4.23 us
    ppermute x1, starting transfers between devices, local(): lax.ppermute(pos[:, images - 1], 'image', [(i, i + 1) for i in range(chai...  3.95 us
    pallas_call x1, Pallas kernels, local(): pl.pallas_call(functools.partial(angular_kernel, images=images), in_specs...  2.98 us
  transfers between devices with their start and end apart: 10, of which 2 were waited for; matrix products, arithmetic and copies ran while one was open for 0% of the time, Pallas kernels for 11%

profile of v7, /device:TPU:1, one launch (start us, length us, event | category | flops | bytes accessed | tf_op | source)
XLA Modules:
  0.0 85.5 jit_solution(13338869636409276969)
XLA Ops:
  0.6 0.7 copy.33
  1.3 2.5 %collective-permute-start = (f32[3,2,128]{2,0,1:T(4,128)S(1)}, f32[3,2,128]{2,0,1:T(4,128)S(1)}, u32[]{:S(2)}, u32[]{:S(2)}) collective-permute-start(f32[3,2,128]{2,0,1:T(4,128)S(1)} %get-tuple-element.91), channel_id=1, source_target_pairs={{0,1},{1,2},{2,3},{3,4},{4,5},{5,6},{6,7},{7,8},{8,9},{9,10},{10,1... | collective-permute-start | bytes 9224 | tf_op jit(solution)/shard_map/ppermute | solution.py:546
  3.8 4.6 %collective-permute-start.1 = (f32[3,2,128]{2,0,1:T(4,128)S(1)}, f32[3,2,128]{2,0,1:T(4,128)S(1)}, u32[]{:S(2)}, u32[]{:S(2)}) collective-permute-start(f32[3,2,128]{2,0,1:T(4,128)S(1)} %get-tuple-element.90), channel_id=1, source_target_pairs={{1,0},{2,1},{3,2},{4,3},{5,4},{6,5},{7,6},{8,7},{9,8},{10,9},{11,1... | collective-permute-start | bytes 9224 | tf_op jit(solution)/shard_map/ppermute | solution.py:546
  8.4 3.9 %collective-permute-start.2 = (f32[3,256]{1,0:T(4,128)S(1)}, f32[3,256]{1,0:T(4,128)S(1)}, u32[]{:S(2)}, u32[]{:S(2)}) collective-permute-start(f32[3,256]{1,0:T(4,128)S(1)} %get-tuple-element.89), channel_id=1, source_target_pairs={{0,16},{16,32},{32,48},{48,64},{64,80},{80,96},{96,112},{1,17},{17... | collective-permute-start | bytes 9224 | tf_op jit(solution)/shard_map/ppermute | solution.py:580
  12.4 1.9 %collective-permute-start.3 = (f32[3,256]{1,0:T(4,128)S(1)}, f32[3,256]{1,0:T(4,128)S(1)}, u32[]{:S(2)}, u32[]{:S(2)}) collective-permute-start(f32[3,256]{1,0:T(4,128)S(1)} %get-tuple-element.88), channel_id=1, source_target_pairs={{16,0},{32,16},{48,32},{64,48},{80,64},{96,80},{112,96},{17,1},{33... | collective-permute-start | bytes 9224 | tf_op jit(solution)/shard_map/ppermute | solution.py:581
  14.3 1.8 %prep.1 = (s32[2,16,256]{2,1,0:T(8,128)S(1)}, s32[2,256]{1,0:T(2,128)S(1)}, bf16[64,24]{1,0:T(8,128)(2,1)S(1)}, bf16[128,192]{1,0:T(8,128)(2,1)S(1)}, bf16[128,1...) custom-call(s32[2,16,256]{2,1,0:T(8,128)} %refs_0_.1, ...), custom_call_target="tpu_custom_call" | custom-call | flops 4000000 | bytes 4000000 | tf_op jit(solution)/shard_map/prep/pallas_call | solution.py:586
  16.2 0.0 collective-permute-done
  16.2 0.0 collective-permute-done.1
  16.2 0.0 collective-permute-done.2.refs_3_.before_ref
  16.2 1.1 %collective-permute-done.3.refs_4_.after_ref = f32[3,256]{1,0:T(4,128)S(1)} collective-permute-done((f32[3,256]{1,0:T(4,128)S(1)}, f32[3,256]{1,0:T(4,128)S(1)}, u32[]{:S(2)}, u32[]{:S(2)}) %collective-permute-start.3) | collective-permute-done | bytes 3104 | tf_op jit(solution)/shard_map/ppermute | solution.py:581
  17.3 4.2 %first.1 = (f32[2,128,128]{2,1,0:T(8,128)S(1)}, f32[2,128,128]{2,1,0:T(8,128)S(1)}, f32[2,10,16,256]{3,2,1,0:T(8,128)S(1)}, f32[2,16,64,256]{3,2,1,0:T(8,128)S(1...) custom-call(f32[3,2,256]{2,1,0:T(2,128)S(1)} %copy.26.refs_0_.pos_re, ...), custom_call_target="tpu_custom_call" | custom-call | tf_op jit(solution)/shard_map/first/pallas_call | solution.py:613
  21.5 0.1 collective-permute-start.4
  21.6 4.8 %collective-permute-start.5 = (f32[2,128,128]{2,1,0:T(8,128)S(1)}, f32[2,128,128]{2,1,0:T(8,128)S(1)}, u32[]{:S(2)}, u32[]{:S(2)}) collective-permute-start(f32[2,128,128]{2,1,0:T(8,128)S(1)} %get-tuple-element.52.refs_0_), channel_id=1, source_target_pairs={{1,0},{2,1},{3,2},{4,3},{5,4},{6,5},{7,6},{8,7},{9,8},{10,9},{11,1... | collective-permute-start | bytes 393224 | tf_op jit(solution)/shard_map/ppermute | solution.py:546
  26.4 4.4 %radial.1 = (f32[2,16,128,256]{3,2,1,0:T(8,128)S(1)}, f32[2,16,128,256]{3,2,1,0:T(8,128)S(1)}, bf16[2,512,4096]{2,1,0:T(8,128)(2,1)S(1)}) custom-call(s32[2,16,256]{2,1,0:T(8,128)S(1)} %get-tuple-element.46.refs_5_.refs_0_, f32[2,10,16,256]{3,2,1,0:T(8,128)S(1)} %get-tuple-element.55.refs_1_.refs_6_, bf16[64,24]{1,0:T(8,128)(2,1)S(1)} %get-tuple-element.56.refs_2_, ...), custom_call_target="tpu_custom_call" | custom-call | flops 1073741824 | bytes 8388608 | tf_op jit(solution)/shard_map/radial/pallas_call | solution.py:635
  30.8 0.0 collective-permute-done.4.refs_2_
  30.8 0.0 collective-permute-done.5.refs_3_
  30.8 13.2 %second.1 = (f32[2,128,128]{2,1,0:T(8,128)S(1)}, f32[2,128,128]{2,1,0:T(8,128)S(1)}, f32[2,128,128]{2,1,0:T(8,128)S(1)}, f32[2,128,128]{2,1,0:T(8,128)S(1)}, f32...) custom-call(f32[2,128,128]{2,1,0:T(8,128)S(1)} %get-tuple-element.52, ...), custom_call_target="tpu_custom_call" | custom-call | tf_op jit(solution)/shard_map/second/pallas_call | solution.py:644
  44.0 0.1 collective-permute-start.6
  44.1 4.8 %collective-permute-start.7 = (f32[2,128,128]{2,1,0:T(8,128)S(1)}, f32[2,128,128]{2,1,0:T(8,128)S(1)}, u32[]{:S(2)}, u32[]{:S(2)}) collective-permute-start(f32[2,128,128]{2,1,0:T(8,128)S(1)} %get-tuple-element.67), channel_id=1, source_target_pairs={{1,0},{2,1},{3,2},{4,3},{5,4},{6,5},{7,6},{8,7},{9,8},{10,9},{11,1... | collective-permute-start | bytes 393224 | tf_op jit(solution)/shard_map/ppermute | solution.py:546
  48.9 3.0 %angular.1.refs_11_ = f32[2,8,16,256]{3,2,1,0:T(8,128)S(1)} custom-call(f32[2,16,128,256]{3,2,1,0:T(8,128)S(1)} %get-tuple-element.59.refs_6_.refs_0_, f32[2,16,128,256]{3,2,1,0:T(8,128)S(1)} %get-tuple-element.72.refs_1_, f32[2,9,128,256]{3,2,1,0:T(8,128)S(1)} %get-tuple-element.73.refs_2_), custom_call_target="tpu_custom_call" | custom-call | flops 1073741824 | bytes 8388608 | tf_op jit(solution)/shard_map/angular/pallas_call | solution.py:664
  51.9 0.0 collective-permute-done.6.refs_2_
  51.9 0.0 collective-permute-done.7.refs_3_
  51.9 0.0 copy-start
  51.9 0.0 copy-start.1
  51.9 0.0 copy-start.2
  51.9 6.0 %third.1 = (f32[3,2,256]{2,1,0:T(2,128)S(1)}, f32[3,2,128]{2,1,0:T(2,128)S(1)}, f32[3,2,128]{2,1,0:T(2,128)S(1)}) custom-call(f32[2,128,128]{2,1,0:T(8,128)S(1)} %get-tuple-element.64.refs_0_, f32[2,128,128]{2,1,0:T(8,128)S(1)} %get-tuple-element.65.refs_1_, f32[2,128,128]{2,1,0:T(8,128)S(1)} %collective-permute-done.6.refs_2_, ...), custom_call_target="tpu_custom_call" | custom-call | tf_op jit(solution)/shard_map/third/pallas_call | solution.py:674
  57.9 0.1 collective-permute-start.8
  58.0 5.0 %collective-permute-start.9 = (f32[3,2,128]{2,1,0:T(2,128)S(1)}, f32[3,2,128]{2,1,0:T(2,128)S(1)}, u32[]{:S(2)}, u32[]{:S(2)}) collective-permute-start(f32[3,2,128]{2,1,0:T(2,128)S(1)} %get-tuple-element.79), channel_id=1, source_target_pairs={{1,0},{2,1},{3,2},{4,3},{5,4},{6,5},{7,6},{8,7},{9,8},{10,9},{11,1... | collective-permute-start | bytes 9224 | tf_op jit(solution)/shard_map/ppermute | solution.py:546
  63.6 0.3 collective-permute-done.8.rlo_ref
  63.9 0.0 collective-permute-done.9.rup_ref
  63.9 0.0 copy-done
  63.9 0.0 copy-done.1
  63.9 0.0 copy-done.2
  63.9 0.1 partial.1
  64.0 20.2 %all_to_all.5 = f32[128,1,128]{2,1,0:T(1,128)S(1)} all-to-all(f32[128,1,128]{2,1,0:T(1,128)S(1)} %bitcast.18), channel_id=1, replica_groups=mesh['image'=8,'space'=16] {'image','space'}, dimensions={0} | all-to-all | bytes 131072 | tf_op jit(solution)/shard_map/all_to_all | solution.py:701
  84.2 1.1 %final.1 = (f32[3,2,256]{2,1,0:T(2,128)}, f32[3,2,256]{2,1,0:T(2,128)}, f32[3,2,256]{2,1,0:T(2,128)}, f32[2]{0:T(128)}) custom-call(f32[128,128]{1,0:T(8,128)S(1)} %bitcast.17, f32[3,2,256]{2,1,0:T(2,128)S(1)} %get-tuple-element.83.force_ref, f32[3,2,256]{2,1,0:T(2,128)S(1)} %copy.26.refs_0_.pos_ref, f32[3,256]{1,0:T(4,128)S(1)} %collective-permute-done.2.refs_3_.before_ref, ...), custom_call_target="tpu_custom_call" | custom-call | tf_op jit(solution)/shard_map/final/pallas_call | solution.py:704
  (5 shorter events, 0.0 us)
Async XLA Ops:
  1.3 14.8 %collective-permute-start = (f32[3,2,128]{2,0,1:T(4,128)S(1)}, f32[3,2,128]{2,0,1:T(4,128)S(1)}, u32[]{:S(2)}, u32[]{:S(2)}) collective-permute-start(f32[3,2,128]{2,0,1:T(4,128)S(1)} %get-tuple-element.91), channel_id=1, source_target_pairs={{0,1},{1,2},{2,3},{3,4},{4,5},{5,6},{6,7},{7,8},{8,9},{9,10},{10,1... | collective-permute-start | bytes 9224 | tf_op jit(solution)/shard_map/ppermute | solution.py:546
  3.8 12.4 %collective-permute-start.1 = (f32[3,2,128]{2,0,1:T(4,128)S(1)}, f32[3,2,128]{2,0,1:T(4,128)S(1)}, u32[]{:S(2)}, u32[]{:S(2)}) collective-permute-start(f32[3,2,128]{2,0,1:T(4,128)S(1)} %get-tuple-element.90), channel_id=1, source_target_pairs={{1,0},{2,1},{3,2},{4,3},{5,4},{6,5},{7,6},{8,7},{9,8},{10,9},{11,1... | collective-permute-start | bytes 9224 | tf_op jit(solution)/shard_map/ppermute | solution.py:546
  8.4 7.8 %collective-permute-start.2 = (f32[3,256]{1,0:T(4,128)S(1)}, f32[3,256]{1,0:T(4,128)S(1)}, u32[]{:S(2)}, u32[]{:S(2)}) collective-permute-start(f32[3,256]{1,0:T(4,128)S(1)} %get-tuple-element.89), channel_id=1, source_target_pairs={{0,16},{16,32},{32,48},{48,64},{64,80},{80,96},{96,112},{1,17},{17... | collective-permute-start | bytes 9224 | tf_op jit(solution)/shard_map/ppermute | solution.py:580
  12.4 4.9 %collective-permute-start.3 = (f32[3,256]{1,0:T(4,128)S(1)}, f32[3,256]{1,0:T(4,128)S(1)}, u32[]{:S(2)}, u32[]{:S(2)}) collective-permute-start(f32[3,256]{1,0:T(4,128)S(1)} %get-tuple-element.88), channel_id=1, source_target_pairs={{16,0},{32,16},{48,32},{64,48},{80,64},{96,80},{112,96},{17,1},{33... | collective-permute-start | bytes 9224 | tf_op jit(solution)/shard_map/ppermute | solution.py:581
  21.5 9.2 %collective-permute-start.4 = (f32[2,128,128]{2,1,0:T(8,128)S(1)}, f32[2,128,128]{2,1,0:T(8,128)S(1)}, u32[]{:S(2)}, u32[]{:S(2)}) collective-permute-start(f32[2,128,128]{2,1,0:T(8,128)S(1)} %get-tuple-element.53.refs_1_), channel_id=1, source_target_pairs={{0,1},{1,2},{2,3},{3,4},{4,5},{5,6},{6,7},{7,8},{8,9},{9,10},{10,1... | collective-permute-start | bytes 393224 | tf_op jit(solution)/shard_map/ppermute | solution.py:546
  21.6 9.2 %collective-permute-start.5 = (f32[2,128,128]{2,1,0:T(8,128)S(1)}, f32[2,128,128]{2,1,0:T(8,128)S(1)}, u32[]{:S(2)}, u32[]{:S(2)}) collective-permute-start(f32[2,128,128]{2,1,0:T(8,128)S(1)} %get-tuple-element.52.refs_0_), channel_id=1, source_target_pairs={{1,0},{2,1},{3,2},{4,3},{5,4},{6,5},{7,6},{8,7},{9,8},{10,9},{11,1... | collective-permute-start | bytes 393224 | tf_op jit(solution)/shard_map/ppermute | solution.py:546
  44.0 7.8 %collective-permute-start.6 = (f32[2,128,128]{2,1,0:T(8,128)S(1)}, f32[2,128,128]{2,1,0:T(8,128)S(1)}, u32[]{:S(2)}, u32[]{:S(2)}) collective-permute-start(f32[2,128,128]{2,1,0:T(8,128)S(1)} %get-tuple-element.66), channel_id=1, source_target_pairs={{0,1},{1,2},{2,3},{3,4},{4,5},{5,6},{6,7},{7,8},{8,9},{9,10},{10,1... | collective-permute-start | bytes 393224 | tf_op jit(solution)/shard_map/ppermute | solution.py:546
  44.1 7.8 %collective-permute-start.7 = (f32[2,128,128]{2,1,0:T(8,128)S(1)}, f32[2,128,128]{2,1,0:T(8,128)S(1)}, u32[]{:S(2)}, u32[]{:S(2)}) collective-permute-start(f32[2,128,128]{2,1,0:T(8,128)S(1)} %get-tuple-element.67), channel_id=1, source_target_pairs={{1,0},{2,1},{3,2},{4,3},{5,4},{6,5},{7,6},{8,7},{9,8},{10,9},{11,1... | collective-permute-start | bytes 393224 | tf_op jit(solution)/shard_map/ppermute | solution.py:546
  51.9 12.0 %copy-start = (f32[2,3,256]{2,0,1:T(2,128)S(1)}, f32[2,3,256]{2,0,1:T(2,128)}, u32[]{:S(2)}) copy-start(f32[2,3,256]{2,0,1:T(2,128)} %param.16) | copy-start | bytes 18436
  51.9 12.0 %copy-start.1 = (f32[3,256]{1,0:T(4,128)S(1)}, f32[3,256]{1,0:T(4,128)}, u32[]{:S(2)}) copy-start(f32[3,256]{1,0:T(4,128)} %start_ref.3) | copy-start | bytes 9220
  51.9 12.0 %copy-start.2 = (f32[3,256]{1,0:T(4,128)S(1)}, f32[3,256]{1,0:T(4,128)}, u32[]{:S(2)}) copy-start(f32[3,256]{1,0:T(4,128)} %end_ref.3) | copy-start | bytes 9220
  57.9 6.0 %collective-permute-start.8 = (f32[3,2,128]{2,1,0:T(2,128)S(1)}, f32[3,2,128]{2,1,0:T(2,128)S(1)}, u32[]{:S(2)}, u32[]{:S(2)}) collective-permute-start(f32[3,2,128]{2,1,0:T(2,128)S(1)} %get-tuple-element.78), channel_id=1, source_target_pairs={{0,1},{1,2},{2,3},{3,4},{4,5},{5,6},{6,7},{7,8},{8,9},{9,10},{10,1... | collective-permute-start | bytes 9224 | tf_op jit(solution)/shard_map/ppermute | solution.py:546
  58.0 5.9 %collective-permute-start.9 = (f32[3,2,128]{2,1,0:T(2,128)S(1)}, f32[3,2,128]{2,1,0:T(2,128)S(1)}, u32[]{:S(2)}, u32[]{:S(2)}) collective-permute-start(f32[3,2,128]{2,1,0:T(2,128)S(1)} %get-tuple-element.79), channel_id=1, source_target_pairs={{1,0},{2,1},{3,2},{4,3},{5,4},{6,5},{7,6},{8,7},{9,8},{10,9},{11,1... | collective-permute-start | bytes 9224 | tf_op jit(solution)/shard_map/ppermute | solution.py:546

commit v8 on v7

--- a/solution.py
+++ b/solution.py
@@ -14,7 +14,7 @@
 NL = 9
 GROUP_FIRST = 2
 GROUP = 8
-PULL = 4
+PULL = 8
 BIG_VMEM = 16 << 20
 SMALL_VMEM = 4 << 20
 
@@ -113,7 +113,7 @@
                 m_ref[l, pl.ds(c0, 16), a0 : a0 + 128] = acc[l]
         return carry
 
-    lax.fori_loop(0, chans // 16, tile, 0)
+    lax.fori_loop(0, chans // 16, tile, 0, unroll=True)
 
 
 def store_yb(yb_ref, angular, slots, atoms):

time: 85.7 us -> 83.9 us (0.979)
  Pallas kernels: 33.8 us -> 32 us
    pallas_call x1, Pallas kernels: 13.2 us -> 11.6 us  [local(): pl.pallas_call(functools.partial(second_kernel, images=images), in_specs=...]
where the time goes in v8:
time: 83.9 us; the launch traced here: 83.7 us
  Pallas kernels  32 us (38%)
  starting transfers between devices  27.7 us (33%)
  blocking collectives  20.2 us (24%)
  between operations  1.65 us (2%)
  waiting for transfers between devices  1.37 us (2%)
    all_to_all x1, blocking collectives, local(): lax.all_to_all(send.reshape(rank, 1, 128), ('image', 'space'), split_axis...  20.2 us
    ppermute x4, starting transfers between devices, neighbours_of(): lax.ppermute(to_below, axis, down)  19.2 us
    pallas_call x1, Pallas kernels, local(): pl.pallas_call(functools.partial(second_kernel, images=images), in_specs=...  11.6 us
    pallas_call x1, Pallas kernels, local(): pl.pallas_call(functools.partial(third_kernel, images=images), in_specs=[...  5.96 us
    pallas_call x1, Pallas kernels, local(): pl.pallas_call(functools.partial(radial_kernel, images=images), in_specs=...  4.37 us
    pallas_call x1, Pallas kernels, local(): pl.pallas_call(functools.partial(first_kernel, images=images), in_specs=[...  4.05 us
    ppermute x1, starting transfers between devices, local(): lax.ppermute(pos[:, images - 1], 'image', [(i, i + 1) for i in range(chai...  3.95 us
    pallas_call x1, Pallas kernels, local(): pl.pallas_call(functools.partial(angular_kernel, images=images), in_specs...  2.98 us
  transfers between devices with their start and end apart: 10, of which 2 were waited for; matrix products, arithmetic and copies ran while one was open for 0% of the time, Pallas kernels for 11%

profile of v8, /device:TPU:1, one launch (start us, length us, event | category | flops | bytes accessed | tf_op | source)
XLA Modules:
  0.0 83.7 jit_solution(9261210170435440717)
XLA Ops:
  0.6 0.7 copy.33
  1.3 2.5 %collective-permute-start = (f32[3,2,128]{2,0,1:T(4,128)S(1)}, f32[3,2,128]{2,0,1:T(4,128)S(1)}, u32[]{:S(2)}, u32[]{:S(2)}) collective-permute-start(f32[3,2,128]{2,0,1:T(4,128)S(1)} %get-tuple-element.91), channel_id=1, source_target_pairs={{0,1},{1,2},{2,3},{3,4},{4,5},{5,6},{6,7},{7,8},{8,9},{9,10},{10,1... | collective-permute-start | bytes 9224 | tf_op jit(solution)/shard_map/ppermute | solution.py:546
  3.8 4.6 %collective-permute-start.1 = (f32[3,2,128]{2,0,1:T(4,128)S(1)}, f32[3,2,128]{2,0,1:T(4,128)S(1)}, u32[]{:S(2)}, u32[]{:S(2)}) collective-permute-start(f32[3,2,128]{2,0,1:T(4,128)S(1)} %get-tuple-element.90), channel_id=1, source_target_pairs={{1,0},{2,1},{3,2},{4,3},{5,4},{6,5},{7,6},{8,7},{9,8},{10,9},{11,1... | collective-permute-start | bytes 9224 | tf_op jit(solution)/shard_map/ppermute | solution.py:546
  8.4 3.9 %collective-permute-start.2 = (f32[3,256]{1,0:T(4,128)S(1)}, f32[3,256]{1,0:T(4,128)S(1)}, u32[]{:S(2)}, u32[]{:S(2)}) collective-permute-start(f32[3,256]{1,0:T(4,128)S(1)} %get-tuple-element.89), channel_id=1, source_target_pairs={{0,16},{16,32},{32,48},{48,64},{64,80},{80,96},{96,112},{1,17},{17... | collective-permute-start | bytes 9224 | tf_op jit(solution)/shard_map/ppermute | solution.py:580
  12.4 1.9 %collective-permute-start.3 = (f32[3,256]{1,0:T(4,128)S(1)}, f32[3,256]{1,0:T(4,128)S(1)}, u32[]{:S(2)}, u32[]{:S(2)}) collective-permute-start(f32[3,256]{1,0:T(4,128)S(1)} %get-tuple-element.88), channel_id=1, source_target_pairs={{16,0},{32,16},{48,32},{64,48},{80,64},{96,80},{112,96},{17,1},{33... | collective-permute-start | bytes 9224 | tf_op jit(solution)/shard_map/ppermute | solution.py:581
  14.3 1.8 %prep.1 = (s32[2,16,256]{2,1,0:T(8,128)S(1)}, s32[2,256]{1,0:T(2,128)S(1)}, bf16[64,24]{1,0:T(8,128)(2,1)S(1)}, bf16[128,192]{1,0:T(8,128)(2,1)S(1)}, bf16[128,1...) custom-call(s32[2,16,256]{2,1,0:T(8,128)} %refs_0_.1, ...), custom_call_target="tpu_custom_call" | custom-call | flops 4000000 | bytes 4000000 | tf_op jit(solution)/shard_map/prep/pallas_call | solution.py:586
  16.2 0.0 collective-permute-done
  16.2 0.0 collective-permute-done.1
  16.2 0.0 collective-permute-done.2.refs_3_.before_ref
  16.2 1.1 %collective-permute-done.3.refs_4_.after_ref = f32[3,256]{1,0:T(4,128)S(1)} collective-permute-done((f32[3,256]{1,0:T(4,128)S(1)}, f32[3,256]{1,0:T(4,128)S(1)}, u32[]{:S(2)}, u32[]{:S(2)}) %collective-permute-start.3) | collective-permute-done | bytes 3104 | tf_op jit(solution)/shard_map/ppermute | solution.py:581
  17.3 4.0 %first.1 = (f32[2,128,128]{2,1,0:T(8,128)S(1)}, f32[2,128,128]{2,1,0:T(8,128)S(1)}, f32[2,10,16,256]{3,2,1,0:T(8,128)S(1)}, f32[2,16,64,256]{3,2,1,0:T(8,128)S(1...) custom-call(f32[3,2,256]{2,1,0:T(2,128)S(1)} %copy.26.refs_0_.pos_re, ...), custom_call_target="tpu_custom_call" | custom-call | tf_op jit(solution)/shard_map/first/pallas_call | solution.py:613
  21.4 0.1 collective-permute-start.4
  21.4 4.8 %collective-permute-start.5 = (f32[2,128,128]{2,1,0:T(8,128)S(1)}, f32[2,128,128]{2,1,0:T(8,128)S(1)}, u32[]{:S(2)}, u32[]{:S(2)}) collective-permute-start(f32[2,128,128]{2,1,0:T(8,128)S(1)} %get-tuple-element.52.refs_0_), channel_id=1, source_target_pairs={{1,0},{2,1},{3,2},{4,3},{5,4},{6,5},{7,6},{8,7},{9,8},{10,9},{11,1... | collective-permute-start | bytes 393224 | tf_op jit(solution)/shard_map/ppermute | solution.py:546
  26.2 4.4 %radial.1 = (f32[2,16,128,256]{3,2,1,0:T(8,128)S(1)}, f32[2,16,128,256]{3,2,1,0:T(8,128)S(1)}, bf16[2,512,4096]{2,1,0:T(8,128)(2,1)S(1)}) custom-call(s32[2,16,256]{2,1,0:T(8,128)S(1)} %get-tuple-element.46.refs_5_.refs_0_, f32[2,10,16,256]{3,2,1,0:T(8,128)S(1)} %get-tuple-element.55.refs_1_.refs_6_, bf16[64,24]{1,0:T(8,128)(2,1)S(1)} %get-tuple-element.56.refs_2_, ...), custom_call_target="tpu_custom_call" | custom-call | flops 1073741824 | bytes 8388608 | tf_op jit(solution)/shard_map/radial/pallas_call | solution.py:635
  30.6 0.0 collective-permute-done.4.refs_2_
  30.6 0.0 collective-permute-done.5.refs_3_
  30.6 11.6 %second.1 = (f32[2,128,128]{2,1,0:T(8,128)S(1)}, f32[2,128,128]{2,1,0:T(8,128)S(1)}, f32[2,128,128]{2,1,0:T(8,128)S(1)}, f32[2,128,128]{2,1,0:T(8,128)S(1)}, f32...) custom-call(f32[2,128,128]{2,1,0:T(8,128)S(1)} %get-tuple-element.52, ...), custom_call_target="tpu_custom_call" | custom-call | tf_op jit(solution)/shard_map/second/pallas_call | solution.py:644
  42.2 0.1 collective-permute-start.6
  42.3 4.8 %collective-permute-start.7 = (f32[2,128,128]{2,1,0:T(8,128)S(1)}, f32[2,128,128]{2,1,0:T(8,128)S(1)}, u32[]{:S(2)}, u32[]{:S(2)}) collective-permute-start(f32[2,128,128]{2,1,0:T(8,128)S(1)} %get-tuple-element.67), channel_id=1, source_target_pairs={{1,0},{2,1},{3,2},{4,3},{5,4},{6,5},{7,6},{8,7},{9,8},{10,9},{11,1... | collective-permute-start | bytes 393224 | tf_op jit(solution)/shard_map/ppermute | solution.py:546
  47.1 3.0 %angular.1.refs_11_ = f32[2,8,16,256]{3,2,1,0:T(8,128)S(1)} custom-call(f32[2,16,128,256]{3,2,1,0:T(8,128)S(1)} %get-tuple-element.59.refs_6_.refs_0_, f32[2,16,128,256]{3,2,1,0:T(8,128)S(1)} %get-tuple-element.72.refs_1_, f32[2,9,128,256]{3,2,1,0:T(8,128)S(1)} %get-tuple-element.73.refs_2_), custom_call_target="tpu_custom_call" | custom-call | flops 1073741824 | bytes 8388608 | tf_op jit(solution)/shard_map/angular/pallas_call | solution.py:664
  50.0 0.0 collective-permute-done.6.refs_2_
  50.1 0.0 collective-permute-done.7.refs_3_
  50.1 0.0 copy-start
  50.1 0.0 copy-start.1
  50.1 0.0 copy-start.2
  50.1 6.0 %third.1 = (f32[3,2,256]{2,1,0:T(2,128)S(1)}, f32[3,2,128]{2,1,0:T(2,128)S(1)}, f32[3,2,128]{2,1,0:T(2,128)S(1)}) custom-call(f32[2,128,128]{2,1,0:T(8,128)S(1)} %get-tuple-element.64.refs_0_, f32[2,128,128]{2,1,0:T(8,128)S(1)} %get-tuple-element.65.refs_1_, f32[2,128,128]{2,1,0:T(8,128)S(1)} %collective-permute-done.6.refs_2_, ...), custom_call_target="tpu_custom_call" | custom-call | tf_op jit(solution)/shard_map/third/pallas_call | solution.py:674
  56.1 0.1 collective-permute-start.8
  56.2 5.0 %collective-permute-start.9 = (f32[3,2,128]{2,1,0:T(2,128)S(1)}, f32[3,2,128]{2,1,0:T(2,128)S(1)}, u32[]{:S(2)}, u32[]{:S(2)}) collective-permute-start(f32[3,2,128]{2,1,0:T(2,128)S(1)} %get-tuple-element.79), channel_id=1, source_target_pairs={{1,0},{2,1},{3,2},{4,3},{5,4},{6,5},{7,6},{8,7},{9,8},{10,9},{11,1... | collective-permute-start | bytes 9224 | tf_op jit(solution)/shard_map/ppermute | solution.py:546
  61.8 0.3 collective-permute-done.8.rlo_ref
  62.1 0.0 collective-permute-done.9.rup_ref
  62.1 0.0 copy-done
  62.1 0.0 copy-done.1
  62.1 0.0 copy-done.2
  62.1 0.1 partial.1
  62.2 20.2 %all_to_all.5 = f32[128,1,128]{2,1,0:T(1,128)S(1)} all-to-all(f32[128,1,128]{2,1,0:T(1,128)S(1)} %bitcast.18), channel_id=1, replica_groups=mesh['image'=8,'space'=16] {'image','space'}, dimensions={0} | all-to-all | bytes 131072 | tf_op jit(solution)/shard_map/all_to_all | solution.py:701
  82.4 1.1 %final.1 = (f32[3,2,256]{2,1,0:T(2,128)}, f32[3,2,256]{2,1,0:T(2,128)}, f32[3,2,256]{2,1,0:T(2,128)}, f32[2]{0:T(128)}) custom-call(f32[128,128]{1,0:T(8,128)S(1)} %bitcast.17, f32[3,2,256]{2,1,0:T(2,128)S(1)} %get-tuple-element.83.force_ref, f32[3,2,256]{2,1,0:T(2,128)S(1)} %copy.26.refs_0_.pos_ref, f32[3,256]{1,0:T(4,128)S(1)} %collective-permute-done.2.refs_3_.before_ref, ...), custom_call_target="tpu_custom_call" | custom-call | tf_op jit(solution)/shard_map/final/pallas_call | solution.py:704
  (5 shorter events, 0.0 us)
Async XLA Ops:
  1.3 14.8 %collective-permute-start = (f32[3,2,128]{2,0,1:T(4,128)S(1)}, f32[3,2,128]{2,0,1:T(4,128)S(1)}, u32[]{:S(2)}, u32[]{:S(2)}) collective-permute-start(f32[3,2,128]{2,0,1:T(4,128)S(1)} %get-tuple-element.91), channel_id=1, source_target_pairs={{0,1},{1,2},{2,3},{3,4},{4,5},{5,6},{6,7},{7,8},{8,9},{9,10},{10,1... | collective-permute-start | bytes 9224 | tf_op jit(solution)/shard_map/ppermute | solution.py:546
  3.8 12.4 %collective-permute-start.1 = (f32[3,2,128]{2,0,1:T(4,128)S(1)}, f32[3,2,128]{2,0,1:T(4,128)S(1)}, u32[]{:S(2)}, u32[]{:S(2)}) collective-permute-start(f32[3,2,128]{2,0,1:T(4,128)S(1)} %get-tuple-element.90), channel_id=1, source_target_pairs={{1,0},{2,1},{3,2},{4,3},{5,4},{6,5},{7,6},{8,7},{9,8},{10,9},{11,1... | collective-permute-start | bytes 9224 | tf_op jit(solution)/shard_map/ppermute | solution.py:546
  8.4 7.8 %collective-permute-start.2 = (f32[3,256]{1,0:T(4,128)S(1)}, f32[3,256]{1,0:T(4,128)S(1)}, u32[]{:S(2)}, u32[]{:S(2)}) collective-permute-start(f32[3,256]{1,0:T(4,128)S(1)} %get-tuple-element.89), channel_id=1, source_target_pairs={{0,16},{16,32},{32,48},{48,64},{64,80},{80,96},{96,112},{1,17},{17... | collective-permute-start | bytes 9224 | tf_op jit(solution)/shard_map/ppermute | solution.py:580
  12.4 4.9 %collective-permute-start.3 = (f32[3,256]{1,0:T(4,128)S(1)}, f32[3,256]{1,0:T(4,128)S(1)}, u32[]{:S(2)}, u32[]{:S(2)}) collective-permute-start(f32[3,256]{1,0:T(4,128)S(1)} %get-tuple-element.88), channel_id=1, source_target_pairs={{16,0},{32,16},{48,32},{64,48},{80,64},{96,80},{112,96},{17,1},{33... | collective-permute-start | bytes 9224 | tf_op jit(solution)/shard_map/ppermute | solution.py:581
  21.4 9.2 %collective-permute-start.4 = (f32[2,128,128]{2,1,0:T(8,128)S(1)}, f32[2,128,128]{2,1,0:T(8,128)S(1)}, u32[]{:S(2)}, u32[]{:S(2)}) collective-permute-start(f32[2,128,128]{2,1,0:T(8,128)S(1)} %get-tuple-element.53.refs_1_), channel_id=1, source_target_pairs={{0,1},{1,2},{2,3},{3,4},{4,5},{5,6},{6,7},{7,8},{8,9},{9,10},{10,1... | collective-permute-start | bytes 393224 | tf_op jit(solution)/shard_map/ppermute | solution.py:546
  21.4 9.2 %collective-permute-start.5 = (f32[2,128,128]{2,1,0:T(8,128)S(1)}, f32[2,128,128]{2,1,0:T(8,128)S(1)}, u32[]{:S(2)}, u32[]{:S(2)}) collective-permute-start(f32[2,128,128]{2,1,0:T(8,128)S(1)} %get-tuple-element.52.refs_0_), channel_id=1, source_target_pairs={{1,0},{2,1},{3,2},{4,3},{5,4},{6,5},{7,6},{8,7},{9,8},{10,9},{11,1... | collective-permute-start | bytes 393224 | tf_op jit(solution)/shard_map/ppermute | solution.py:546
  42.2 7.8 %collective-permute-start.6 = (f32[2,128,128]{2,1,0:T(8,128)S(1)}, f32[2,128,128]{2,1,0:T(8,128)S(1)}, u32[]{:S(2)}, u32[]{:S(2)}) collective-permute-start(f32[2,128,128]{2,1,0:T(8,128)S(1)} %get-tuple-element.66), channel_id=1, source_target_pairs={{0,1},{1,2},{2,3},{3,4},{4,5},{5,6},{6,7},{7,8},{8,9},{9,10},{10,1... | collective-permute-start | bytes 393224 | tf_op jit(solution)/shard_map/ppermute | solution.py:546
  42.3 7.8 %collective-permute-start.7 = (f32[2,128,128]{2,1,0:T(8,128)S(1)}, f32[2,128,128]{2,1,0:T(8,128)S(1)}, u32[]{:S(2)}, u32[]{:S(2)}) collective-permute-start(f32[2,128,128]{2,1,0:T(8,128)S(1)} %get-tuple-element.67), channel_id=1, source_target_pairs={{1,0},{2,1},{3,2},{4,3},{5,4},{6,5},{7,6},{8,7},{9,8},{10,9},{11,1... | collective-permute-start | bytes 393224 | tf_op jit(solution)/shard_map/ppermute | solution.py:546
  50.1 12.0 %copy-start = (f32[2,3,256]{2,0,1:T(2,128)S(1)}, f32[2,3,256]{2,0,1:T(2,128)}, u32[]{:S(2)}) copy-start(f32[2,3,256]{2,0,1:T(2,128)} %param.16) | copy-start | bytes 18436
  50.1 12.0 %copy-start.1 = (f32[3,256]{1,0:T(4,128)S(1)}, f32[3,256]{1,0:T(4,128)}, u32[]{:S(2)}) copy-start(f32[3,256]{1,0:T(4,128)} %start_ref.3) | copy-start | bytes 9220
  50.1 12.0 %copy-start.2 = (f32[3,256]{1,0:T(4,128)S(1)}, f32[3,256]{1,0:T(4,128)}, u32[]{:S(2)}) copy-start(f32[3,256]{1,0:T(4,128)} %end_ref.3) | copy-start | bytes 9220
  56.1 6.0 %collective-permute-start.8 = (f32[3,2,128]{2,1,0:T(2,128)S(1)}, f32[3,2,128]{2,1,0:T(2,128)S(1)}, u32[]{:S(2)}, u32[]{:S(2)}) collective-permute-start(f32[3,2,128]{2,1,0:T(2,128)S(1)} %get-tuple-element.78), channel_id=1, source_target_pairs={{0,1},{1,2},{2,3},{3,4},{4,5},{5,6},{6,7},{7,8},{8,9},{9,10},{10,1... | collective-permute-start | bytes 9224 | tf_op jit(solution)/shard_map/ppermute | solution.py:546
  56.2 5.9 %collective-permute-start.9 = (f32[3,2,128]{2,1,0:T(2,128)S(1)}, f32[3,2,128]{2,1,0:T(2,128)S(1)}, u32[]{:S(2)}, u32[]{:S(2)}) collective-permute-start(f32[3,2,128]{2,1,0:T(2,128)S(1)} %get-tuple-element.79), channel_id=1, source_target_pairs={{1,0},{2,1},{3,2},{4,3},{5,4},{6,5},{7,6},{8,7},{9,8},{10,9},{11,1... | collective-permute-start | bytes 9224 | tf_op jit(solution)/shard_map/ppermute | solution.py:546
